TPU v7x, 512 devices: a whole 4x4x16 slice. The times are simulated.
512 devices in a mesh: dp: 64 (over x, z_hi, y, core), tensor: 8 (over z_lo).
Axes of the slice: x: 4, y: 4, z: 16 (z_hi: 2, z_lo: 8; z = z_hi * 8 + z_lo), core: 2. Of those that a mesh axis runs over, the one named last changes fastest.
Arguments:
- acts: bfloat16 [8192, 2048], P('dp', 'tensor'), may hold values from -54 to 54
- partner: bfloat16 [8192, 2048], P('dp', 'tensor'), may hold values from -54 to 54
- hidden: bfloat16 [14336, 8192], P('dp', 'tensor'), may hold values from -6 to 6
- down_weight: bfloat16 [14336, 2048], P('dp', 'tensor'), may hold values from -0.046875 to 0.046875
Outputs:
- grad_hidden: bfloat16 [14336, 8192], P('dp', 'tensor')
- grad_weight: float32 [14336, 2048], P('dp', 'tensor')
- cka: float32 [], replicated
All inputs are finite; a program needn't handle non-finite values.
Results may differ from a plain program's by a relative error of at most 0.0059.
Values may be sent and summed in bfloat16 or wider, within the bound.
No kernel may reach another device: no remote copies, remote signals or barrier semaphores. Data moves between devices by JAX's collectives and lax.ppermute only.
A program may use at most 64 MiB of HBM per device.

v0:
```python
import jax
import jax.numpy as jnp
from jax import lax
from jax.sharding import PartitionSpec as P


def center_rows(values):
    floats = values.astype(jnp.float32)
    return (floats - jnp.mean(floats, axis=0, keepdims=True)).astype(jnp.bfloat16)


def token_gram(values):
    return lax.dot_general(
        values, values, (((1,), (1,)), ((), ())), preferred_element_type=jnp.float32
    )


def local(acts, partner, hidden, down_weight):
    rows = acts.shape[0]
    width = acts.shape[1] * lax.axis_size("tensor")
    total = rows * lax.axis_size("dp")
    scale = float(total * width)
    centered_x = center_rows(acts)
    centered_y = center_rows(partner)
    gram_x, gram_y = lax.psum((token_gram(centered_x), token_gram(centered_y)), "tensor")
    sxx, syy, sxy = lax.psum(
        (jnp.sum(gram_x * gram_x), jnp.sum(gram_y * gram_y), jnp.sum(gram_x * gram_y)), "dp"
    )
    root = jnp.sqrt(sxx * syy)
    cka = sxy / root
    ratio = sxy / sxx
    coef = -2.0 * scale / root
    mixed = gram_y - ratio * gram_x
    grad = (
        coef * jnp.dot(mixed, centered_x.astype(jnp.float32), precision=lax.Precision.HIGHEST)
    ).astype(jnp.bfloat16)
    columns = lax.all_gather(grad, "dp", axis=0, tiled=True)
    token_block = lax.all_to_all(columns, "tensor", split_axis=0, concat_axis=1, tiled=True)
    part_grad = token_block
    grad_hidden = lax.dot_general(
        lax.all_gather(down_weight, "tensor", axis=1, tiled=True),
        part_grad,
        (((1,), (1,)), ((), ())),
        preferred_element_type=jnp.float32,
    ).astype(jnp.bfloat16)
    part_grad = columns
    grad_weight = lax.dot_general(
        lax.all_gather(hidden, "tensor", axis=1, tiled=True),
        part_grad,
        (((1,), (0,)), ((), ())),
        preferred_element_type=jnp.float32,
    )
    return (grad_hidden, grad_weight, cka)


def solution(mesh):
    in_specs = (P("dp", "tensor"), P("dp", "tensor"), P("dp", "tensor"), P("dp", "tensor"))
    out_specs = (P("dp", "tensor"), P("dp", "tensor"), P())
    return jax.shard_map(local, mesh=mesh, in_specs=in_specs, out_specs=out_specs, check_vma=False)
```

profile of v0, /device:TPU:1, one launch (start us, length us, event | category | flops | bytes accessed | tf_op | source)
XLA Modules:
  0.0 862.2 jit_solution(9282641246402705492)
XLA Ops:
  7.2 0.0 all-reduce.4.cloned.1.call-start
  7.2 0.9 convert_reduce_fusion
  8.1 0.9 convert_reduce_fusion.1
  9.0 1.7 fusion.4
  10.7 1.7 fusion.10
  12.4 0.0 all-reduce.4.cloned.1.call-update
  12.4 0.0 all-gather.3.cloned.1.call-start
  12.5 121.3 %all-reduce.4.cloned.1.call-done = (f32[128,128]{1,0:T(8,128)}, f32[128,128]{1,0:T(8,128)}) async-done(((f32[128,128]{1,0:T(8,128)}, f32[128,128]{1,0:T(8,128)}), (f32[128,128]{1,0:T(8,128)}, f32[128,128]{1,0:T(8,128)})) %all-reduce.4.cloned.1.call-update) | async-done | bytes 131088 | tf_op jit(solution)/shard_map/psum | solution.py:25
  133.7 1.5 multiply_reduce_fusion
  135.2 284.3 %all-reduce = (f32[]{:T(128)}, f32[]{:T(128)}, f32[]{:T(128)}) all-reduce(f32[]{:T(128)} %get-tuple-element.5, f32[]{:T(128)} %get-tuple-element.4, f32[]{:T(128)} %get-tuple-element.3), channel_id=1, replica_groups=mesh['dp'=64,'tensor'=8] {'dp'}, use_global_device_ids=true, to_apply=%region_3.0 | all-reduce | flops 3 | bytes 24 | tf_op jit(solution)/shard_map/psum | solution.py:26
  422.2 1.7 fusion.1
  424.0 0.0 all-gather.3.cloned.1.call-update
  424.0 127.7 %all-gather.3.cloned.1.call-done = bf16[8192,256]{1,0:T(8,128)(2,1)} async-done(((bf16[128,256]{1,0:T(8,128)(2,1)}), bf16[8192,256]{1,0:T(8,128)(2,1)}) %all-gather.3.cloned.1.call-update) | async-done | bytes 4194320 | tf_op jit(solution)/shard_map/all_gather | solution.py:37
  551.7 6.5 copy.7
  558.2 0.0 copy-start
  558.2 4.7 all-to-all-start
  562.9 0.0 all-gather.5.cloned.1.call-start
  562.9 0.7 all-gather.5.cloned.1.call-update
  563.6 0.0 copy-done
  563.6 281.1 %all_gather.10 = bf16[224,2048]{1,0:T(8,128)(2,1)S(1)} all-gather(bf16[224,256]{1,0:T(8,128)(2,1)S(1)} %copy-done), channel_id=1, replica_groups=mesh['dp'=64,'tensor'=8] {'tensor'}, dimensions={1}, use_global_device_ids=true | all-gather | bytes 1032192 | tf_op jit(solution)/shard_map/all_gather | solution.py:41
  845.4 0.0 all-gather.5.cloned.1.call-done
  845.4 5.1 convolution_bitcast_fusion
  850.5 0.0 all-to-all-done
  850.5 4.1 fusion
  (2 shorter events, 0.0 us)
Async XLA Ops:
  7.2 126.6 %all-reduce.4.cloned.1.call-start = ((), (), s32[]{:S(2)}) async-start(), calls=%async_computation.3 | async-start | bytes 262144 | tf_op jit(solution)/shard_map/psum | solution.py:25
  12.4 539.3 %all-gather.3.cloned.1.call-start = ((), (), s32[]{:S(2)}) async-start(), calls=%async_computation.1 | async-start | bytes 4259840 | tf_op jit(solution)/shard_map/all_gather | solution.py:37
  558.2 5.4 copy-start
  558.2 292.3 %all-to-all-start = ((bf16[8,1024,256]{1,2,0:T(8,128)(2,1)}), bf16[8,1024,256]{1,2,0:T(8,128)(2,1)}, u32[]{:S(2)}, u32[]{:S(2)}) async-start(bf16[8,1024,256]{1,2,0:T(8,128)(2,1)} %copy.7), calls=%async_computation | async-start | bytes 8388608 | tf_op jit(solution)/shard_map/all_to_all | solution.py:38
  562.9 282.5 %all-gather.5.cloned.1.call-start = ((), (), s32[]{:S(2)}) async-start(), calls=%async_computation.2 | async-start | bytes 4128768 | tf_op jit(solution)/shard_map/all_gather | solution.py:48
Sparse Core Ops, SparseCore 0:
  12.5 121.1 all-reduce.3
  424.1 127.5 all-gather.2
  565.7 194.5 all-gather.4
where the time goes:
time: 865 us; the launch traced here: 862 us
  blocking collectives  565 us (65%)
  waiting for transfers between devices  250 us (29%)
  between operations  18.3 us (2%)
  matrix products  14.3 us (2%)
    psum x1, blocking collectives, local(): lax.psum((jnp.sum(gram_x * gram_x), jnp.sum(gram_y * gram_y), jnp.sum(gra...  284 us
    all_gather x1, blocking collectives, local(): lax.all_gather(down_weight, 'tensor', axis=1, tiled=True)  281 us
    all_gather x1, waiting for transfers between devices, local(): columns = lax.all_gather(grad, 'dp', axis=0, tiled=True)  128 us
    psum x1, waiting for transfers between devices, local(): lax.psum((token_gram(centered_x), token_gram(centered_y)), 'tensor')  121 us
  transfers between devices with their start and end apart: 4, of which 2 were waited for; matrix products, arithmetic and copies ran while one was open for 1% of the time, Pallas kernels for 0%

commit v1 on v0

v1 whole, which is shorter than its diff:
```python
import itertools

import jax
import jax.numpy as jnp
from jax import lax
from jax.sharding import Mesh, PartitionSpec as P

NAMES = ("x", "zh", "y", "c", "t")
SIZES = {"x": 4, "zh": 2, "y": 4, "c": 2, "t": 8}
BF16 = jnp.bfloat16
F32 = jnp.float32


def center_rows(values):
    floats = values.astype(F32)
    return (floats - jnp.mean(floats, axis=0, keepdims=True)).astype(BF16)


def permutation(names, target):
    pairs = []
    for place in itertools.product(*[range(SIZES[n]) for n in names]):
        goal = target(dict(zip(names, place)))
        source, dest = 0, 0
        for name, coordinate in zip(names, place):
            source = source * SIZES[name] + coordinate
            dest = dest * SIZES[name] + goal[name]
        pairs.append((source, dest))
    return pairs


def permute(values, names, target):
    return lax.ppermute(values, names, permutation(names, target))


def to_plane(flip):
    def target(d):
        return {"x": d["t"] // 2, "zh": (d["t"] + flip) % 2, "t": 2 * d["x"] + d["zh"]}

    return target


def gather_weight(weight):
    blocks = weight[None]
    t = lax.axis_index("t")
    for bit in (1, 2, 4):
        other = permute(blocks, ("t",), lambda d, bit=bit: {"t": d["t"] ^ bit})
        low = (t & bit) == 0
        blocks = jnp.concatenate(
            [jnp.where(low, blocks, other), jnp.where(low, other, blocks)], axis=0
        )
    return blocks


def local(acts, partner, hidden, down_weight):
    rows, width = acts.shape
    units = hidden.shape[0]
    scale = float(rows * 64 * width * 8)
    both = jnp.concatenate([center_rows(acts), center_rows(partner)], axis=1)
    first = permute(both, ("x", "zh", "t"), to_plane(0))
    second = permute(both, ("x", "zh", "t"), to_plane(1))
    weights = gather_weight(down_weight)
    even = lax.axis_index("zh") == 0
    low = jnp.where(even, first, second)
    high = jnp.where(even, second, first)
    y_pair = jnp.concatenate([low[:, width:], high[:, width:]], axis=1)
    gram_y = lax.dot_general(
        y_pair, y_pair, (((1,), (1,)), ((), ())), preferred_element_type=F32
    ).astype(BF16)
    chunk = jnp.concatenate([low[:, :width], high[:, :width], gram_y], axis=1)
    chunks = jnp.broadcast_to(chunk[None], (16,) + chunk.shape)
    plane = lax.all_to_all(chunks, ("x", "y"), split_axis=0, concat_axis=0)
    other = permute(plane, ("c",), lambda d: {"c": 1 - d["c"]})
    core = lax.axis_index("c") == 0
    pair = jnp.stack([jnp.where(core, plane, other), jnp.where(core, other, plane)])
    pair = pair.reshape(2, 4, 4, rows, 2 * width + rows)
    xs = pair[..., : 2 * width].transpose(2, 0, 3, 1, 4).reshape(8, rows, 8 * width)
    grams_y = jnp.sum(pair[..., 2 * width :].astype(F32), axis=1)
    grams_y = grams_y.transpose(1, 0, 2, 3).reshape(8, rows, rows)
    grams_x = lax.dot_general(
        xs, xs, (((2,), (2,)), ((0,), (0,))), preferred_element_type=F32
    )
    sums = jnp.stack(
        [jnp.sum(grams_x * grams_x), jnp.sum(grams_y * grams_y), jnp.sum(grams_x * grams_y)]
    )
    tile = jnp.broadcast_to(sums[None, :, None], (8, 3, 128))
    tiles = lax.all_to_all(tile, ("t",), split_axis=0, concat_axis=0)
    sums = jnp.sum(tiles, axis=0)[:, 0]
    sxx, syy, sxy = sums[0], sums[1], sums[2]
    root = jnp.sqrt(sxx * syy)
    cka = sxy / root
    ratio = sxy / sxx
    coef = -2.0 * scale / root
    mixed = grams_y - ratio * grams_x
    mixed_high = mixed.astype(BF16)
    mixed_low = (mixed - mixed_high.astype(F32)).astype(BF16)
    product = lax.dot_general(
        jnp.concatenate([mixed_high, mixed_low], axis=1),
        xs,
        (((2,), (1,)), ((0,), (0,))),
        preferred_element_type=F32,
    )
    grad = (coef * (product[:, :rows] + product[:, rows:])).astype(BF16)
    grad = grad.reshape(8 * rows, 8 * width)
    partial = lax.dot_general(
        hidden, grad, (((1,), (0,)), ((), ())), preferred_element_type=F32
    ).astype(BF16)
    parts = partial.reshape(units, 8, width).transpose(1, 0, 2)
    parts = lax.all_to_all(parts, ("t",), split_axis=0, concat_axis=0)
    grad_weight = jnp.sum(parts.astype(F32), axis=0)
    full_weight = weights.transpose(1, 0, 2).reshape(units, 8 * width)
    grad_hidden = lax.dot_general(
        full_weight, grad, (((1,), (1,)), ((), ())), preferred_element_type=F32
    ).astype(BF16)
    return (grad_hidden, grad_weight, cka)


def solution(mesh):
    shape = tuple(SIZES[n] for n in NAMES)
    fine = Mesh(mesh.devices.reshape(shape), NAMES)
    spec = P(("x", "zh", "y", "c"), "t")
    return jax.shard_map(
        local, mesh=fine, in_specs=(spec,) * 4, out_specs=(spec, spec, P()), check_vma=False
    )
```

time: 865 us -> 259 us (0.30)
  blocking collectives: 565 us -> 61.2 us
  waiting for transfers between devices: 250 us -> 86.6 us
  starting transfers between devices: 4.8 us -> 60.4 us
  between operations: 18.3 us -> 5.42 us
  local copies, waits for them, and re-layouts: 6.46 us -> 17 us
    psum x1 -> x0, blocking collectives: 284 us -> none  [local(): lax.psum((jnp.sum(gram_x * gram_x), jnp.sum(gram_y * gram_y), jnp.sum(gra...]
    all_gather x1 -> x0, blocking collectives: 281 us -> none  [local(): lax.all_gather(down_weight, 'tensor', axis=1, tiled=True)]
    all_gather x2 -> x0, waiting for transfers between devices: 128 us -> none  [the longest x1 128 us: local(): columns = lax.all_gather(grad, 'dp', axis=0, tiled=True)]
    psum x1 -> x0, waiting for transfers between devices: 121 us -> none  [local(): lax.psum((token_gram(centered_x), token_gram(centered_y)), 'tensor')]
    ppermute x0 -> x6, waiting for transfers between devices: none -> 86.6 us  [permute(): return lax.ppermute(values, names, permutation(names, target))]
    all_to_all x0 -> x2, blocking collectives: none -> 61.2 us  [the longest x1 37.1 us: local(): plane = lax.all_to_all(chunks, ('x', 'y'), split_axis=0, concat_axis=0)]
    ppermute x0 -> x6, starting transfers between devices: none -> 56.9 us  [permute(): return lax.ppermute(values, names, permutation(names, target))]
    reshape x0 -> x3, local copies, waits for them, and re-layouts: none -> 8.85 us  [the longest x1 7.75 us: local(): pair[..., :2 * width].transpose(2, 0, 3, 1, 4).reshape(8, rows, 8 * width)]
  transfers between devices with their start and end apart: 4 -> 7, of which waited for: 2 -> 5; matrix products, arithmetic and copies ran while one was open for 1% -> 2% of each run, Pallas kernels for 0% -> 0%
where the time goes in v1:
time: 259 us; the launch traced here: 258 us
  waiting for transfers between devices  86.6 us (33%)
  blocking collectives  61.2 us (24%)
  starting transfers between devices  60.4 us (23%)
  local copies, waits for them, and re-layouts  17 us (7%)
  matrix products  15.6 us (6%)
  other arithmetic  11.6 us (4%)
  between operations  5.42 us (2%)
    ppermute x6, waiting for transfers between devices, permute(): return lax.ppermute(values, names, permutation(names, target))  86.6 us
    ppermute x6, starting transfers between devices, permute(): return lax.ppermute(values, names, permutation(names, target))  56.9 us
    all_to_all x1, blocking collectives, local(): plane = lax.all_to_all(chunks, ('x', 'y'), split_axis=0, concat_axis=0)  37.1 us
    all_to_all x1, blocking collectives, local(): tiles = lax.all_to_all(tile, ('t',), split_axis=0, concat_axis=0)  24.1 us
    reshape x1, local copies, waits for them, and re-layouts, local(): pair[..., :2 * width].transpose(2, 0, 3, 1, 4).reshape(8, rows, 8 * width)  7.75 us
    dot_general x1, matrix products, local(): lax.dot_general(xs, xs, (((2,), (2,)), ((0,), (0,))), preferred_element_t...  5.34 us
  transfers between devices with their start and end apart: 7, of which 5 were waited for; matrix products, arithmetic and copies ran while one was open for 2% of the time, Pallas kernels for 0%

profile of v1, /device:TPU:1, one launch (start us, length us, event | category | flops | bytes accessed | tf_op | source)
XLA Modules:
  0.0 257.9 jit_solution(6222716979802609599)
XLA Ops:
  0.6 0.0 copy-start
  0.6 0.9 convert_reduce_fusion.2
  1.6 0.9 convert_reduce_fusion.3
  2.5 0.9 fusion.10
  3.4 0.7 collective-permute-start.3
  4.1 17.5 %collective-permute-start.4 = (bf16[128,512]{1,0:T(8,128)(2,1)S(1)}, bf16[128,512]{1,0:T(8,128)(2,1)S(1)}, u32[]{:S(2)}, u32[]{:S(2)}) collective-permute-start(bf16[128,512]{1,0:T(8,128)(2,1)S(1)} %pad_maximum_fusion.4), channel_id=1, source_target_pairs={{0,64},{1,0},{2,192},{3,128},{4,320},{5,256},{6,448},{7,384},{64,6... | collective-permute-start | bytes 393224 | tf_op jit(solution)/shard_map/ppermute | solution.py:32
  21.6 0.0 collective-permute-done.3
  21.6 14.0 %collective-permute-done.4 = bf16[128,512]{1,0:T(8,128)(2,1)S(1)} collective-permute-done((bf16[128,512]{1,0:T(8,128)(2,1)S(1)}, bf16[128,512]{1,0:T(8,128)(2,1)S(1)}, u32[]{:S(2)}, u32[]{:S(2)}) %collective-permute-start.4) | collective-permute-done | bytes 131104 | tf_op jit(solution)/shard_map/ppermute | solution.py:32
  35.6 0.2 convolution_convert_fusion.2
  35.8 0.1 copy.22
  35.9 0.3 broadcast_in_dim.7
  36.3 37.1 %all_to_all.15 = bf16[16,128,640]{2,1,0:T(8,128)(2,1)S(1)} all-to-all(bf16[16,128,640]{2,1,0:T(8,128)(2,1)S(1)} %broadcast_in_dim.7), channel_id=1, replica_groups=mesh['x'=4,'zh'=2,'y'=4,'c'=2,'t'=8] {'x','y'}, dimensions={0} | all-to-all | bytes 5242880 | tf_op jit(solution)/shard_map/all_to_all | solution.py:71
  73.4 4.2 %collective-permute-start.5 = (bf16[16,128,640]{2,1,0:T(8,128)(2,1)S(1)}, bf16[16,128,640]{2,1,0:T(8,128)(2,1)}, u32[]{:S(2)}, u32[]{:S(2)}) collective-permute-start(bf16[16,128,640]{2,1,0:T(8,128)(2,1)S(1)} %all_to_all.15), channel_id=1, source_target_pairs={{0,8},{8,0},{1,9},{9,1},{2,10},{10,2},{3,11},{11,3},{4,12},{12,4},... | collective-permute-start | bytes 7864328 | tf_op jit(solution)/shard_map/ppermute | solution.py:32
  77.6 4.6 %collective-permute-done.5 = bf16[16,128,640]{2,1,0:T(8,128)(2,1)} collective-permute-done((bf16[16,128,640]{2,1,0:T(8,128)(2,1)S(1)}, bf16[16,128,640]{2,1,0:T(8,128)(2,1)}, u32[]{:S(2)}, u32[]{:S(2)}) %collective-permute-start.5) | collective-permute-done | bytes 2621472 | tf_op jit(solution)/shard_map/ppermute | solution.py:32
  82.2 2.2 broadcast_select_fusion
  84.5 0.2 convert_reduce_fusion
  84.6 0.4 fusion.3
  85.1 0.7 multiply_reduce_fusion
  85.8 5.2 %copy.23 = bf16[4,2,128,4,512]{4,3,2,1,0:T(4,128)(2,1)} copy(bf16[4,2,128,4,512]{4,2,0,3,1:T(8,128)(2,1)S(1)} %fusion.3) | data formatting | bytes 8388608 | tf_op jit(solution)/shard_map/transpose | solution.py:76
  91.0 7.8 %reshape.43 = bf16[8,128,2048]{2,1,0:T(8,128)(2,1)} reshape(bf16[4,2,128,4,512]{4,3,2,1,0:T(4,128)(2,1)} %copy.23) | data formatting | bytes 8388608 | tf_op jit(solution)/shard_map/reshape | solution.py:76
  98.8 5.3 %multiply_reduce_fusion.1 = (f32[]{:T(128)}, f32[]{:T(128)}, f32[8,128,128]{2,1,0:T(8,128)S(1)}) fusion(f32[4,2,128,128]{3,2,1,0:T(8,128)S(1)} %copy.24, bf16[8,128,2048]{2,1,0:T(8,128)(2,1)} %reshape.43), kind=kOutput, calls=%fused_computation.26 | convolution fusion | flops 537395200 | bytes 5242888 | tf_op jit(solution)/shard_map/dot_general | solution.py:79
  104.1 2.0 pad_maximum_fusion.5
  106.1 0.1 broadcast_in_dim.8
  106.2 24.1 %all_to_all.16 = f32[8,3,128]{2,1,0:T(4,128)S(1)} all-to-all(f32[8,3,128]{2,1,0:T(4,128)S(1)} %broadcast_in_dim.8), channel_id=1, replica_groups=mesh['x'=4,'zh'=2,'y'=4,'c'=2,'t'=8] {'t'}, dimensions={0} | all-to-all | bytes 24576 | tf_op jit(solution)/shard_map/all_to_all | solution.py:86
  130.3 0.5 fusion.19
  133.6 0.1 fusion.9
  133.7 4.5 %fusion.4 = f32[8,256,2048]{2,1,0:T(8,128)S(1)} fusion(bf16[8,128,2048]{2,1,0:T(8,128)(2,1)} %reshape.43, bf16[8,128,128]{2,1,0:T(8,128)(2,1)S(1)} %get-tuple-element.8, bf16[8,128,128]{2,1,0:T(8,128)(2,1)S(1)} %get-tuple-element.7), kind=kOutput, calls=%fused_computation.17 | convolution fusion | flops 1074790400 | bytes 21495808 | tf_op jit(solution)/shard_map/dot_general | solution.py:96
  138.2 2.1 fusion.1
  140.3 0.0 copy-start.1
  140.3 1.9 copy-done.1
  142.2 0.0 copy-done
  142.2 0.0 copy-start.2
  142.2 1.1 convolution_convert_fusion
  143.4 1.0 copy.34
  144.4 3.6 %all-to-all-start.2 = ((bf16[8,224,256]{2,1,0:T(8,128)(2,1)}), bf16[8,224,256]{2,1,0:T(8,128)(2,1)S(1)}, u32[]{:S(2)}, u32[]{:S(2)}) async-start(bf16[8,224,256]{2,1,0:T(8,128)(2,1)} %bitcast.45), calls=%async_computation.2 | async-start | bytes 1835008 | tf_op jit(solution)/shard_map/all_to_all | solution.py:108
  148.0 0.0 copy-done.2
  148.0 3.2 %collective-permute-start = (bf16[1,224,256]{2,1,0:T(8,128)(2,1)S(1)}, bf16[1,224,256]{2,1,0:T(8,128)(2,1)S(1)}, u32[]{:S(2)}, u32[]{:S(2)}) collective-permute-start(bf16[1,224,256]{2,1,0:T(8,128)(2,1)S(1)} %bitcast.55), channel_id=1, source_target_pairs={{0,1},{1,0},{2,3},{3,2},{4,5},{5,4},{6,7},{7,6},{8,9},{9,8},{10,11... | collective-permute-start | bytes 344072 | tf_op jit(solution)/shard_map/ppermute | solution.py:32
  151.2 15.2 %collective-permute-done = bf16[1,224,256]{2,1,0:T(8,128)(2,1)S(1)} collective-permute-done((bf16[1,224,256]{2,1,0:T(8,128)(2,1)S(1)}, bf16[1,224,256]{2,1,0:T(8,128)(2,1)S(1)}, u32[]{:S(2)}, u32[]{:S(2)}) %collective-permute-start) | collective-permute-done | bytes 114720 | tf_op jit(solution)/shard_map/ppermute | solution.py:32
  166.5 25.5 %collective-permute-start.1 = (bf16[2,224,256]{2,1,0:T(8,128)(2,1)S(1)}, bf16[2,224,256]{2,1,0:T(8,128)(2,1)S(1)}, u32[]{:S(2)}, u32[]{:S(2)}) collective-permute-start(bf16[2,224,256]{2,1,0:T(8,128)(2,1)S(1)} %pad_maximum_fusion.2), channel_id=1, source_target_pairs={{0,2},{1,3},{2,0},{3,1},{4,6},{5,7},{6,4},{7,5},{8,10},{9,11},{10,... | collective-permute-start | bytes 688136 | tf_op jit(solution)/shard_map/ppermute | solution.py:32
  192.0 11.9 %collective-permute-done.1 = bf16[2,224,256]{2,1,0:T(8,128)(2,1)S(1)} collective-permute-done((bf16[2,224,256]{2,1,0:T(8,128)(2,1)S(1)}, bf16[2,224,256]{2,1,0:T(8,128)(2,1)S(1)}, u32[]{:S(2)}, u32[]{:S(2)}) %collective-permute-start.1) | collective-permute-done | bytes 229408 | tf_op jit(solution)/shard_map/ppermute | solution.py:32
  204.0 5.7 %collective-permute-start.2 = (bf16[4,224,256]{2,1,0:T(8,128)(2,1)S(1)}, bf16[4,224,256]{2,1,0:T(8,128)(2,1)S(1)}, u32[]{:S(2)}, u32[]{:S(2)}) collective-permute-start(bf16[4,224,256]{2,1,0:T(8,128)(2,1)S(1)} %pad_maximum_fusion.1), channel_id=1, source_target_pairs={{0,4},{1,5},{2,6},{3,7},{4,0},{5,1},{6,2},{7,3},{8,12},{9,13},{10,... | collective-permute-start | bytes 1376264 | tf_op jit(solution)/shard_map/ppermute | solution.py:32
  209.7 41.0 %collective-permute-done.2 = bf16[4,224,256]{2,1,0:T(8,128)(2,1)S(1)} collective-permute-done((bf16[4,224,256]{2,1,0:T(8,128)(2,1)S(1)}, bf16[4,224,256]{2,1,0:T(8,128)(2,1)S(1)}, u32[]{:S(2)}, u32[]{:S(2)}) %collective-permute-start.2) | collective-permute-done | bytes 458784 | tf_op jit(solution)/shard_map/ppermute | solution.py:32
  250.7 0.1 broadcast_select_fusion.3
  250.8 0.1 maximum_bitcast_fusion
  250.8 0.1 copy.32
  251.6 4.4 %convolution_convert_fusion.1 = bf16[224,1024]{1,0:T(8,128)(2,1)} fusion(bf16[224,2048]{1,0:T(8,128)(2,1)S(1)} %bitcast.53, bf16[1024,2048]{1,0:T(8,128)(2,1)} %bitcast.52), kind=kOutput, calls=%fused_computation.12 | convolution fusion | flops 939753472 | bytes 5570560 | tf_op jit(solution)/shard_map/dot_general | solution.py:111
  256.0 0.0 all-to-all-done.2
  256.0 0.8 convert_reduce_fusion.1
  (13 shorter events, 0.3 us)
Async XLA Ops:
  0.6 141.6 %copy-start = (bf16[224,1024]{1,0:T(8,128)(2,1)S(1)}, bf16[224,1024]{1,0:T(8,128)(2,1)}, u32[]{:S(2)}) copy-start(bf16[224,1024]{1,0:T(8,128)(2,1)} %param.6) | copy-start | bytes 1376260
  3.4 18.2 %collective-permute-start.3 = (bf16[128,512]{1,0:T(8,128)(2,1)S(1)}, bf16[128,512]{1,0:T(8,128)(2,1)S(1)}, u32[]{:S(2)}, u32[]{:S(2)}) collective-permute-start(bf16[128,512]{1,0:T(8,128)(2,1)S(1)} %pad_maximum_fusion.4), channel_id=1, source_target_pairs={{0,0},{1,64},{2,128},{3,192},{4,256},{5,320},{6,384},{7,448},{64,1... | collective-permute-start | bytes 393224 | tf_op jit(solution)/shard_map/ppermute | solution.py:32
  4.1 31.5 %collective-permute-start.4 = (bf16[128,512]{1,0:T(8,128)(2,1)S(1)}, bf16[128,512]{1,0:T(8,128)(2,1)S(1)}, u32[]{:S(2)}, u32[]{:S(2)}) collective-permute-start(bf16[128,512]{1,0:T(8,128)(2,1)S(1)} %pad_maximum_fusion.4), channel_id=1, source_target_pairs={{0,64},{1,0},{2,192},{3,128},{4,320},{5,256},{6,448},{7,384},{64,6... | collective-permute-start | bytes 393224 | tf_op jit(solution)/shard_map/ppermute | solution.py:32
  73.4 8.9 %collective-permute-start.5 = (bf16[16,128,640]{2,1,0:T(8,128)(2,1)S(1)}, bf16[16,128,640]{2,1,0:T(8,128)(2,1)}, u32[]{:S(2)}, u32[]{:S(2)}) collective-permute-start(bf16[16,128,640]{2,1,0:T(8,128)(2,1)S(1)} %all_to_all.15), channel_id=1, source_target_pairs={{0,8},{8,0},{1,9},{9,1},{2,10},{10,2},{3,11},{11,3},{4,12},{12,4},... | collective-permute-start | bytes 7864328 | tf_op jit(solution)/shard_map/ppermute | solution.py:32
  140.3 1.9 copy-start.1
  142.2 5.7 %copy-start.2 = (bf16[224,256]{1,0:T(8,128)(2,1)S(1)}, bf16[224,256]{1,0:T(8,128)(2,1)}, u32[]{:S(2)}) copy-start(bf16[224,256]{1,0:T(8,128)(2,1)} %param.7) | copy-start | bytes 344068
  144.4 111.6 %all-to-all-start.2 = ((bf16[8,224,256]{2,1,0:T(8,128)(2,1)}), bf16[8,224,256]{2,1,0:T(8,128)(2,1)S(1)}, u32[]{:S(2)}, u32[]{:S(2)}) async-start(bf16[8,224,256]{2,1,0:T(8,128)(2,1)} %bitcast.45), calls=%async_computation.2 | async-start | bytes 1835008 | tf_op jit(solution)/shard_map/all_to_all | solution.py:108
  148.0 18.4 %collective-permute-start = (bf16[1,224,256]{2,1,0:T(8,128)(2,1)S(1)}, bf16[1,224,256]{2,1,0:T(8,128)(2,1)S(1)}, u32[]{:S(2)}, u32[]{:S(2)}) collective-permute-start(bf16[1,224,256]{2,1,0:T(8,128)(2,1)S(1)} %bitcast.55), channel_id=1, source_target_pairs={{0,1},{1,0},{2,3},{3,2},{4,5},{5,4},{6,7},{7,6},{8,9},{9,8},{10,11... | collective-permute-start | bytes 344072 | tf_op jit(solution)/shard_map/ppermute | solution.py:32
  166.5 37.4 %collective-permute-start.1 = (bf16[2,224,256]{2,1,0:T(8,128)(2,1)S(1)}, bf16[2,224,256]{2,1,0:T(8,128)(2,1)S(1)}, u32[]{:S(2)}, u32[]{:S(2)}) collective-permute-start(bf16[2,224,256]{2,1,0:T(8,128)(2,1)S(1)} %pad_maximum_fusion.2), channel_id=1, source_target_pairs={{0,2},{1,3},{2,0},{3,1},{4,6},{5,7},{6,4},{7,5},{8,10},{9,11},{10,... | collective-permute-start | bytes 688136 | tf_op jit(solution)/shard_map/ppermute | solution.py:32
  204.0 46.7 %collective-permute-start.2 = (bf16[4,224,256]{2,1,0:T(8,128)(2,1)S(1)}, bf16[4,224,256]{2,1,0:T(8,128)(2,1)S(1)}, u32[]{:S(2)}, u32[]{:S(2)}) collective-permute-start(bf16[4,224,256]{2,1,0:T(8,128)(2,1)S(1)} %pad_maximum_fusion.1), channel_id=1, source_target_pairs={{0,4},{1,5},{2,6},{3,7},{4,0},{5,1},{6,2},{7,3},{8,12},{9,13},{10,... | collective-permute-start | bytes 1376264 | tf_op jit(solution)/shard_map/ppermute | solution.py:32

commit v2 on v1

v2 whole, which is shorter than its diff:
```python
import functools
import itertools

import jax
import jax.numpy as jnp
from jax import lax
from jax.experimental import pallas as pl
from jax.experimental.pallas import tpu as pltpu
from jax.sharding import Mesh, PartitionSpec as P


NAMES = ("x", "zh", "y", "c", "t")
SIZES = {"x": 4, "zh": 2, "y": 4, "c": 2, "t": 8}
BF16 = jnp.bfloat16
F32 = jnp.float32
ROWS = 128
WIDTH = 256
SLICE = ROWS // 8
PIECE = ROWS + SLICE
CHUNK = 2 * PIECE + 16


def permutation(names, target):
    pairs = []
    for place in itertools.product(*[range(SIZES[n]) for n in names]):
        goal = target(dict(zip(names, place)))
        source, dest = 0, 0
        for name, coordinate in zip(names, place):
            source = source * SIZES[name] + coordinate
            dest = dest * SIZES[name] + goal[name]
        pairs.append((source, dest))
    return pairs


def permute(values, names, target):
    return lax.ppermute(values, names, permutation(names, target))


def exchange(values, names):
    return lax.all_to_all(values, names, split_axis=0, concat_axis=0)


def to_plane(flip):
    def target(d):
        return {"x": d["t"] // 2, "zh": (d["t"] + flip) % 2, "t": 2 * d["x"] + d["zh"]}

    return target


def gram(values):
    return lax.dot_general(values, values, (((1,), (1,)), ((), ())), preferred_element_type=F32)


def center(values):
    floats = values.astype(F32)
    return (floats - jnp.mean(floats, axis=0, keepdims=True)).astype(BF16)


def source_kernel(acts_ref, partner_ref, x_ref, grams_ref):
    x = center(acts_ref[...])
    x_ref[...] = x
    y = center(partner_ref[...])
    grams_ref[:, :SLICE, :] = gram(x).reshape(8, SLICE, ROWS)
    grams_ref[:, SLICE:, :] = gram(y).reshape(8, SLICE, ROWS)


def split(values, parts):
    pieces = []
    for _ in range(parts):
        piece = values.astype(BF16)
        values = values - piece.astype(F32)
        pieces.append(piece)
    return pieces


def slice_kernel(x_ref, parts_ref, piece_ref, tiles_ref):
    total = jnp.sum(parts_ref[...], axis=0)
    gx, gy = total[:SLICE], total[SLICE:]
    piece_ref[:ROWS, :] = x_ref[...]
    high, low = split(gy, 2)
    piece_ref[ROWS:, :ROWS] = high
    piece_ref[ROWS:, ROWS:] = low
    rows = [jnp.sum(v, axis=0, keepdims=True) for v in (gx * gx, gy * gy, gx * gy)]
    tile = jnp.concatenate(rows + [jnp.zeros((5, ROWS), F32)], axis=0)
    tiles_ref[...] = jnp.broadcast_to(tile[None], tiles_ref.shape)


def chunk_kernel(flag_ref, first_ref, second_ref, tiles_ref, chunk_ref):
    even = flag_ref[0] == 0
    first, second = first_ref[...], second_ref[...]
    low = jnp.where(even, first, second)
    high = jnp.where(even, second, first)
    chunk_ref[:ROWS, :] = low[:ROWS]
    chunk_ref[ROWS : 2 * ROWS, :] = high[:ROWS]
    chunk_ref[2 * ROWS : 2 * ROWS + SLICE, :] = low[ROWS:]
    chunk_ref[2 * ROWS + SLICE : 2 * PIECE, :] = high[ROWS:]
    total = jnp.sum(tiles_ref[...], axis=0)[:3]
    pieces = [p.astype(F32) for p in split(total, 3)]
    block = jnp.concatenate(pieces + [jnp.zeros((7, ROWS), F32)], axis=0)
    chunk_ref[2 * PIECE :, :] = jnp.concatenate([block, block], axis=1).astype(BF16)


def main_kernel(
    scale, core_ref, own_ref, other_ref, own_sums_ref, other_sums_ref, hidden_ref,
    grad_ref, parts_ref, cka_ref, sums_ref, total_ref,
):
    step = pl.program_id(0)

    @pl.when(step == 0)
    def _():
        tiles = own_sums_ref[...].astype(F32) + other_sums_ref[...].astype(F32)
        block = jnp.sum(tiles.reshape(16, 16, WIDTH), axis=0)[:, :ROWS]
        sums = block[0:3] + block[3:6] + block[6:9]
        sums = jnp.sum(sums, axis=1, keepdims=True)
        sxx, syy, sxy = sums[0:1], sums[1:2], sums[2:3]
        root = jnp.sqrt(sxx * syy)
        sums_ref[0:1, :] = jnp.broadcast_to(sxy / sxx, (1, ROWS))
        sums_ref[1:2, :] = jnp.broadcast_to(-2.0 * scale / root, (1, ROWS))
        cka_ref[...] = jnp.broadcast_to(sxy / root, cka_ref.shape)

    def work(block_ref):
        pieces = [block_ref[t // 2, 0, pl.ds((t % 2) * ROWS, ROWS), :] for t in range(8)]
        gx = gram(pieces[0])
        for piece in pieces[1:]:
            gx = gx + gram(piece)
        slices = []
        for t in range(8):
            rows = block_ref[t // 2, 0, pl.ds(2 * ROWS + (t % 2) * SLICE, SLICE), :].astype(F32)
            slices.append(rows[:, :ROWS] + rows[:, ROWS:])
        gy = jnp.concatenate(slices, axis=0)
        mixed = gy - sums_ref[0:1, :] * gx
        high, low = split(mixed, 2)
        both = jnp.concatenate([high, low], axis=0)
        coef = sums_ref[1:2, :]
        coef = jnp.concatenate([coef, coef], axis=1)
        for t in range(8):
            product = jnp.dot(both, pieces[t], preferred_element_type=F32)
            block = (coef * (product[:ROWS] + product[ROWS:])).astype(BF16)
            columns = slice(t * WIDTH, (t + 1) * WIDTH)
            grad_ref[:, columns] = block
            added = jnp.dot(hidden_ref[...], block, preferred_element_type=F32)

            @pl.when(step == 0)
            def _():
                total_ref[:, columns] = added

            @pl.when(jnp.logical_and(step > 0, step < 7))
            def _():
                total_ref[:, columns] += added

            @pl.when(step == 7)
            def _():
                parts_ref[t] = (total_ref[:, columns] + added).astype(BF16)

    @pl.when(step < 4)
    def _():
        work(own_ref)

    @pl.when(step >= 4)
    def _():
        work(other_ref)


def combine(core, plane, other, hidden, scale):
    units = hidden.shape[0]
    plane = plane.reshape(4, 4, CHUNK, WIDTH)
    other = other.reshape(4, 4, CHUNK, WIDTH)

    def place(i, core):
        return lax.rem(i, 4) * 2 + lax.rem(core[0] + i // 4, 2)

    sums = pl.BlockSpec((4, 4, 16, WIDTH), lambda i, core: (0, 0, 2 * PIECE // 16, 0))
    return pl.pallas_call(
        functools.partial(main_kernel, scale),
        grid_spec=pltpu.PrefetchScalarGridSpec(
            num_scalar_prefetch=1,
            grid=(8,),
            in_specs=[
                pl.BlockSpec((4, 1, CHUNK, WIDTH), lambda i, core: (0, jnp.minimum(i, 3), 0, 0)),
                pl.BlockSpec((4, 1, CHUNK, WIDTH), lambda i, core: (0, jnp.maximum(i - 4, 0), 0, 0)),
                sums,
                sums,
                pl.BlockSpec((units, ROWS), lambda i, core: (0, place(i, core))),
            ],
            out_specs=[
                pl.BlockSpec((ROWS, 8 * WIDTH), lambda i, core: (place(i, core), 0)),
                pl.BlockSpec((8, units, WIDTH), lambda i, core: (0, 0, 0)),
                pl.BlockSpec((8, ROWS), lambda i, core: (0, 0)),
            ],
            scratch_shapes=[pltpu.VMEM((8, ROWS), F32), pltpu.VMEM((units, 8 * WIDTH), F32)],
        ),
        out_shape=[
            jax.ShapeDtypeStruct((8 * ROWS, 8 * WIDTH), BF16),
            jax.ShapeDtypeStruct((8, units, WIDTH), BF16),
            jax.ShapeDtypeStruct((8, ROWS), F32),
        ],
        compiler_params=pltpu.CompilerParams(vmem_limit_bytes=32 << 20),
        name="combine",
    )(core, plane, other, plane, other, hidden)


def hidden_kernel(place_ref, near_ref, far_ref, grad_ref, out_ref, total_ref):
    step = pl.program_id(0)

    def add(weight):
        product = lax.dot_general(
            weight, grad_ref[...], (((1,), (1,)), ((), ())), preferred_element_type=F32
        )

        @pl.when(step == 0)
        def _():
            total_ref[...] = product

        @pl.when(jnp.logical_and(step > 0, step < 7))
        def _():
            total_ref[...] += product

        @pl.when(step == 7)
        def _():
            out_ref[...] = (total_ref[...] + product).astype(BF16)

    @pl.when(step < 4)
    def _():
        add(near_ref[0])

    @pl.when(step >= 4)
    def _():
        add(far_ref[0])


def hidden_gradient(place, near, far, grad):
    units = near.shape[1]

    def column(k, place):
        bits = lax.rem(k, 2) * 4 + lax.rem(k // 2, 2) * 2 + k // 4
        return lax.bitwise_xor(place[0], bits)

    tokens = grad.shape[0]
    return pl.pallas_call(
        hidden_kernel,
        grid_spec=pltpu.PrefetchScalarGridSpec(
            num_scalar_prefetch=1,
            grid=(8,),
            in_specs=[
                pl.BlockSpec((1, units, WIDTH), lambda k, place: (jnp.minimum(k, 3), 0, 0)),
                pl.BlockSpec((1, units, WIDTH), lambda k, place: (jnp.maximum(k - 4, 0), 0, 0)),
                pl.BlockSpec((tokens, WIDTH), lambda k, place: (0, column(k, place))),
            ],
            out_specs=pl.BlockSpec((units, tokens), lambda k, place: (0, 0)),
            scratch_shapes=[pltpu.VMEM((units, tokens), F32)],
        ),
        out_shape=jax.ShapeDtypeStruct((units, tokens), BF16),
        cost_estimate=pl.CostEstimate(
            flops=2 * units * tokens * 8 * WIDTH, bytes_accessed=6 << 20, transcendentals=0
        ),
        name="hidden_gradient",
    )(place, near, far, grad)


def local(acts, partner, hidden, down_weight):
    scale = float(ROWS * 64 * WIDTH * 8)
    vmem = pl.BlockSpec(memory_space=pltpu.VMEM)
    smem = pl.BlockSpec(memory_space=pltpu.SMEM)
    shape = jax.ShapeDtypeStruct
    near = down_weight[None]
    far = permute(near, ("t",), lambda d: {"t": d["t"] ^ 4})
    near = jnp.concatenate([near, far], axis=0)
    far = permute(near, ("t",), lambda d: {"t": d["t"] ^ 2})
    near = jnp.concatenate([near, far], axis=0)
    far = permute(near, ("t",), lambda d: {"t": d["t"] ^ 1})
    x, grams = pl.pallas_call(
        source_kernel,
        in_specs=[vmem, vmem],
        out_specs=[vmem, vmem],
        out_shape=[shape((ROWS, WIDTH), BF16), shape((8, 2 * SLICE, ROWS), F32)],
        name="source",
    )(acts, partner)
    grams = exchange(grams, ("t",))
    piece, tiles = pl.pallas_call(
        slice_kernel,
        in_specs=[vmem, vmem],
        out_specs=[vmem, vmem],
        out_shape=[shape((PIECE, WIDTH), BF16), shape((16, 8, ROWS), F32)],
        name="slices",
    )(x, grams)
    first = permute(piece, ("x", "zh", "t"), to_plane(0))
    second = permute(piece, ("x", "zh", "t"), to_plane(1))
    tiles = exchange(tiles, ("zh", "t"))
    flag = lax.axis_index("zh").astype(jnp.int32).reshape(1)
    chunk = pl.pallas_call(
        chunk_kernel,
        in_specs=[smem, vmem, vmem, vmem],
        out_specs=vmem,
        out_shape=shape((CHUNK, WIDTH), BF16),
        name="chunk",
    )(flag, first, second, tiles)
    plane = exchange(jnp.broadcast_to(chunk[None], (16,) + chunk.shape), ("x", "y"))
    other = permute(plane, ("c",), lambda d: {"c": 1 - d["c"]})
    core = lax.axis_index("c").astype(jnp.int32).reshape(1)
    grad, parts, cka = combine(core, plane, other, hidden, scale)
    parts = exchange(parts, ("t",))
    grad_weight = jnp.sum(parts.astype(F32), axis=0)
    place = lax.axis_index("t").astype(jnp.int32).reshape(1)
    grad_hidden = hidden_gradient(place, near, far, grad)
    return (grad_hidden, grad_weight, cka[0, 0])


def solution(mesh):
    shape = tuple(SIZES[n] for n in NAMES)
    fine = Mesh(mesh.devices.reshape(shape), NAMES)
    spec = P(("x", "zh", "y", "c"), "t")
    return jax.shard_map(
        local, mesh=fine, in_specs=(spec,) * 4, out_specs=(spec, spec, P()), check_vma=False
    )
```

time: 259 us -> 235 us (0.907)
  Pallas kernels: 0 us -> 43.9 us
  matrix products: 15.6 us -> 0 us
  starting transfers between devices: 60.4 us -> 48.1 us
  local copies, waits for them, and re-layouts: 17 us -> 4.99 us
  waiting for transfers between devices: 86.6 us -> 75.1 us
  other arithmetic: 11.6 us -> 0.88 us
  between operations: 5.42 us -> 0.75 us
    pallas_call x0 -> x5, Pallas kernels: none -> 43.9 us  [the longest x1 31.5 us: combine(): pl.pallas_call(functools.partial(main_kernel, scale), grid_spec=pltpu.Pre...]
    ppermute x6, starting transfers between devices: 56.9 us -> 33.6 us  [permute(): return lax.ppermute(values, names, permutation(names, target))]
    dot_general x5 -> x0, matrix products: 15.6 us -> none  [the longest x1 5.34 us: local(): lax.dot_general(xs, xs, (((2,), (2,)), ((0,), (0,))), preferred_element_t...]
    ppermute x6, waiting for transfers between devices: 86.6 us -> 75.1 us  [permute(): return lax.ppermute(values, names, permutation(names, target))]
    all_to_all x1 -> x2, starting transfers between devices: 3.55 us -> 14.4 us  [exchange(): return lax.all_to_all(values, names, split_axis=0, concat_axis=0)]
    reshape x3 -> x0, local copies, waits for them, and re-layouts: 8.85 us -> none  [the longest x1 7.75 us: local(): pair[..., :2 * width].transpose(2, 0, 3, 1, 4).reshape(8, rows, 8 * width)]
    transpose x2 -> x0, local copies, waits for them, and re-layouts: 5.2 us -> none  [the longest x1 5.17 us: local(): pair[..., :2 * width].transpose(2, 0, 3, 1, 4).reshape(8, rows, 8 * width)]
    convert_element_type x3 -> x0, other arithmetic: 3.12 us -> none  [the longest x1 2.09 us: local(): grad = (coef * (product[:, :rows] + product[:, rows:])).astype(BF16)]
  transfers between devices with their start and end apart: 7 -> 8, of which waited for: 5 -> 5; matrix products, arithmetic and copies ran while one was open for 2% -> 0% of each run, Pallas kernels for 0% -> 3%
where the time goes in v2:
time: 235 us; the launch traced here: 234 us
  waiting for transfers between devices  75.1 us (32%)
  blocking collectives  60.8 us (26%)
  starting transfers between devices  48.1 us (20%)
  Pallas kernels  43.9 us (19%)
  local copies, waits for them, and re-layouts  4.99 us (2%)
    ppermute x6, waiting for transfers between devices, permute(): return lax.ppermute(values, names, permutation(names, target))  75.1 us
    all_to_all x2, blocking collectives, exchange(): return lax.all_to_all(values, names, split_axis=0, concat_axis=0)  60.8 us
    ppermute x6, starting transfers between devices, permute(): return lax.ppermute(values, names, permutation(names, target))  33.6 us
    pallas_call x1, Pallas kernels, combine(): pl.pallas_call(functools.partial(main_kernel, scale), grid_spec=pltpu.Pre...  31.5 us
    all_to_all x2, starting transfers between devices, exchange(): return lax.all_to_all(values, names, split_axis=0, concat_axis=0)  14.4 us
    pallas_call x1, Pallas kernels, hidden_gradient(): pl.pallas_call(hidden_kernel, grid_spec=pltpu.PrefetchScalarGridSpec(num_...  7.46 us
  transfers between devices with their start and end apart: 8, of which 5 were waited for; matrix products, arithmetic and copies ran while one was open for 0% of the time, Pallas kernels for 3%

profile of v2, /device:TPU:1, one launch (start us, length us, event | category | flops | bytes accessed | tf_op | source)
XLA Modules:
  0.0 234.5 jit_solution(13847976255611351328)
XLA Ops:
  0.6 1.8 source.1
  2.4 23.5 %all_to_all.20.parts_ref = f32[8,32,128]{2,1,0:T(8,128)} all-to-all(f32[8,32,128]{2,1,0:T(8,128)} %get-tuple-element.11), channel_id=1, replica_groups=mesh['x'=4,'zh'=2,'y'=4,'c'=2,'t'=8] {'t'}, dimensions={0} | all-to-all | bytes 262144 | tf_op jit(solution)/shard_map/all_to_all | solution.py:40
  25.9 1.6 slices.1
  27.5 7.4 %all-to-all-start.1 = ((f32[16,8,128]{2,1,0:T(8,128)}), f32[16,8,128]{2,1,0:T(8,128)S(1)}, u32[]{:S(2)}, u32[]{:S(2)}) async-start(f32[16,8,128]{2,1,0:T(8,128)} %get-tuple-element.13), calls=%async_computation.1 | async-start | bytes 131072 | tf_op jit(solution)/shard_map/all_to_all | solution.py:40
  34.9 1.5 collective-permute-start.3
  36.5 12.6 %collective-permute-start.4 = (bf16[144,256]{1,0:T(8,128)(2,1)}, bf16[144,256]{1,0:T(8,128)(2,1)S(1)}, u32[]{:S(2)}, u32[]{:S(2)}) collective-permute-start(bf16[144,256]{1,0:T(8,128)(2,1)} %get-tuple-element.12), channel_id=1, source_target_pairs={{0,64},{1,0},{2,192},{3,128},{4,320},{5,256},{6,448},{7,384},{64,6... | collective-permute-start | bytes 221192 | tf_op jit(solution)/shard_map/ppermute | solution.py:36
  49.1 0.0 collective-permute-done.3.first_ref
  49.1 0.0 copy-start.6
  49.1 4.7 %collective-permute-done.4.second_ref = bf16[144,256]{1,0:T(8,128)(2,1)S(1)} collective-permute-done((bf16[144,256]{1,0:T(8,128)(2,1)}, bf16[144,256]{1,0:T(8,128)(2,1)S(1)}, u32[]{:S(2)}, u32[]{:S(2)}) %collective-permute-start.4) | collective-permute-done | bytes 73760 | tf_op jit(solution)/shard_map/ppermute | solution.py:36
  53.8 0.0 copy-start.7
  53.8 0.0 all-to-all-done.1.tiles_ref
  53.8 0.0 copy-start.5
  53.8 0.0 copy-done.6
  53.8 0.6 copy-done.7
  54.5 0.0 copy-done.5
  54.5 1.6 chunk.1
  56.1 1.1 broadcast_in_dim.10
  57.2 0.0 copy-start.1
  57.2 37.3 %all_to_all.21 = bf16[16,304,256]{2,1,0:T(8,128)(2,1)S(1)} all-to-all(bf16[16,304,256]{2,1,0:T(8,128)(2,1)S(1)} %broadcast_in_dim.10), channel_id=1, replica_groups=mesh['x'=4,'zh'=2,'y'=4,'c'=2,'t'=8] {'x','y'}, dimensions={0} | all-to-all | bytes 4980736 | tf_op jit(solution)/shard_map/all_to_all | solution.py:40
  94.5 8.3 %collective-permute-start.5 = (bf16[16,304,256]{2,1,0:T(8,128)(2,1)S(1)}, bf16[16,304,256]{2,1,0:T(8,128)(2,1)}, u32[]{:S(2)}, u32[]{:S(2)}) collective-permute-start(bf16[16,304,256]{2,1,0:T(8,128)(2,1)S(1)} %all_to_all.21), channel_id=1, source_target_pairs={{0,8},{8,0},{1,9},{9,1},{2,10},{10,2},{3,11},{11,3},{4,12},{12,4},... | collective-permute-start | bytes 7471112 | tf_op jit(solution)/shard_map/ppermute | solution.py:36
  102.8 4.5 %collective-permute-done.5 = bf16[16,304,256]{2,1,0:T(8,128)(2,1)} collective-permute-done((bf16[16,304,256]{2,1,0:T(8,128)(2,1)S(1)}, bf16[16,304,256]{2,1,0:T(8,128)(2,1)}, u32[]{:S(2)}, u32[]{:S(2)}) %collective-permute-start.5) | collective-permute-done | bytes 2490400 | tf_op jit(solution)/shard_map/ppermute | solution.py:36
  107.3 0.0 copy-done.1
  107.3 0.0 copy-start.4
  107.3 31.5 %combine.1 = (bf16[1024,2048]{1,0:T(8,128)(2,1)S(1)}, bf16[8,224,256]{2,1,0:T(8,128)(2,1)}, f32[8,128]{1,0:T(8,128)S(1)}) custom-call(s32[1]{0:T(128)} %bitcast.2.core_ref, bf16[4,4,304,256]{3,2,1,0:T(8,128)(2,1)S(1)} %bitcast.7, bf16[4,4,304,256]{3,2,1,0:T(8,128)(2,1)} %bitcast.5.other_ref.other_sums_ref, bf16[4,4,304,256]{3,2,1,0:T(8,128)(2,1)S(1)} %bitcast.8, ...), custom_call_target="tpu_custom_call" | custom-call | tf_op jit(solution)/shard_map/combine/pallas_call | solution.py:173
  138.7 0.0 copy-start
  138.8 2.0 copy-done
  140.7 7.0 %all-to-all-start.3 = ((bf16[8,224,256]{2,1,0:T(8,128)(2,1)}), bf16[8,224,256]{2,1,0:T(8,128)(2,1)S(1)}, u32[]{:S(2)}, u32[]{:S(2)}) async-start(bf16[8,224,256]{2,1,0:T(8,128)(2,1)} %get-tuple-element.15), calls=%async_computation.3 | async-start | bytes 1835008 | tf_op jit(solution)/shard_map/all_to_all | solution.py:40
  147.7 0.0 copy-done.4
  147.7 7.3 %collective-permute-start = (bf16[1,224,256]{2,1,0:T(8,128)(2,1)S(1)}, bf16[1,224,256]{2,1,0:T(8,128)(2,1)S(1)}, u32[]{:S(2)}, u32[]{:S(2)}) collective-permute-start(bf16[1,224,256]{2,1,0:T(8,128)(2,1)S(1)} %bitcast.9), channel_id=1, source_target_pairs={{0,4},{1,5},{2,6},{3,7},{4,0},{5,1},{6,2},{7,3},{8,12},{9,13},{10,... | collective-permute-start | bytes 344072 | tf_op jit(solution)/shard_map/ppermute | solution.py:36
  155.0 47.6 %collective-permute-done = bf16[1,224,256]{2,1,0:T(8,128)(2,1)S(1)} collective-permute-done((bf16[1,224,256]{2,1,0:T(8,128)(2,1)S(1)}, bf16[1,224,256]{2,1,0:T(8,128)(2,1)S(1)}, u32[]{:S(2)}, u32[]{:S(2)}) %collective-permute-start) | collective-permute-done | bytes 114720 | tf_op jit(solution)/shard_map/ppermute | solution.py:36
  202.6 1.9 collective-permute-start.1
  204.5 8.3 %collective-permute-done.1 = bf16[2,224,256]{2,1,0:T(8,128)(2,1)S(1)} collective-permute-done((bf16[2,224,256]{2,1,0:T(8,128)(2,1)S(1)}, bf16[2,224,256]{2,1,0:T(8,128)(2,1)S(1)}, u32[]{:S(2)}, u32[]{:S(2)}) %collective-permute-start.1) | collective-permute-done | bytes 229408 | tf_op jit(solution)/shard_map/ppermute | solution.py:36
  212.9 0.0 copy-start.2
  212.9 1.9 collective-permute-start.2
  214.9 0.5 slice.3
  215.4 10.1 %collective-permute-done.2.far_ref = bf16[4,224,256]{2,1,0:T(8,128)(2,1)S(1)} collective-permute-done((bf16[4,224,256]{2,1,0:T(8,128)(2,1)S(1)}, bf16[4,224,256]{2,1,0:T(8,128)(2,1)S(1)}, u32[]{:S(2)}, u32[]{:S(2)}) %collective-permute-start.2) | collective-permute-done | bytes 458784 | tf_op jit(solution)/shard_map/ppermute | solution.py:36
  225.4 0.0 copy-start.3
  225.4 0.0 copy-done.2
  225.4 0.8 copy-done.3
  226.2 7.5 %hidden_gradient.1 = bf16[224,1024]{1,0:T(8,128)(2,1)} custom-call(s32[1]{0:T(128)} %bitcast.place_ref, bf16[4,224,256]{2,1,0:T(8,128)(2,1)} %copy-done.2, bf16[4,224,256]{2,1,0:T(8,128)(2,1)} %copy-done.3, bf16[1024,2048]{1,0:T(8,128)(2,1)} %copy-done), custom_call_target="tpu_custom_call" | custom-call | flops 939524096 | bytes 6291456 | tf_op jit(solution)/shard_map/hidden_gradient/pallas_call | solution.py:239
  233.7 0.0 all-to-all-done.3
  233.7 0.8 convert_reduce_fusion
  (2 shorter events, 0.1 us)
Async XLA Ops:
  27.5 26.3 %all-to-all-start.1 = ((f32[16,8,128]{2,1,0:T(8,128)}), f32[16,8,128]{2,1,0:T(8,128)S(1)}, u32[]{:S(2)}, u32[]{:S(2)}) async-start(f32[16,8,128]{2,1,0:T(8,128)} %get-tuple-element.13), calls=%async_computation.1 | async-start | bytes 131072 | tf_op jit(solution)/shard_map/all_to_all | solution.py:40
  34.9 14.2 %collective-permute-start.3 = (bf16[144,256]{1,0:T(8,128)(2,1)}, bf16[144,256]{1,0:T(8,128)(2,1)S(1)}, u32[]{:S(2)}, u32[]{:S(2)}) collective-permute-start(bf16[144,256]{1,0:T(8,128)(2,1)} %get-tuple-element.12), channel_id=1, source_target_pairs={{0,0},{1,64},{2,128},{3,192},{4,256},{5,320},{6,384},{7,448},{64,1... | collective-permute-start | bytes 221192 | tf_op jit(solution)/shard_map/ppermute | solution.py:36
  36.5 17.4 %collective-permute-start.4 = (bf16[144,256]{1,0:T(8,128)(2,1)}, bf16[144,256]{1,0:T(8,128)(2,1)S(1)}, u32[]{:S(2)}, u32[]{:S(2)}) collective-permute-start(bf16[144,256]{1,0:T(8,128)(2,1)} %get-tuple-element.12), channel_id=1, source_target_pairs={{0,64},{1,0},{2,192},{3,128},{4,320},{5,256},{6,448},{7,384},{64,6... | collective-permute-start | bytes 221192 | tf_op jit(solution)/shard_map/ppermute | solution.py:36
  49.1 4.7 %copy-start.6 = (bf16[144,256]{1,0:T(8,128)(2,1)}, bf16[144,256]{1,0:T(8,128)(2,1)S(1)}, u32[]{:S(2)}) copy-start(bf16[144,256]{1,0:T(8,128)(2,1)S(1)} %collective-permute-done.3.first_ref) | copy-start | bytes 221188
  53.8 0.6 copy-start.7
  53.8 0.7 copy-start.5
  57.2 50.1 %copy-start.1 = (bf16[224,1024]{1,0:T(8,128)(2,1)S(1)}, bf16[224,1024]{1,0:T(8,128)(2,1)}, u32[]{:S(2)}) copy-start(bf16[224,1024]{1,0:T(8,128)(2,1)} %hidden_ref.1) | copy-start | bytes 1376260
  94.5 12.8 %collective-permute-start.5 = (bf16[16,304,256]{2,1,0:T(8,128)(2,1)S(1)}, bf16[16,304,256]{2,1,0:T(8,128)(2,1)}, u32[]{:S(2)}, u32[]{:S(2)}) collective-permute-start(bf16[16,304,256]{2,1,0:T(8,128)(2,1)S(1)} %all_to_all.21), channel_id=1, source_target_pairs={{0,8},{8,0},{1,9},{9,1},{2,10},{10,2},{3,11},{11,3},{4,12},{12,4},... | collective-permute-start | bytes 7471112 | tf_op jit(solution)/shard_map/ppermute | solution.py:36
  107.3 40.5 %copy-start.4 = (bf16[224,256]{1,0:T(8,128)(2,1)S(1)}, bf16[224,256]{1,0:T(8,128)(2,1)}, u32[]{:S(2)}) copy-start(bf16[224,256]{1,0:T(8,128)(2,1)} %param.7) | copy-start | bytes 344068
  138.7 2.0 copy-start
  140.7 93.0 %all-to-all-start.3 = ((bf16[8,224,256]{2,1,0:T(8,128)(2,1)}), bf16[8,224,256]{2,1,0:T(8,128)(2,1)S(1)}, u32[]{:S(2)}, u32[]{:S(2)}) async-start(bf16[8,224,256]{2,1,0:T(8,128)(2,1)} %get-tuple-element.15), calls=%async_computation.3 | async-start | bytes 1835008 | tf_op jit(solution)/shard_map/all_to_all | solution.py:40
  147.7 54.9 %collective-permute-start = (bf16[1,224,256]{2,1,0:T(8,128)(2,1)S(1)}, bf16[1,224,256]{2,1,0:T(8,128)(2,1)S(1)}, u32[]{:S(2)}, u32[]{:S(2)}) collective-permute-start(bf16[1,224,256]{2,1,0:T(8,128)(2,1)S(1)} %bitcast.9), channel_id=1, source_target_pairs={{0,4},{1,5},{2,6},{3,7},{4,0},{5,1},{6,2},{7,3},{8,12},{9,13},{10,... | collective-permute-start | bytes 344072 | tf_op jit(solution)/shard_map/ppermute | solution.py:36
  202.6 10.2 %collective-permute-start.1 = (bf16[2,224,256]{2,1,0:T(8,128)(2,1)S(1)}, bf16[2,224,256]{2,1,0:T(8,128)(2,1)S(1)}, u32[]{:S(2)}, u32[]{:S(2)}) collective-permute-start(bf16[2,224,256]{2,1,0:T(8,128)(2,1)S(1)} %pad_maximum_fusion.1), channel_id=1, source_target_pairs={{0,2},{1,3},{2,0},{3,1},{4,6},{5,7},{6,4},{7,5},{8,10},{9,11},{10,... | collective-permute-start | bytes 688136 | tf_op jit(solution)/shard_map/ppermute | solution.py:36
  212.9 12.5 %copy-start.2 = (bf16[4,224,256]{2,1,0:T(8,128)(2,1)}, bf16[4,224,256]{2,1,0:T(8,128)(2,1)S(1)}, u32[]{:S(2)}) copy-start(bf16[4,224,256]{2,1,0:T(8,128)(2,1)S(1)} %pad_maximum_fusion.near_ref) | copy-start | bytes 1376260
  212.9 12.5 %collective-permute-start.2 = (bf16[4,224,256]{2,1,0:T(8,128)(2,1)S(1)}, bf16[4,224,256]{2,1,0:T(8,128)(2,1)S(1)}, u32[]{:S(2)}, u32[]{:S(2)}) collective-permute-start(bf16[4,224,256]{2,1,0:T(8,128)(2,1)S(1)} %pad_maximum_fusion.near_ref), channel_id=1, source_target_pairs={{0,1},{1,0},{2,3},{3,2},{4,5},{5,4},{6,7},{7,6},{8,9},{9,8},{10,11... | collective-permute-start | bytes 1376264 | tf_op jit(solution)/shard_map/ppermute | solution.py:36
  225.4 0.8 copy-start.3

commit v3 on v1

v3 whole, which is shorter than its diff:
```python
import functools
import itertools

import jax
import jax.numpy as jnp
from jax import lax
from jax.experimental import pallas as pl
from jax.experimental.pallas import tpu as pltpu
from jax.sharding import Mesh, PartitionSpec as P


NAMES = ("x", "zh", "y", "c", "t")
SIZES = {"x": 4, "zh": 2, "y": 4, "c": 2, "t": 8}
BF16 = jnp.bfloat16
F32 = jnp.float32
ROWS = 128
WIDTH = 256
SLICE = ROWS // 8
PIECE = ROWS + SLICE
CHUNK = 2 * PIECE + 16


def permutation(names, target):
    pairs = []
    for place in itertools.product(*[range(SIZES[n]) for n in names]):
        goal = target(dict(zip(names, place)))
        source, dest = 0, 0
        for name, coordinate in zip(names, place):
            source = source * SIZES[name] + coordinate
            dest = dest * SIZES[name] + goal[name]
        pairs.append((source, dest))
    return pairs


def permute(values, names, target):
    return lax.ppermute(values, names, permutation(names, target))


def exchange(values, names):
    return lax.all_to_all(values, names, split_axis=0, concat_axis=0)


def to_plane(flip):
    def target(d):
        return {"x": d["t"] // 2, "zh": (d["t"] + flip) % 2, "t": 2 * d["x"] + d["zh"]}

    return target


def gram(values):
    return lax.dot_general(values, values, (((1,), (1,)), ((), ())), preferred_element_type=F32)


def center(values):
    floats = values.astype(F32)
    return (floats - jnp.mean(floats, axis=0, keepdims=True)).astype(BF16)


def source_kernel(acts_ref, partner_ref, x_ref, grams_ref):
    x = center(acts_ref[...])
    x_ref[...] = x
    y = center(partner_ref[...])
    grams_ref[:, :SLICE, :] = gram(x).reshape(8, SLICE, ROWS)
    grams_ref[:, SLICE:, :] = gram(y).reshape(8, SLICE, ROWS)


def split(values, parts):
    pieces = []
    for _ in range(parts):
        piece = values.astype(BF16)
        values = values - piece.astype(F32)
        pieces.append(piece)
    return pieces


def slice_kernel(x_ref, parts_ref, piece_ref, sums_ref):
    total = jnp.sum(parts_ref[...], axis=0)
    gx, gy = total[:SLICE], total[SLICE:]
    piece_ref[:ROWS, :] = x_ref[...]
    high, low = split(gy, 2)
    piece_ref[ROWS:, :ROWS] = high
    piece_ref[ROWS:, ROWS:] = low
    rows = [jnp.sum(v, axis=0, keepdims=True) for v in (gx * gx, gy * gy, gx * gy)]
    rows = [p.astype(F32) for p in split(jnp.concatenate(rows, axis=0), 3)]
    block = jnp.concatenate(rows + [jnp.zeros((7, ROWS), F32)], axis=0)
    sums_ref[...] = jnp.concatenate([block, jnp.zeros_like(block)], axis=1).astype(BF16)


def sums_kernel(rows_ref, tiles_ref):
    block = jnp.sum(rows_ref[...].astype(F32).reshape(16, 16, WIDTH), axis=0)[:, :ROWS]
    sums = block[0:3] + block[3:6] + block[6:9]
    tile = jnp.concatenate([sums, jnp.zeros((5, ROWS), F32)], axis=0)
    tiles_ref[...] = jnp.broadcast_to(tile[None], tiles_ref.shape)


def plane_sums(plane):
    return pl.pallas_call(
        sums_kernel,
        grid=(1,),
        in_specs=[pl.BlockSpec((4, 4, 16, WIDTH), lambda i: (0, 0, 2 * PIECE // 16, 0))],
        out_specs=pl.BlockSpec((32, 8, ROWS), lambda i: (0, 0, 0)),
        out_shape=jax.ShapeDtypeStruct((32, 8, ROWS), F32),
        name="plane_sums",
    )(plane)


def gram_kernel(block_ref, out_ref):
    pieces = [block_ref[t // 2, 0, pl.ds((t % 2) * ROWS, ROWS), :] for t in range(8)]
    out_ref[0] = gram(jnp.concatenate(pieces, axis=1))


def plane_grams(plane):
    return pl.pallas_call(
        gram_kernel,
        grid=(4,),
        in_specs=[pl.BlockSpec((4, 1, CHUNK, WIDTH), lambda i: (0, i, 0, 0))],
        out_specs=pl.BlockSpec((1, ROWS, ROWS), lambda i: (i, 0, 0)),
        out_shape=jax.ShapeDtypeStruct((4, ROWS, ROWS), F32),
        cost_estimate=pl.CostEstimate(
            flops=4 << 30, bytes_accessed=16 << 20, transcendentals=0
        ),
        name="plane_grams",
    )(plane)


def mix_kernel(
    scale, core_ref, own_gram_ref, other_gram_ref, own_rows_ref, other_rows_ref, tiles_ref,
    hidden_ref, mixed_ref, product_ref, cka_ref,
):
    sums = jnp.sum(jnp.sum(tiles_ref[...], axis=0), axis=1, keepdims=True)
    sxx, syy, sxy = sums[0:1], sums[1:2], sums[2:3]
    root = jnp.sqrt(sxx * syy)
    ratio = jnp.broadcast_to(sxy / sxx, (1, ROWS))
    coef = jnp.broadcast_to(-2.0 * scale / root, (1, ROWS))
    cka_ref[...] = jnp.broadcast_to(sxy / root, cka_ref.shape)
    core = core_ref[0]
    for b in range(8):
        y = b % 4
        gram_ref, rows_ref = (own_gram_ref, own_rows_ref) if b < 4 else (other_gram_ref, other_rows_ref)
        slices = []
        for t in range(8):
            rows = rows_ref[t // 2, y, pl.ds((t % 2) * SLICE, SLICE), :].astype(F32)
            slices.append(rows[:, :ROWS] + rows[:, ROWS:])
        mixed = coef * (jnp.concatenate(slices, axis=0) - ratio * gram_ref[y])
        mixed_ref[b] = mixed
        place = y * 2 + (core if b < 4 else 1 - core)
        hidden = hidden_ref[:, pl.ds(pl.multiple_of(place * ROWS, ROWS), ROWS)]
        product = jnp.dot(
            jnp.concatenate([hidden, hidden], axis=1),
            jnp.concatenate(split(mixed, 2), axis=0),
            preferred_element_type=F32,
        )
        product_ref[:, b * ROWS : (b + 1) * ROWS] = product.astype(BF16)


def mix(core, own_gram, other_gram, plane, other, tiles, hidden, scale):
    units = hidden.shape[0]
    smem = pl.BlockSpec(memory_space=pltpu.SMEM)
    rows = pl.BlockSpec((4, 4, 2 * SLICE, WIDTH), lambda i: (0, 0, ROWS // SLICE, 0))
    whole = lambda *shape: pl.BlockSpec(shape, lambda i: (0,) * len(shape))
    return pl.pallas_call(
        functools.partial(mix_kernel, scale),
        grid=(1,),
        in_specs=[
            smem,
            whole(4, ROWS, ROWS),
            whole(4, ROWS, ROWS),
            rows,
            rows,
            whole(32, 8, ROWS),
            whole(units, 8 * ROWS),
        ],
        out_specs=[whole(8, ROWS, ROWS), whole(units, 8 * ROWS), whole(8, ROWS)],
        out_shape=[
            jax.ShapeDtypeStruct((8, ROWS, ROWS), F32),
            jax.ShapeDtypeStruct((units, 8 * ROWS), BF16),
            jax.ShapeDtypeStruct((8, ROWS), F32),
        ],
        name="mix",
    )(core, own_gram, other_gram, plane, other, tiles, hidden)


def reversed_bits(k):
    return lax.rem(k, 2) * 4 + lax.rem(k // 2, 2) * 2 + k // 4


def column_blocks(first):
    def index(k, place):
        t = lax.bitwise_xor(place[0], reversed_bits(first + k))
        return (t // 2, 0, lax.rem(t, 2), 0)

    return pl.BlockSpec((1, 4, ROWS, WIDTH), index)


def weight_kernel(place_ref, product_ref, own_ref, other_ref, out_ref):
    half = 4 * ROWS
    value = jnp.dot(
        product_ref[:, :half], own_ref[...].reshape(half, WIDTH), preferred_element_type=F32
    )
    value = value + jnp.dot(
        product_ref[:, half:], other_ref[...].reshape(half, WIDTH), preferred_element_type=F32
    )
    out_ref[0] = value.astype(out_ref.dtype)


def weight_parts(place, product, plane, other, first, dtype):
    units = product.shape[0]
    return pl.pallas_call(
        weight_kernel,
        grid_spec=pltpu.PrefetchScalarGridSpec(
            num_scalar_prefetch=1,
            grid=(4,),
            in_specs=[
                pl.BlockSpec((units, 8 * ROWS), lambda k, place: (0, 0)),
                column_blocks(first),
                column_blocks(first),
            ],
            out_specs=pl.BlockSpec((1, units, WIDTH), lambda k, place: (k, 0, 0)),
        ),
        out_shape=jax.ShapeDtypeStruct((4, units, WIDTH), dtype),
        cost_estimate=pl.CostEstimate(
            flops=2 * units * 8 * ROWS * 4 * WIDTH, bytes_accessed=4 << 20, transcendentals=0
        ),
        name="weight_parts",
    )(place, product, plane, other)


def hidden_kernel(
    place_ref, core_ref, near_ref, far_ref, own_ref, other_ref, mixed_ref, out_ref, total_ref
):
    step = pl.program_id(0)
    half = 4 * ROWS
    weight = jnp.where(step < 4, near_ref[0], far_ref[0])
    for ref, columns in ((own_ref, slice(0, half)), (other_ref, slice(half, 2 * half))):
        product = lax.dot_general(
            weight,
            ref[...].reshape(half, WIDTH),
            (((1,), (1,)), ((), ())),
            preferred_element_type=F32,
        )

        @pl.when(step == 0)
        def _(product=product, columns=columns):
            total_ref[:, columns] = product

        @pl.when(step > 0)
        def _(product=product, columns=columns):
            total_ref[:, columns] += product

    @pl.when(step == 7)
    def _():
        for b in range(8):
            high, low = split(total_ref[:, b * ROWS : (b + 1) * ROWS], 2)
            mixed_high, mixed_low = split(mixed_ref[b], 2)
            value = lax.dot_general(
                jnp.concatenate([high, high, low], axis=1),
                jnp.concatenate([mixed_high, mixed_low, mixed_high], axis=1),
                (((1,), (1,)), ((), ())),
                preferred_element_type=F32,
            )
            place = b % 4 * 2 + (core_ref[0] if b < 4 else 1 - core_ref[0])
            out_ref[:, pl.ds(pl.multiple_of(place * ROWS, ROWS), ROWS)] = value.astype(BF16)


def hidden_gradient(place, core, near, far, plane, other, mixed):
    units = near.shape[1]
    tokens = 8 * ROWS
    blocks = pl.BlockSpec(
        (1, 4, ROWS, WIDTH), lambda k, place, core: column_blocks(0).index_map(k, place)
    )
    return pl.pallas_call(
        hidden_kernel,
        grid_spec=pltpu.PrefetchScalarGridSpec(
            num_scalar_prefetch=2,
            grid=(8,),
            in_specs=[
                pl.BlockSpec((1, units, WIDTH), lambda k, *_: (jnp.minimum(k, 3), 0, 0)),
                pl.BlockSpec((1, units, WIDTH), lambda k, *_: (jnp.maximum(k - 4, 0), 0, 0)),
                blocks,
                blocks,
                pl.BlockSpec((8, ROWS, ROWS), lambda k, *_: (0, 0, 0)),
            ],
            out_specs=pl.BlockSpec((units, tokens), lambda k, *_: (0, 0)),
            scratch_shapes=[pltpu.VMEM((units, tokens), F32)],
        ),
        out_shape=jax.ShapeDtypeStruct((units, tokens), BF16),
        cost_estimate=pl.CostEstimate(
            flops=2 * units * tokens * 8 * WIDTH, bytes_accessed=8 << 20, transcendentals=0
        ),
        name="hidden_gradient",
    )(place, core, near, far, plane, other, mixed)


def flip(bit):
    return lambda d: {"t": d["t"] ^ bit}


def local(acts, partner, hidden, down_weight):
    scale = float(ROWS * 64 * WIDTH * 8)
    vmem = pl.BlockSpec(memory_space=pltpu.VMEM)
    shape = jax.ShapeDtypeStruct
    place = lax.axis_index("t").astype(jnp.int32).reshape(1)
    core = lax.axis_index("c").astype(jnp.int32).reshape(1)
    near = down_weight[None]
    far = permute(near, ("t",), flip(4))
    near = jnp.concatenate([near, far], axis=0)
    far = permute(near, ("t",), flip(2))
    near = jnp.concatenate([near, far], axis=0)
    far = permute(near, ("t",), flip(1))
    x, grams = pl.pallas_call(
        source_kernel,
        in_specs=[vmem, vmem],
        out_specs=[vmem, vmem],
        out_shape=[shape((ROWS, WIDTH), BF16), shape((8, 2 * SLICE, ROWS), F32)],
        name="source",
    )(acts, partner)
    grams = exchange(grams, ("t",))
    piece, sums = pl.pallas_call(
        slice_kernel,
        in_specs=[vmem, vmem],
        out_specs=[vmem, vmem],
        out_shape=[shape((PIECE, WIDTH), BF16), shape((16, WIDTH), BF16)],
        name="slices",
    )(x, grams)
    first = permute(piece, ("x", "zh", "t"), to_plane(0))
    second = permute(piece, ("x", "zh", "t"), to_plane(1))
    even = lax.axis_index("zh") == 0
    low = jnp.where(even, first, second)
    high = jnp.where(even, second, first)
    chunk = jnp.concatenate([low[:ROWS], high[:ROWS], low[ROWS:], high[ROWS:], sums], axis=0)
    plane = exchange(jnp.broadcast_to(chunk[None], (16,) + chunk.shape), ("x", "y"))
    other = permute(plane, ("c",), lambda d: {"c": 1 - d["c"]})
    plane = plane.reshape(4, 4, CHUNK, WIDTH)
    other = other.reshape(4, 4, CHUNK, WIDTH)
    tiles = plane_sums(plane)
    tiles = exchange(tiles, ("zh", "c", "t"))
    mixed, product, cka = mix(
        core, plane_grams(plane), plane_grams(other), plane, other, tiles, hidden, scale
    )
    sent = weight_parts(place, product, plane, other, 4, BF16)
    sent = permute(sent, ("t",), flip(1))
    kept = weight_parts(place, product, plane, other, 0, F32)
    later = permute((kept[2:] + sent[2:].astype(F32)).astype(BF16), ("t",), flip(2))
    kept = kept[:2] + sent[:2].astype(F32)
    last = permute((kept[1] + later[1].astype(F32)).astype(BF16), ("t",), flip(4))
    grad_weight = kept[0] + later[0].astype(F32) + last.astype(F32)
    grad_hidden = hidden_gradient(place, core, near, far, plane, other, mixed)
    return (grad_hidden, grad_weight, cka[0, 0])


def solution(mesh):
    shape = tuple(SIZES[n] for n in NAMES)
    fine = Mesh(mesh.devices.reshape(shape), NAMES)
    spec = P(("x", "zh", "y", "c"), "t")
    return jax.shard_map(
        local, mesh=fine, in_specs=(spec,) * 4, out_specs=(spec, spec, P()), check_vma=False
    )
```

time: 259 us -> 193 us (0.75)
  waiting for transfers between devices: 86.6 us -> 20.5 us
  Pallas kernels: 0 us -> 33.5 us
  matrix products: 15.6 us -> 0 us
  local copies, waits for them, and re-layouts: 17 us -> 3.52 us
  blocking collectives: 61.2 us -> 72.7 us
  other arithmetic: 11.6 us -> 2.08 us
  between operations: 5.42 us -> 0.81 us
  starting transfers between devices: 60.4 us -> 56.8 us
    ppermute x6 -> x9, waiting for transfers between devices: 86.6 us -> 12.6 us  [permute(): return lax.ppermute(values, names, permutation(names, target))]
    pallas_call x0 -> x9, Pallas kernels: none -> 33.5 us  [the longest x1 9.22 us: hidden_gradient(): pl.pallas_call(hidden_kernel, grid_spec=pltpu.PrefetchScalarGridSpec(num_...]
    dot_general x5 -> x0, matrix products: 15.6 us -> none  [the longest x1 5.34 us: local(): lax.dot_general(xs, xs, (((2,), (2,)), ((0,), (0,))), preferred_element_t...]
    all_to_all x2, blocking collectives: 61.2 us -> 72.7 us  [exchange(): return lax.all_to_all(values, names, split_axis=0, concat_axis=0)]
    reshape x3 -> x0, local copies, waits for them, and re-layouts: 8.85 us -> none  [the longest x1 7.75 us: local(): pair[..., :2 * width].transpose(2, 0, 3, 1, 4).reshape(8, rows, 8 * width)]
    ppermute x6 -> x9, starting transfers between devices: 56.9 us -> 48.1 us  [permute(): return lax.ppermute(values, names, permutation(names, target))]
    all_to_all x1, waiting for transfers between devices: 0.01 us -> 7.82 us  [exchange(): return lax.all_to_all(values, names, split_axis=0, concat_axis=0)]
    transpose x2 -> x0, local copies, waits for them, and re-layouts: 5.2 us -> none  [the longest x1 5.17 us: local(): pair[..., :2 * width].transpose(2, 0, 3, 1, 4).reshape(8, rows, 8 * width)]
  transfers between devices with their start and end apart: 7 -> 10, of which waited for: 5 -> 5; matrix products, arithmetic and copies ran while one was open for 2% -> 1% of each run, Pallas kernels for 0% -> 12%
where the time goes in v3:
time: 193 us; the launch traced here: 190 us
  blocking collectives  72.7 us (38%)
  starting transfers between devices  56.8 us (29%)
  Pallas kernels  33.5 us (17%)
  waiting for transfers between devices  20.5 us (11%)
  local copies, waits for them, and re-layouts  3.52 us (2%)
  other arithmetic  2.08 us (1%)
    all_to_all x2, blocking collectives, exchange(): return lax.all_to_all(values, names, split_axis=0, concat_axis=0)  72.7 us
    ppermute x9, starting transfers between devices, permute(): return lax.ppermute(values, names, permutation(names, target))  48.1 us
    ppermute x9, waiting for transfers between devices, permute(): return lax.ppermute(values, names, permutation(names, target))  12.6 us
    pallas_call x1, Pallas kernels, hidden_gradient(): pl.pallas_call(hidden_kernel, grid_spec=pltpu.PrefetchScalarGridSpec(num_...  9.22 us
    all_to_all x1, starting transfers between devices, exchange(): return lax.all_to_all(values, names, split_axis=0, concat_axis=0)  8.72 us
    pallas_call x2, Pallas kernels, weight_parts(): pl.pallas_call(weight_kernel, grid_spec=pltpu.PrefetchScalarGridSpec(num_...  8.49 us
    pallas_call x2, Pallas kernels, plane_grams(): pl.pallas_call(gram_kernel, grid=(4,), in_specs=[pl.BlockSpec((4, 1, CHUN...  8.14 us
    all_to_all x1, waiting for transfers between devices, exchange(): return lax.all_to_all(values, names, split_axis=0, concat_axis=0)  7.82 us
  transfers between devices with their start and end apart: 10, of which 5 were waited for; matrix products, arithmetic and copies ran while one was open for 1% of the time, Pallas kernels for 12%

profile of v3, /device:TPU:1, one launch (start us, length us, event | category | flops | bytes accessed | tf_op | source)
XLA Modules:
  0.0 189.9 jit_solution(3666786819921085136)
XLA Ops:
  0.6 1.8 source.1
  2.4 23.5 %all_to_all.15.parts_ref = f32[8,32,128]{2,1,0:T(8,128)} all-to-all(f32[8,32,128]{2,1,0:T(8,128)} %get-tuple-element.11), channel_id=1, replica_groups=mesh['x'=4,'zh'=2,'y'=4,'c'=2,'t'=8] {'t'}, dimensions={0} | all-to-all | bytes 262144 | tf_op jit(solution)/shard_map/all_to_all | solution.py:40
  25.9 1.6 slices.1
  27.5 7.9 %collective-permute-start.4 = (bf16[144,256]{1,0:T(8,128)(2,1)}, bf16[144,256]{1,0:T(8,128)(2,1)S(1)}, u32[]{:S(2)}, u32[]{:S(2)}) collective-permute-start(bf16[144,256]{1,0:T(8,128)(2,1)} %get-tuple-element.12), channel_id=1, source_target_pairs={{0,64},{1,0},{2,192},{3,128},{4,320},{5,256},{6,448},{7,384},{64,6... | collective-permute-start | bytes 221192 | tf_op jit(solution)/shard_map/ppermute | solution.py:36
  35.4 1.5 collective-permute-start.3
  37.0 0.9 collective-permute-done.4
  37.8 0.0 collective-permute-done.3
  37.9 0.7 constant_dynamic-update-slice_fusion
  38.6 0.2 broadcast_in_dim.10
  38.8 49.2 %all_to_all.16 = bf16[16,304,256]{2,1,0:T(8,128)(2,1)S(1)} all-to-all(bf16[16,304,256]{2,1,0:T(8,128)(2,1)S(1)} %broadcast_in_dim.10), channel_id=1, replica_groups=mesh['x'=4,'zh'=2,'y'=4,'c'=2,'t'=8] {'x','y'}, dimensions={0} | all-to-all | bytes 4980736 | tf_op jit(solution)/shard_map/all_to_all | solution.py:40
  88.0 0.0 copy-start
  88.0 4.1 %collective-permute-start.5 = (bf16[16,304,256]{2,1,0:T(8,128)(2,1)S(1)}, bf16[16,304,256]{2,1,0:T(8,128)(2,1)}, u32[]{:S(2)}, u32[]{:S(2)}) collective-permute-start(bf16[16,304,256]{2,1,0:T(8,128)(2,1)S(1)} %all_to_all.16), channel_id=1, source_target_pairs={{0,8},{8,0},{1,9},{9,1},{2,10},{10,2},{3,11},{11,3},{4,12},{12,4},... | collective-permute-start | bytes 7471112 | tf_op jit(solution)/shard_map/ppermute | solution.py:36
  92.1 0.0 copy-done
  92.1 1.6 plane_sums.1
  93.7 8.7 %all-to-all-start.2 = ((f32[32,8,128]{2,1,0:T(8,128)}), f32[32,8,128]{2,1,0:T(8,128)S(1)}, u32[]{:S(2)}, u32[]{:S(2)}) async-start(f32[32,8,128]{2,1,0:T(8,128)} %plane_sums.1), calls=%async_computation.2 | async-start | bytes 262144 | tf_op jit(solution)/shard_map/all_to_all | solution.py:40
  102.4 4.1 %plane_grams.2.own_gram_ref = f32[4,128,128]{2,1,0:T(8,128)} custom-call(bf16[4,4,304,256]{3,2,1,0:T(8,128)(2,1)} %bitcast.13), custom_call_target="tpu_custom_call" | custom-call | flops 4294967296 | bytes 16777216 | tf_op jit(solution)/shard_map/plane_grams/pallas_call | solution.py:113
  106.5 0.0 collective-permute-done.5
  106.5 4.1 %plane_grams.3.other_gram_ref = f32[4,128,128]{2,1,0:T(8,128)} custom-call(bf16[4,4,304,256]{3,2,1,0:T(8,128)(2,1)} %bitcast.4.block_ref.other_rows_ref.other_ref), custom_call_target="tpu_custom_call" | custom-call | flops 4294967296 | bytes 16777216 | tf_op jit(solution)/shard_map/plane_grams/pallas_call | solution.py:113
  110.6 7.8 %all-to-all-done.2.tiles_ref = f32[32,8,128]{2,1,0:T(8,128)S(1)} async-done(((f32[32,8,128]{2,1,0:T(8,128)}), f32[32,8,128]{2,1,0:T(8,128)S(1)}, u32[]{:S(2)}, u32[]{:S(2)}) %all-to-all-start.2) | async-done | bytes 131104 | tf_op jit(solution)/shard_map/all_to_all | solution.py:40
  118.4 0.0 copy-start.2
  118.4 0.7 copy-done.2
  119.0 2.7 %mix.1 = (f32[8,128,128]{2,1,0:T(8,128)}, bf16[224,1024]{1,0:T(8,128)(2,1)}, f32[8,128]{1,0:T(8,128)}) custom-call(s32[1]{0:T(128)} %bitcast.1.core_ref, f32[4,128,128]{2,1,0:T(8,128)} %plane_grams.2.own_gram_ref, f32[4,128,128]{2,1,0:T(8,128)} %plane_grams.3.other_gram_ref, bf16[4,4,304,256]{3,2,1,0:T(8,128)(2,1)} %bitcast.14, ...), custom_call_target="tpu_custom_call" | custom-call | tf_op jit(solution)/shard_map/mix/pallas_call | solution.py:161
  121.8 0.0 copy-start.4
  121.8 4.2 %weight_parts.3 = bf16[4,224,256]{2,1,0:T(8,128)(2,1)} custom-call(s32[1]{0:T(128)} %bitcast.place_ref, bf16[224,1024]{1,0:T(8,128)(2,1)} %get-tuple-element.15.product_ref, bf16[4,4,304,256]{3,2,1,0:T(8,128)(2,1)} %bitcast.15, bf16[4,4,304,256]{3,2,1,0:T(8,128)(2,1)} %bitcast.4.block_ref.other_rows_ref.other_ref), custom_call_target="tpu_custom_call" | custom-call | flops 469762048 | bytes 4194304 | tf_op jit(solution)/shard_map/weight_parts/pallas_call | solution.py:208
  126.0 1.9 %collective-permute-start.6 = (bf16[4,224,256]{2,1,0:T(8,128)(2,1)}, bf16[4,224,256]{2,1,0:T(8,128)(2,1)S(1)}, u32[]{:S(2)}, u32[]{:S(2)}) collective-permute-start(bf16[4,224,256]{2,1,0:T(8,128)(2,1)} %weight_parts.3), channel_id=1, source_target_pairs={{0,1},{1,0},{2,3},{3,2},{4,5},{5,4},{6,7},{7,6},{8,9},{9,8},{10,11... | collective-permute-start | bytes 1376264 | tf_op jit(solution)/shard_map/ppermute | solution.py:36
  127.9 0.0 copy-done.4
  127.9 3.4 %collective-permute-start = (bf16[1,224,256]{2,1,0:T(8,128)(2,1)S(1)}, bf16[1,224,256]{2,1,0:T(8,128)(2,1)S(1)}, u32[]{:S(2)}, u32[]{:S(2)}) collective-permute-start(bf16[1,224,256]{2,1,0:T(8,128)(2,1)S(1)} %bitcast.18), channel_id=1, source_target_pairs={{0,4},{1,5},{2,6},{3,7},{4,0},{5,1},{6,2},{7,3},{8,12},{9,13},{10,... | collective-permute-start | bytes 344072 | tf_op jit(solution)/shard_map/ppermute | solution.py:36
  131.3 7.4 %collective-permute-done = bf16[1,224,256]{2,1,0:T(8,128)(2,1)S(1)} collective-permute-done((bf16[1,224,256]{2,1,0:T(8,128)(2,1)S(1)}, bf16[1,224,256]{2,1,0:T(8,128)(2,1)S(1)}, u32[]{:S(2)}, u32[]{:S(2)}) %collective-permute-start) | collective-permute-done | bytes 114720 | tf_op jit(solution)/shard_map/ppermute | solution.py:36
  138.8 8.4 %collective-permute-start.1 = (bf16[2,224,256]{2,1,0:T(8,128)(2,1)S(1)}, bf16[2,224,256]{2,1,0:T(8,128)(2,1)S(1)}, u32[]{:S(2)}, u32[]{:S(2)}) collective-permute-start(bf16[2,224,256]{2,1,0:T(8,128)(2,1)S(1)} %pad_maximum_fusion.1), channel_id=1, source_target_pairs={{0,2},{1,3},{2,0},{3,1},{4,6},{5,7},{6,4},{7,5},{8,10},{9,11},{10,... | collective-permute-start | bytes 688136 | tf_op jit(solution)/shard_map/ppermute | solution.py:36
  147.2 4.3 %weight_parts.2 = f32[4,224,256]{2,1,0:T(8,128)} custom-call(s32[1]{0:T(128)} %bitcast.place_ref, bf16[224,1024]{1,0:T(8,128)(2,1)} %get-tuple-element.15.product_ref, bf16[4,4,304,256]{3,2,1,0:T(8,128)(2,1)} %bitcast.16, bf16[4,4,304,256]{3,2,1,0:T(8,128)(2,1)} %bitcast.4.block_ref.other_rows_ref.other_ref), custom_call_target="tpu_custom_call" | custom-call | flops 469762048 | bytes 4194304 | tf_op jit(solution)/shard_map/weight_parts/pallas_call | solution.py:208
  151.5 0.0 collective-permute-done.6
  151.5 1.3 fusion
  152.7 1.9 %collective-permute-start.7 = (bf16[2,224,256]{2,1,0:T(8,128)(2,1)S(1)}, bf16[2,224,256]{2,1,0:T(8,128)(2,1)S(1)}, u32[]{:S(2)}, u32[]{:S(2)}) collective-permute-start(bf16[2,224,256]{2,1,0:T(8,128)(2,1)S(1)} %get-tuple-element.17), channel_id=1, source_target_pairs={{0,2},{1,3},{2,0},{3,1},{4,6},{5,7},{6,4},{7,5},{8,10},{9,11},{10,... | collective-permute-start | bytes 688136 | tf_op jit(solution)/shard_map/ppermute | solution.py:36
  154.7 0.0 collective-permute-done.1
  154.7 0.0 copy-start.1
  154.7 10.7 %collective-permute-start.2 = (bf16[4,224,256]{2,1,0:T(8,128)(2,1)S(1)}, bf16[4,224,256]{2,1,0:T(8,128)(2,1)S(1)}, u32[]{:S(2)}, u32[]{:S(2)}) collective-permute-start(bf16[4,224,256]{2,1,0:T(8,128)(2,1)S(1)} %pad_maximum_fusion.near_ref), channel_id=1, source_target_pairs={{0,1},{1,0},{2,3},{3,2},{4,5},{5,4},{6,7},{7,6},{8,9},{9,8},{10,11... | collective-permute-start | bytes 1376264 | tf_op jit(solution)/shard_map/ppermute | solution.py:36
  165.5 0.2 collective-permute-done.7
  165.7 8.1 %collective-permute-start.8 = (bf16[224,256]{1,0:T(8,128)(2,1)S(1)}, bf16[224,256]{1,0:T(8,128)(2,1)S(1)}, u32[]{:S(2)}, u32[]{:S(2)}) collective-permute-start(bf16[224,256]{1,0:T(8,128)(2,1)S(1)} %fusion.4), channel_id=1, source_target_pairs={{0,4},{1,5},{2,6},{3,7},{4,0},{5,1},{6,2},{7,3},{8,12},{9,13},{10,... | collective-permute-start | bytes 344072 | tf_op jit(solution)/shard_map/ppermute | solution.py:36
  173.8 1.2 slice.51
  175.0 4.1 %collective-permute-done.2.far_ref = bf16[4,224,256]{2,1,0:T(8,128)(2,1)S(1)} collective-permute-done((bf16[4,224,256]{2,1,0:T(8,128)(2,1)S(1)}, bf16[4,224,256]{2,1,0:T(8,128)(2,1)S(1)}, u32[]{:S(2)}, u32[]{:S(2)}) %collective-permute-start.2) | collective-permute-done | bytes 458784 | tf_op jit(solution)/shard_map/ppermute | solution.py:36
  179.1 0.0 copy-start.3
  179.2 0.0 copy-done.1
  179.2 0.8 copy-done.3
  179.9 9.2 %hidden_gradient.1 = bf16[224,1024]{1,0:T(8,128)(2,1)} custom-call(s32[1]{0:T(128)} %bitcast.place_ref, s32[1]{0:T(128)} %bitcast.1.core_ref, bf16[4,224,256]{2,1,0:T(8,128)(2,1)} %copy-done.1, bf16[4,224,256]{2,1,0:T(8,128)(2,1)} %copy-done.3, bf16[4,4,304,256]{3,2,1,0:T(8,128)(2,1)} %bitcast.17, ...), custom_call_target="tpu_custom_call" | custom-call | flops 939524096 | bytes 8388608 | tf_op jit(solution)/shard_map/hidden_gradient/pallas_call | solution.py:271
  189.2 0.0 collective-permute-done.8
  189.2 0.7 fusion.3
  (8 shorter events, 0.1 us)
Async XLA Ops:
  27.5 10.4 %collective-permute-start.4 = (bf16[144,256]{1,0:T(8,128)(2,1)}, bf16[144,256]{1,0:T(8,128)(2,1)S(1)}, u32[]{:S(2)}, u32[]{:S(2)}) collective-permute-start(bf16[144,256]{1,0:T(8,128)(2,1)} %get-tuple-element.12), channel_id=1, source_target_pairs={{0,64},{1,0},{2,192},{3,128},{4,320},{5,256},{6,448},{7,384},{64,6... | collective-permute-start | bytes 221192 | tf_op jit(solution)/shard_map/ppermute | solution.py:36
  35.4 2.4 %collective-permute-start.3 = (bf16[144,256]{1,0:T(8,128)(2,1)}, bf16[144,256]{1,0:T(8,128)(2,1)S(1)}, u32[]{:S(2)}, u32[]{:S(2)}) collective-permute-start(bf16[144,256]{1,0:T(8,128)(2,1)} %get-tuple-element.12), channel_id=1, source_target_pairs={{0,0},{1,64},{2,128},{3,192},{4,256},{5,320},{6,384},{7,448},{64,1... | collective-permute-start | bytes 221192 | tf_op jit(solution)/shard_map/ppermute | solution.py:36
  88.0 4.1 %copy-start = (bf16[16,304,256]{2,1,0:T(8,128)(2,1)}, bf16[16,304,256]{2,1,0:T(8,128)(2,1)S(1)}, u32[]{:S(2)}) copy-start(bf16[16,304,256]{2,1,0:T(8,128)(2,1)S(1)} %all_to_all.16) | copy-start | bytes 7471108
  88.0 18.5 %collective-permute-start.5 = (bf16[16,304,256]{2,1,0:T(8,128)(2,1)S(1)}, bf16[16,304,256]{2,1,0:T(8,128)(2,1)}, u32[]{:S(2)}, u32[]{:S(2)}) collective-permute-start(bf16[16,304,256]{2,1,0:T(8,128)(2,1)S(1)} %all_to_all.16), channel_id=1, source_target_pairs={{0,8},{8,0},{1,9},{9,1},{2,10},{10,2},{3,11},{11,3},{4,12},{12,4},... | collective-permute-start | bytes 7471112 | tf_op jit(solution)/shard_map/ppermute | solution.py:36
  93.7 24.7 %all-to-all-start.2 = ((f32[32,8,128]{2,1,0:T(8,128)}), f32[32,8,128]{2,1,0:T(8,128)S(1)}, u32[]{:S(2)}, u32[]{:S(2)}) async-start(f32[32,8,128]{2,1,0:T(8,128)} %plane_sums.1), calls=%async_computation.2 | async-start | bytes 262144 | tf_op jit(solution)/shard_map/all_to_all | solution.py:40
  118.4 0.7 copy-start.2
  121.8 6.1 %copy-start.4 = (bf16[224,256]{1,0:T(8,128)(2,1)S(1)}, bf16[224,256]{1,0:T(8,128)(2,1)}, u32[]{:S(2)}) copy-start(bf16[224,256]{1,0:T(8,128)(2,1)} %param.7) | copy-start | bytes 344068
  126.0 25.5 %collective-permute-start.6 = (bf16[4,224,256]{2,1,0:T(8,128)(2,1)}, bf16[4,224,256]{2,1,0:T(8,128)(2,1)S(1)}, u32[]{:S(2)}, u32[]{:S(2)}) collective-permute-start(bf16[4,224,256]{2,1,0:T(8,128)(2,1)} %weight_parts.3), channel_id=1, source_target_pairs={{0,1},{1,0},{2,3},{3,2},{4,5},{5,4},{6,7},{7,6},{8,9},{9,8},{10,11... | collective-permute-start | bytes 1376264 | tf_op jit(solution)/shard_map/ppermute | solution.py:36
  127.9 10.9 %collective-permute-start = (bf16[1,224,256]{2,1,0:T(8,128)(2,1)S(1)}, bf16[1,224,256]{2,1,0:T(8,128)(2,1)S(1)}, u32[]{:S(2)}, u32[]{:S(2)}) collective-permute-start(bf16[1,224,256]{2,1,0:T(8,128)(2,1)S(1)} %bitcast.18), channel_id=1, source_target_pairs={{0,4},{1,5},{2,6},{3,7},{4,0},{5,1},{6,2},{7,3},{8,12},{9,13},{10,... | collective-permute-start | bytes 344072 | tf_op jit(solution)/shard_map/ppermute | solution.py:36
  138.8 15.9 %collective-permute-start.1 = (bf16[2,224,256]{2,1,0:T(8,128)(2,1)S(1)}, bf16[2,224,256]{2,1,0:T(8,128)(2,1)S(1)}, u32[]{:S(2)}, u32[]{:S(2)}) collective-permute-start(bf16[2,224,256]{2,1,0:T(8,128)(2,1)S(1)} %pad_maximum_fusion.1), channel_id=1, source_target_pairs={{0,2},{1,3},{2,0},{3,1},{4,6},{5,7},{6,4},{7,5},{8,10},{9,11},{10,... | collective-permute-start | bytes 688136 | tf_op jit(solution)/shard_map/ppermute | solution.py:36
  152.7 12.9 %collective-permute-start.7 = (bf16[2,224,256]{2,1,0:T(8,128)(2,1)S(1)}, bf16[2,224,256]{2,1,0:T(8,128)(2,1)S(1)}, u32[]{:S(2)}, u32[]{:S(2)}) collective-permute-start(bf16[2,224,256]{2,1,0:T(8,128)(2,1)S(1)} %get-tuple-element.17), channel_id=1, source_target_pairs={{0,2},{1,3},{2,0},{3,1},{4,6},{5,7},{6,4},{7,5},{8,10},{9,11},{10,... | collective-permute-start | bytes 688136 | tf_op jit(solution)/shard_map/ppermute | solution.py:36
  154.7 24.4 %copy-start.1 = (bf16[4,224,256]{2,1,0:T(8,128)(2,1)}, bf16[4,224,256]{2,1,0:T(8,128)(2,1)S(1)}, u32[]{:S(2)}) copy-start(bf16[4,224,256]{2,1,0:T(8,128)(2,1)S(1)} %pad_maximum_fusion.near_ref) | copy-start | bytes 1376260
  154.7 24.4 %collective-permute-start.2 = (bf16[4,224,256]{2,1,0:T(8,128)(2,1)S(1)}, bf16[4,224,256]{2,1,0:T(8,128)(2,1)S(1)}, u32[]{:S(2)}, u32[]{:S(2)}) collective-permute-start(bf16[4,224,256]{2,1,0:T(8,128)(2,1)S(1)} %pad_maximum_fusion.near_ref), channel_id=1, source_target_pairs={{0,1},{1,0},{2,3},{3,2},{4,5},{5,4},{6,7},{7,6},{8,9},{9,8},{10,11... | collective-permute-start | bytes 1376264 | tf_op jit(solution)/shard_map/ppermute | solution.py:36
  165.7 23.5 %collective-permute-start.8 = (bf16[224,256]{1,0:T(8,128)(2,1)S(1)}, bf16[224,256]{1,0:T(8,128)(2,1)S(1)}, u32[]{:S(2)}, u32[]{:S(2)}) collective-permute-start(bf16[224,256]{1,0:T(8,128)(2,1)S(1)} %fusion.4), channel_id=1, source_target_pairs={{0,4},{1,5},{2,6},{3,7},{4,0},{5,1},{6,2},{7,3},{8,12},{9,13},{10,... | collective-permute-start | bytes 344072 | tf_op jit(solution)/shard_map/ppermute | solution.py:36
  179.1 0.8 copy-start.3

commit v4 on v3

v4 whole, which is shorter than its diff:
```python
import functools
import itertools

import jax
import jax.numpy as jnp
from jax import lax
from jax.experimental import pallas as pl
from jax.experimental.pallas import tpu as pltpu
from jax.sharding import Mesh, PartitionSpec as P


NAMES = ("x", "zh", "y", "c", "t")
SIZES = {"x": 4, "zh": 2, "y": 4, "c": 2, "t": 8}
BF16 = jnp.bfloat16
F32 = jnp.float32
ROWS = 128
WIDTH = 256
CHUNK = 3 * ROWS
PARAMS = pltpu.CompilerParams(vmem_limit_bytes=16 << 20)
VMEM = pl.BlockSpec(memory_space=pltpu.VMEM)
SMEM = pl.BlockSpec(memory_space=pltpu.SMEM)


def permutation(names, target):
    pairs = []
    for place in itertools.product(*[range(SIZES[n]) for n in names]):
        goal = target(dict(zip(names, place)))
        source, dest = 0, 0
        for name, coordinate in zip(names, place):
            source = source * SIZES[name] + coordinate
            dest = dest * SIZES[name] + goal[name]
        pairs.append((source, dest))
    return pairs


def permute(values, names, target):
    return lax.ppermute(values, names, permutation(names, target))


def exchange(values, names):
    return lax.all_to_all(values, names, split_axis=0, concat_axis=0)


def to_plane(flip):
    def target(d):
        return {"x": d["t"] // 2, "zh": (d["t"] + flip) % 2, "t": 2 * d["x"] + d["zh"]}

    return target


def gram(values):
    return lax.dot_general(values, values, (((1,), (1,)), ((), ())), preferred_element_type=F32)


def center(values):
    floats = values.astype(F32)
    return (floats - jnp.mean(floats, axis=0, keepdims=True)).astype(BF16)


def source_kernel(acts_ref, partner_ref, out_ref):
    out_ref[:ROWS, :] = center(acts_ref[...])
    out_ref[ROWS:, :] = center(partner_ref[...])


def split(values, parts):
    pieces = []
    for _ in range(parts):
        piece = values.astype(BF16)
        values = values - piece.astype(F32)
        pieces.append(piece)
    return pieces


def chunk_kernel(flag_ref, first_ref, second_ref, chunk_ref):
    even = flag_ref[0] == 0
    first, second = first_ref[...], second_ref[...]
    low = jnp.where(even, first, second)
    high = jnp.where(even, second, first)
    chunk_ref[:ROWS, :] = low[:ROWS]
    chunk_ref[ROWS : 2 * ROWS, :] = high[:ROWS]
    gram_y = gram(jnp.concatenate([low[ROWS:], high[ROWS:]], axis=1))
    chunk_ref[2 * ROWS :, :] = jnp.concatenate(split(gram_y, 2), axis=1)


def gram_kernel(plane_ref, x_ref, y_ref, tiles_ref):
    sums = jnp.zeros((3, ROWS), F32)
    for y in range(0, 4, 2):
        rows = [
            jnp.concatenate(
                [plane_ref[t // 2, y + i, pl.ds((t % 2) * ROWS, ROWS), :] for t in range(8)], axis=1
            )
            for i in range(2)
        ]
        pair = gram(jnp.concatenate(rows, axis=0))
        for i in range(2):
            gram_x = pair[i * ROWS : (i + 1) * ROWS, i * ROWS : (i + 1) * ROWS]
            gram_y = jnp.zeros((ROWS, ROWS), F32)
            for x in range(4):
                parts = plane_ref[x, y + i, pl.ds(2 * ROWS, ROWS), :].astype(F32)
                gram_y = gram_y + (parts[:, :ROWS] + parts[:, ROWS:])
            x_ref[y + i] = gram_x
            y_ref[y + i] = gram_y
            products = (gram_x * gram_x, gram_y * gram_y, gram_x * gram_y)
            sums = sums + jnp.concatenate(
                [jnp.sum(v, axis=0, keepdims=True) for v in products], axis=0
            )
    tile = jnp.concatenate([sums, jnp.zeros((5, ROWS), F32)], axis=0)
    tiles_ref[...] = jnp.broadcast_to(tile[None], tiles_ref.shape)


def plane_grams(plane):
    return pl.pallas_call(
        gram_kernel,
        in_specs=[VMEM],
        out_specs=[VMEM] * 3,
        out_shape=[
            jax.ShapeDtypeStruct((4, ROWS, ROWS), F32),
            jax.ShapeDtypeStruct((4, ROWS, ROWS), F32),
            jax.ShapeDtypeStruct((16, 8, ROWS), F32),
        ],
        compiler_params=PARAMS,
        cost_estimate=pl.CostEstimate(
            flops=2 << 30, bytes_accessed=4 << 20, transcendentals=0
        ),
        name="plane_grams",
    )(plane)


def mix_kernel(
    scale, core_ref, own_x_ref, own_y_ref, other_x_ref, other_y_ref, tiles_ref, hidden_ref,
    mixed_ref, product_ref, cka_ref,
):
    sums = jnp.sum(jnp.sum(tiles_ref[...], axis=0), axis=1, keepdims=True)
    sxx, syy, sxy = sums[0:1], sums[1:2], sums[2:3]
    root = jnp.sqrt(sxx * syy)
    ratio = jnp.broadcast_to(sxy / sxx, (1, ROWS))
    coef = jnp.broadcast_to(-2.0 * scale / root, (1, ROWS))
    cka_ref[...] = jnp.broadcast_to(sxy / root, cka_ref.shape)
    core = core_ref[0]
    for b in range(8):
        x_ref, y_ref = (own_x_ref, own_y_ref) if b < 4 else (other_x_ref, other_y_ref)
        mixed = coef * (y_ref[b % 4] - ratio * x_ref[b % 4])
        mixed_ref[b] = mixed
        place = b % 4 * 2 + (core if b < 4 else 1 - core)
        hidden = hidden_ref[:, pl.ds(pl.multiple_of(place * ROWS, ROWS), ROWS)]
        product = jnp.dot(
            jnp.concatenate([hidden, hidden], axis=1),
            jnp.concatenate(split(mixed, 2), axis=0),
            preferred_element_type=F32,
        )
        product_ref[:, b * ROWS : (b + 1) * ROWS] = product.astype(BF16)


def mix(core, own, other, tiles, hidden, scale):
    return pl.pallas_call(
        functools.partial(mix_kernel, scale),
        in_specs=[SMEM] + [VMEM] * 6,
        out_specs=[VMEM] * 3,
        out_shape=[
            jax.ShapeDtypeStruct((8, ROWS, ROWS), F32),
            jax.ShapeDtypeStruct(hidden.shape, BF16),
            jax.ShapeDtypeStruct((8, ROWS), F32),
        ],
        compiler_params=PARAMS,
        name="mix",
    )(core, own[0], own[1], other[0], other[1], tiles, hidden)


def column_block(place, k):
    return lax.bitwise_xor(place, (k % 2) * 4 + (k // 2 % 2) * 2 + k // 4)


def token_rows(ref, t):
    start = pl.multiple_of(lax.rem(t, 2) * ROWS, ROWS)
    return ref[lax.div(t, 2), :, pl.ds(start, ROWS), :].reshape(4 * ROWS, WIDTH)


def weight_kernel(first, place_ref, product_ref, own_ref, other_ref, out_ref):
    half = 4 * ROWS
    for k in range(4):
        t = column_block(place_ref[0], first + k)
        value = jnp.dot(
            product_ref[:, :half], token_rows(own_ref, t), preferred_element_type=F32
        )
        value = value + jnp.dot(
            product_ref[:, half:], token_rows(other_ref, t), preferred_element_type=F32
        )
        out_ref[k] = value.astype(out_ref.dtype)


def weight_parts(place, product, plane, other, first, dtype):
    units = product.shape[0]
    return pl.pallas_call(
        functools.partial(weight_kernel, first),
        in_specs=[SMEM] + [VMEM] * 3,
        out_specs=VMEM,
        out_shape=jax.ShapeDtypeStruct((4, units, WIDTH), dtype),
        compiler_params=PARAMS,
        cost_estimate=pl.CostEstimate(
            flops=2 * units * 8 * ROWS * 4 * WIDTH, bytes_accessed=4 << 20, transcendentals=0
        ),
        name="weight_parts",
    )(place, product, plane, other)


def hidden_kernel(
    place_ref, core_ref, near_ref, far_ref, own_ref, other_ref, mixed_ref, out_ref
):
    for ref, first in ((own_ref, 0), (other_ref, 4)):
        total = None
        for k in range(8):
            product = lax.dot_general(
                near_ref[k] if k < 4 else far_ref[k - 4],
                token_rows(ref, column_block(place_ref[0], k)),
                (((1,), (1,)), ((), ())),
                preferred_element_type=F32,
            )
            total = product if total is None else total + product
        for y in range(4):
            high, low = split(total[:, y * ROWS : (y + 1) * ROWS], 2)
            mixed_high, mixed_low = split(mixed_ref[first + y], 2)
            value = lax.dot_general(
                jnp.concatenate([high, high, low], axis=1),
                jnp.concatenate([mixed_high, mixed_low, mixed_high], axis=1),
                (((1,), (1,)), ((), ())),
                preferred_element_type=F32,
            )
            place = y * 2 + (core_ref[0] if first == 0 else 1 - core_ref[0])
            out_ref[:, pl.ds(pl.multiple_of(place * ROWS, ROWS), ROWS)] = value.astype(BF16)


def hidden_gradient(place, core, near, far, plane, other, mixed):
    units = near.shape[1]
    tokens = 8 * ROWS
    return pl.pallas_call(
        hidden_kernel,
        in_specs=[SMEM] * 2 + [VMEM] * 5,
        out_specs=VMEM,
        out_shape=jax.ShapeDtypeStruct((units, tokens), BF16),
        compiler_params=PARAMS,
        cost_estimate=pl.CostEstimate(
            flops=2 * units * tokens * 8 * WIDTH, bytes_accessed=8 << 20, transcendentals=0
        ),
        name="hidden_gradient",
    )(place, core, near, far, plane, other, mixed)


def flip(bit):
    return lambda d: {"t": d["t"] ^ bit}


def local(acts, partner, hidden, down_weight):
    scale = float(ROWS * 64 * WIDTH * 8)
    shape = jax.ShapeDtypeStruct
    place = lax.axis_index("t").astype(jnp.int32).reshape(1)
    core = lax.axis_index("c").astype(jnp.int32).reshape(1)
    half = lax.axis_index("zh").astype(jnp.int32).reshape(1)
    near = down_weight[None]
    far = permute(near, ("t",), flip(4))
    near = jnp.concatenate([near, far], axis=0)
    far = permute(near, ("t",), flip(2))
    near = jnp.concatenate([near, far], axis=0)
    far = permute(near, ("t",), flip(1))
    piece = pl.pallas_call(
        source_kernel,
        in_specs=[VMEM] * 2,
        out_specs=VMEM,
        out_shape=shape((2 * ROWS, WIDTH), BF16),
        compiler_params=PARAMS,
        name="source",
    )(acts, partner)
    first = permute(piece, ("x", "zh", "t"), to_plane(0))
    second = permute(piece, ("x", "zh", "t"), to_plane(1))
    chunk = pl.pallas_call(
        chunk_kernel,
        in_specs=[SMEM] + [VMEM] * 2,
        out_specs=VMEM,
        out_shape=shape((CHUNK, WIDTH), BF16),
        compiler_params=PARAMS,
        name="chunk",
    )(half, first, second)
    plane = exchange(jnp.broadcast_to(chunk[None], (16,) + chunk.shape), ("x", "y"))
    other = permute(plane, ("c",), lambda d: {"c": 1 - d["c"]})
    plane = plane.reshape(4, 4, CHUNK, WIDTH)
    other = other.reshape(4, 4, CHUNK, WIDTH)
    own_grams = plane_grams(plane)
    tiles = exchange(own_grams[2], ("c", "t"))
    mixed, product, cka = mix(core, own_grams, plane_grams(other), tiles, hidden, scale)
    sent = weight_parts(place, product, plane, other, 4, BF16)
    sent = permute(sent, ("t",), flip(1))
    kept = weight_parts(place, product, plane, other, 0, F32)
    later = permute((kept[2:] + sent[2:].astype(F32)).astype(BF16), ("t",), flip(2))
    kept = kept[:2] + sent[:2].astype(F32)
    last = permute((kept[1] + later[1].astype(F32)).astype(BF16), ("t",), flip(4))
    grad_weight = kept[0] + later[0].astype(F32) + last.astype(F32)
    grad_hidden = hidden_gradient(place, core, near, far, plane, other, mixed)
    return (grad_hidden, grad_weight, cka[0, 0])


def solution(mesh):
    shape = tuple(SIZES[n] for n in NAMES)
    fine = Mesh(mesh.devices.reshape(shape), NAMES)
    spec = P(("x", "zh", "y", "c"), "t")
    return jax.shard_map(
        local, mesh=fine, in_specs=(spec,) * 4, out_specs=(spec, spec, P()), check_vma=False
    )
```

time: 193 us -> 178 us (0.922)
  the two profiles are of different devices: /device:TPU:1 before, /device:TPU:32 now
where the time goes in v4:
time: 178 us; the launch traced here: 177 us
  starting transfers between devices  58.7 us (33%)
  waiting for transfers between devices  50.2 us (28%)
  blocking collectives  42.4 us (24%)
  Pallas kernels  15.3 us (9%)
  local copies, waits for them, and re-layouts  8.45 us (5%)
    ppermute x9, waiting for transfers between devices, permute(): return lax.ppermute(values, names, permutation(names, target))  45.8 us
    all_to_all x1, blocking collectives, exchange(): return lax.all_to_all(values, names, split_axis=0, concat_axis=0)  42.4 us
    ppermute x9, starting transfers between devices, permute(): return lax.ppermute(values, names, permutation(names, target))  39.8 us
    all_to_all x1, starting transfers between devices, exchange(): return lax.all_to_all(values, names, split_axis=0, concat_axis=0)  18.8 us
    unnamed x20, local copies, waits for them, and re-layouts  7.64 us
    pallas_call x2, Pallas kernels, weight_parts(): pl.pallas_call(functools.partial(weight_kernel, first), in_specs=[SMEM] +...  5.12 us
    pallas_call x2, Pallas kernels, plane_grams(): pl.pallas_call(gram_kernel, in_specs=[VMEM], out_specs=[VMEM] * 3, out_sh...  4.75 us
    pallas_call x1, Pallas kernels, hidden_gradient(): pl.pallas_call(hidden_kernel, in_specs=[SMEM] * 2 + [VMEM] * 5, out_specs...  4.6 us
  transfers between devices with their start and end apart: 10, of which 8 were waited for; matrix products, arithmetic and copies ran while one was open for 0% of the time, Pallas kernels for 7%

profile of v4, /device:TPU:32, one launch (start us, length us, event | category | flops | bytes accessed | tf_op | source)
XLA Modules:
  0.0 176.8 jit_solution(11704190217083326067)
XLA Ops:
  0.6 0.0 copy-start.7
  0.6 0.8 copy-done.7
  1.5 0.0 copy-start.8
  1.5 0.8 copy-done.8
  2.4 14.4 %collective-permute-start.3 = (bf16[256,256]{1,0:T(8,128)(2,1)S(1)}, bf16[256,256]{1,0:T(8,128)(2,1)S(1)}, u32[]{:S(2)}, u32[]{:S(2)}) collective-permute-start(bf16[256,256]{1,0:T(8,128)(2,1)S(1)} %source.1), channel_id=1, source_target_pairs={{0,0},{1,64},{2,128},{3,192},{4,256},{5,320},{6,384},{7,448},{64,1... | collective-permute-start | bytes 393224 | tf_op jit(solution)/shard_map/ppermute | solution.py:37
  16.7 1.9 %collective-permute-start.4 = (bf16[256,256]{1,0:T(8,128)(2,1)S(1)}, bf16[256,256]{1,0:T(8,128)(2,1)S(1)}, u32[]{:S(2)}, u32[]{:S(2)}) collective-permute-start(bf16[256,256]{1,0:T(8,128)(2,1)S(1)} %source.1), channel_id=1, source_target_pairs={{0,64},{1,0},{2,192},{3,128},{4,320},{5,256},{6,448},{7,384},{64,6... | collective-permute-start | bytes 393224 | tf_op jit(solution)/shard_map/ppermute | solution.py:37
  18.7 1.5 collective-permute-done.3.first_ref
  20.2 12.1 %collective-permute-done.4.second_ref = bf16[256,256]{1,0:T(8,128)(2,1)S(1)} collective-permute-done((bf16[256,256]{1,0:T(8,128)(2,1)S(1)}, bf16[256,256]{1,0:T(8,128)(2,1)S(1)}, u32[]{:S(2)}, u32[]{:S(2)}) %collective-permute-start.4) | collective-permute-done | bytes 131104 | tf_op jit(solution)/shard_map/ppermute | solution.py:37
  32.3 0.2 chunk.1
  32.5 0.3 broadcast_in_dim.10
  32.8 42.4 %all_to_all.10 = bf16[16,384,256]{2,1,0:T(8,128)(2,1)S(1)} all-to-all(bf16[16,384,256]{2,1,0:T(8,128)(2,1)S(1)} %broadcast_in_dim.10), channel_id=1, replica_groups=mesh['x'=4,'zh'=2,'y'=4,'c'=2,'t'=8] {'x','y'}, dimensions={0} | all-to-all | bytes 6291456 | tf_op jit(solution)/shard_map/all_to_all | solution.py:41
  75.2 1.9 %collective-permute-start.5 = (bf16[16,384,256]{2,1,0:T(8,128)(2,1)S(1)}, bf16[16,384,256]{2,1,0:T(8,128)(2,1)}, u32[]{:S(2)}, u32[]{:S(2)}) collective-permute-start(bf16[16,384,256]{2,1,0:T(8,128)(2,1)S(1)} %all_to_all.10), channel_id=1, source_target_pairs={{0,8},{8,0},{1,9},{9,1},{2,10},{10,2},{3,11},{11,3},{4,12},{12,4},... | collective-permute-start | bytes 9437192 | tf_op jit(solution)/shard_map/ppermute | solution.py:37
  77.1 1.4 plane_grams.2
  78.6 0.0 copy-start.1
  78.6 0.7 copy-done.1
  79.3 18.8 %all-to-all-start.1 = ((f32[16,8,128]{2,1,0:T(8,128)}), f32[16,8,128]{2,1,0:T(8,128)S(1)}, u32[]{:S(2)}, u32[]{:S(2)}) async-start(f32[16,8,128]{2,1,0:T(8,128)} %get-tuple-element.15), calls=%async_computation.1 | async-start | bytes 131072 | tf_op jit(solution)/shard_map/all_to_all | solution.py:41
  98.1 0.0 collective-permute-done.5
  98.1 3.3 %plane_grams.3 = (f32[4,128,128]{2,1,0:T(8,128)S(1)}, f32[4,128,128]{2,1,0:T(8,128)S(1)}, f32[16,8,128]{2,1,0:T(8,128)}) custom-call(bf16[4,4,384,256]{3,2,1,0:T(8,128)(2,1)} %bitcast.5.plane_ref.other_ref), custom_call_target="tpu_custom_call" | custom-call | flops 2147483648 | bytes 4194304 | tf_op jit(solution)/shard_map/plane_grams/pallas_call | solution.py:112
  101.4 0.0 copy-start.3
  101.4 0.7 copy-done.3
  102.1 0.0 copy-start.5
  102.1 0.7 copy-done.5
  102.8 4.4 %all-to-all-done.1.tiles_ref = f32[16,8,128]{2,1,0:T(8,128)S(1)} async-done(((f32[16,8,128]{2,1,0:T(8,128)}), f32[16,8,128]{2,1,0:T(8,128)S(1)}, u32[]{:S(2)}, u32[]{:S(2)}) %all-to-all-start.1) | async-done | bytes 65568 | tf_op jit(solution)/shard_map/all_to_all | solution.py:41
  107.2 1.0 copy-done
  108.2 0.9 copy-done.2
  109.2 0.9 copy-done.4
  110.1 0.9 copy-done.6
  111.1 0.6 mix.1
  111.6 0.0 copy-start.9
  111.6 2.6 %weight_parts.3 = bf16[4,224,256]{2,1,0:T(8,128)(2,1)S(1)} custom-call(s32[1]{0:T(128)} %bitcast.place_ref, bf16[224,1024]{1,0:T(8,128)(2,1)S(1)} %get-tuple-element.17.product_ref, bf16[4,4,384,256]{3,2,1,0:T(8,128)(2,1)S(1)} %bitcast.14, bf16[4,4,384,256]{3,2,1,0:T(8,128)(2,1)} %bitcast.5.plane_ref.other_ref), custom_call_target="tpu_custom_call" | custom-call | flops 469762048 | bytes 4194304 | tf_op jit(solution)/shard_map/weight_parts/pallas_call | solution.py:193
  114.2 3.7 %collective-permute-start.6 = (bf16[4,224,256]{2,1,0:T(8,128)(2,1)S(1)}, bf16[4,224,256]{2,1,0:T(8,128)(2,1)S(1)}, u32[]{:S(2)}, u32[]{:S(2)}) collective-permute-start(bf16[4,224,256]{2,1,0:T(8,128)(2,1)S(1)} %weight_parts.3), channel_id=1, source_target_pairs={{0,1},{1,0},{2,3},{3,2},{4,5},{5,4},{6,7},{7,6},{8,9},{9,8},{10,11... | collective-permute-start | bytes 1376264 | tf_op jit(solution)/shard_map/ppermute | solution.py:37
  117.9 0.0 copy-done.9
  117.9 2.6 %collective-permute-start = (bf16[1,224,256]{2,1,0:T(8,128)(2,1)S(1)}, bf16[1,224,256]{2,1,0:T(8,128)(2,1)S(1)}, u32[]{:S(2)}, u32[]{:S(2)}) collective-permute-start(bf16[1,224,256]{2,1,0:T(8,128)(2,1)S(1)} %bitcast.17), channel_id=1, source_target_pairs={{0,4},{1,5},{2,6},{3,7},{4,0},{5,1},{6,2},{7,3},{8,12},{9,13},{10,... | collective-permute-start | bytes 344072 | tf_op jit(solution)/shard_map/ppermute | solution.py:37
  120.5 15.5 %collective-permute-done = bf16[1,224,256]{2,1,0:T(8,128)(2,1)S(1)} collective-permute-done((bf16[1,224,256]{2,1,0:T(8,128)(2,1)S(1)}, bf16[1,224,256]{2,1,0:T(8,128)(2,1)S(1)}, u32[]{:S(2)}, u32[]{:S(2)}) %collective-permute-start) | collective-permute-done | bytes 114720 | tf_op jit(solution)/shard_map/ppermute | solution.py:37
  136.0 1.9 %collective-permute-start.1 = (bf16[2,224,256]{2,1,0:T(8,128)(2,1)S(1)}, bf16[2,224,256]{2,1,0:T(8,128)(2,1)S(1)}, u32[]{:S(2)}, u32[]{:S(2)}) collective-permute-start(bf16[2,224,256]{2,1,0:T(8,128)(2,1)S(1)} %pad_maximum_fusion.1), channel_id=1, source_target_pairs={{0,2},{1,3},{2,0},{3,1},{4,6},{5,7},{6,4},{7,5},{8,10},{9,11},{10,... | collective-permute-start | bytes 688136 | tf_op jit(solution)/shard_map/ppermute | solution.py:37
  138.0 2.5 %weight_parts.2 = f32[4,224,256]{2,1,0:T(8,128)S(1)} custom-call(s32[1]{0:T(128)} %bitcast.place_ref, bf16[224,1024]{1,0:T(8,128)(2,1)S(1)} %get-tuple-element.17.product_ref, bf16[4,4,384,256]{3,2,1,0:T(8,128)(2,1)S(1)} %bitcast.15, bf16[4,4,384,256]{3,2,1,0:T(8,128)(2,1)} %bitcast.5.plane_ref.other_ref), custom_call_target="tpu_custom_call" | custom-call | flops 469762048 | bytes 4194304 | tf_op jit(solution)/shard_map/weight_parts/pallas_call | solution.py:193
  140.5 0.0 collective-permute-done.6
  140.5 0.1 fusion
  140.6 4.8 %collective-permute-start.7 = (bf16[2,224,256]{2,1,0:T(8,128)(2,1)S(1)}, bf16[2,224,256]{2,1,0:T(8,128)(2,1)S(1)}, u32[]{:S(2)}, u32[]{:S(2)}) collective-permute-start(bf16[2,224,256]{2,1,0:T(8,128)(2,1)S(1)} %get-tuple-element.19), channel_id=1, source_target_pairs={{0,2},{1,3},{2,0},{3,1},{4,6},{5,7},{6,4},{7,5},{8,10},{9,11},{10,... | collective-permute-start | bytes 688136 | tf_op jit(solution)/shard_map/ppermute | solution.py:37
  145.5 5.2 %collective-permute-done.1 = bf16[2,224,256]{2,1,0:T(8,128)(2,1)S(1)} collective-permute-done((bf16[2,224,256]{2,1,0:T(8,128)(2,1)S(1)}, bf16[2,224,256]{2,1,0:T(8,128)(2,1)S(1)}, u32[]{:S(2)}, u32[]{:S(2)}) %collective-permute-start.1) | collective-permute-done | bytes 229408 | tf_op jit(solution)/shard_map/ppermute | solution.py:37
  150.7 4.3 %collective-permute-start.2 = (bf16[4,224,256]{2,1,0:T(8,128)(2,1)S(1)}, bf16[4,224,256]{2,1,0:T(8,128)(2,1)S(1)}, u32[]{:S(2)}, u32[]{:S(2)}) collective-permute-start(bf16[4,224,256]{2,1,0:T(8,128)(2,1)S(1)} %pad_maximum_fusion.near_ref), channel_id=1, source_target_pairs={{0,1},{1,0},{2,3},{3,2},{4,5},{5,4},{6,7},{7,6},{8,9},{9,8},{10,11... | collective-permute-start | bytes 1376264 | tf_op jit(solution)/shard_map/ppermute | solution.py:37
  155.0 0.5 collective-permute-done.7
  155.5 4.4 %collective-permute-start.8 = (bf16[224,256]{1,0:T(8,128)(2,1)S(1)}, bf16[224,256]{1,0:T(8,128)(2,1)S(1)}, u32[]{:S(2)}, u32[]{:S(2)}) collective-permute-start(bf16[224,256]{1,0:T(8,128)(2,1)S(1)} %fusion.4), channel_id=1, source_target_pairs={{0,4},{1,5},{2,6},{3,7},{4,0},{5,1},{6,2},{7,3},{8,12},{9,13},{10,... | collective-permute-start | bytes 344072 | tf_op jit(solution)/shard_map/ppermute | solution.py:37
  160.0 0.5 slice.35
  160.5 5.7 %collective-permute-done.2.far_ref = bf16[4,224,256]{2,1,0:T(8,128)(2,1)S(1)} collective-permute-done((bf16[4,224,256]{2,1,0:T(8,128)(2,1)S(1)}, bf16[4,224,256]{2,1,0:T(8,128)(2,1)S(1)}, u32[]{:S(2)}, u32[]{:S(2)}) %collective-permute-start.2) | collective-permute-done | bytes 458784 | tf_op jit(solution)/shard_map/ppermute | solution.py:37
  166.2 4.6 %hidden_gradient.1 = bf16[224,1024]{1,0:T(8,128)(2,1)} custom-call(s32[1]{0:T(128)} %bitcast.place_ref, s32[1]{0:T(128)} %bitcast.1.core_ref, bf16[4,224,256]{2,1,0:T(8,128)(2,1)S(1)} %pad_maximum_fusion.near_ref, bf16[4,224,256]{2,1,0:T(8,128)(2,1)S(1)} %collective-permute-done.2.far_ref, bf16[4,4,384,256]{3,2,1,0:T(8,128)(2,1)S(1)} %bitcast.16, ...), custom_call_target="tpu_custom_call" | custom-call | flops 939524096 | bytes 8388608 | tf_op jit(solution)/shard_map/hidden_gradient/pallas_call | solution.py:235
  170.8 5.2 %collective-permute-done.8 = bf16[224,256]{1,0:T(8,128)(2,1)S(1)} collective-permute-done((bf16[224,256]{1,0:T(8,128)(2,1)S(1)}, bf16[224,256]{1,0:T(8,128)(2,1)S(1)}, u32[]{:S(2)}, u32[]{:S(2)}) %collective-permute-start.8) | collective-permute-done | bytes 114720 | tf_op jit(solution)/shard_map/ppermute | solution.py:37
  176.0 0.7 fusion.3
  (8 shorter events, 0.1 us)
Async XLA Ops:
  0.6 0.8 copy-start.7
  1.5 0.8 copy-start.8
  2.4 17.9 %collective-permute-start.3 = (bf16[256,256]{1,0:T(8,128)(2,1)S(1)}, bf16[256,256]{1,0:T(8,128)(2,1)S(1)}, u32[]{:S(2)}, u32[]{:S(2)}) collective-permute-start(bf16[256,256]{1,0:T(8,128)(2,1)S(1)} %source.1), channel_id=1, source_target_pairs={{0,0},{1,64},{2,128},{3,192},{4,256},{5,320},{6,384},{7,448},{64,1... | collective-permute-start | bytes 393224 | tf_op jit(solution)/shard_map/ppermute | solution.py:37
  16.7 15.6 %collective-permute-start.4 = (bf16[256,256]{1,0:T(8,128)(2,1)S(1)}, bf16[256,256]{1,0:T(8,128)(2,1)S(1)}, u32[]{:S(2)}, u32[]{:S(2)}) collective-permute-start(bf16[256,256]{1,0:T(8,128)(2,1)S(1)} %source.1), channel_id=1, source_target_pairs={{0,64},{1,0},{2,192},{3,128},{4,320},{5,256},{6,448},{7,384},{64,6... | collective-permute-start | bytes 393224 | tf_op jit(solution)/shard_map/ppermute | solution.py:37
  75.2 22.9 %collective-permute-start.5 = (bf16[16,384,256]{2,1,0:T(8,128)(2,1)S(1)}, bf16[16,384,256]{2,1,0:T(8,128)(2,1)}, u32[]{:S(2)}, u32[]{:S(2)}) collective-permute-start(bf16[16,384,256]{2,1,0:T(8,128)(2,1)S(1)} %all_to_all.10), channel_id=1, source_target_pairs={{0,8},{8,0},{1,9},{9,1},{2,10},{10,2},{3,11},{11,3},{4,12},{12,4},... | collective-permute-start | bytes 9437192 | tf_op jit(solution)/shard_map/ppermute | solution.py:37
  78.6 0.7 copy-start.1
  79.3 27.9 %all-to-all-start.1 = ((f32[16,8,128]{2,1,0:T(8,128)}), f32[16,8,128]{2,1,0:T(8,128)S(1)}, u32[]{:S(2)}, u32[]{:S(2)}) async-start(f32[16,8,128]{2,1,0:T(8,128)} %get-tuple-element.15), calls=%async_computation.1 | async-start | bytes 131072 | tf_op jit(solution)/shard_map/all_to_all | solution.py:41
  101.4 0.7 copy-start.3
  102.1 0.7 copy-start.5
  107.2 1.0 copy-start
  108.2 0.9 copy-start.2
  109.2 0.9 copy-start.4
  110.1 0.9 copy-start.6
  111.6 6.3 %copy-start.9 = (bf16[224,256]{1,0:T(8,128)(2,1)S(1)}, bf16[224,256]{1,0:T(8,128)(2,1)}, u32[]{:S(2)}) copy-start(bf16[224,256]{1,0:T(8,128)(2,1)} %param.7) | copy-start | bytes 344068
  114.2 26.3 %collective-permute-start.6 = (bf16[4,224,256]{2,1,0:T(8,128)(2,1)S(1)}, bf16[4,224,256]{2,1,0:T(8,128)(2,1)S(1)}, u32[]{:S(2)}, u32[]{:S(2)}) collective-permute-start(bf16[4,224,256]{2,1,0:T(8,128)(2,1)S(1)} %weight_parts.3), channel_id=1, source_target_pairs={{0,1},{1,0},{2,3},{3,2},{4,5},{5,4},{6,7},{7,6},{8,9},{9,8},{10,11... | collective-permute-start | bytes 1376264 | tf_op jit(solution)/shard_map/ppermute | solution.py:37
  117.9 18.1 %collective-permute-start = (bf16[1,224,256]{2,1,0:T(8,128)(2,1)S(1)}, bf16[1,224,256]{2,1,0:T(8,128)(2,1)S(1)}, u32[]{:S(2)}, u32[]{:S(2)}) collective-permute-start(bf16[1,224,256]{2,1,0:T(8,128)(2,1)S(1)} %bitcast.17), channel_id=1, source_target_pairs={{0,4},{1,5},{2,6},{3,7},{4,0},{5,1},{6,2},{7,3},{8,12},{9,13},{10,... | collective-permute-start | bytes 344072 | tf_op jit(solution)/shard_map/ppermute | solution.py:37
  136.0 14.7 %collective-permute-start.1 = (bf16[2,224,256]{2,1,0:T(8,128)(2,1)S(1)}, bf16[2,224,256]{2,1,0:T(8,128)(2,1)S(1)}, u32[]{:S(2)}, u32[]{:S(2)}) collective-permute-start(bf16[2,224,256]{2,1,0:T(8,128)(2,1)S(1)} %pad_maximum_fusion.1), channel_id=1, source_target_pairs={{0,2},{1,3},{2,0},{3,1},{4,6},{5,7},{6,4},{7,5},{8,10},{9,11},{10,... | collective-permute-start | bytes 688136 | tf_op jit(solution)/shard_map/ppermute | solution.py:37
  140.6 14.9 %collective-permute-start.7 = (bf16[2,224,256]{2,1,0:T(8,128)(2,1)S(1)}, bf16[2,224,256]{2,1,0:T(8,128)(2,1)S(1)}, u32[]{:S(2)}, u32[]{:S(2)}) collective-permute-start(bf16[2,224,256]{2,1,0:T(8,128)(2,1)S(1)} %get-tuple-element.19), channel_id=1, source_target_pairs={{0,2},{1,3},{2,0},{3,1},{4,6},{5,7},{6,4},{7,5},{8,10},{9,11},{10,... | collective-permute-start | bytes 688136 | tf_op jit(solution)/shard_map/ppermute | solution.py:37
  150.7 15.5 %collective-permute-start.2 = (bf16[4,224,256]{2,1,0:T(8,128)(2,1)S(1)}, bf16[4,224,256]{2,1,0:T(8,128)(2,1)S(1)}, u32[]{:S(2)}, u32[]{:S(2)}) collective-permute-start(bf16[4,224,256]{2,1,0:T(8,128)(2,1)S(1)} %pad_maximum_fusion.near_ref), channel_id=1, source_target_pairs={{0,1},{1,0},{2,3},{3,2},{4,5},{5,4},{6,7},{7,6},{8,9},{9,8},{10,11... | collective-permute-start | bytes 1376264 | tf_op jit(solution)/shard_map/ppermute | solution.py:37
  155.5 20.5 %collective-permute-start.8 = (bf16[224,256]{1,0:T(8,128)(2,1)S(1)}, bf16[224,256]{1,0:T(8,128)(2,1)S(1)}, u32[]{:S(2)}, u32[]{:S(2)}) collective-permute-start(bf16[224,256]{1,0:T(8,128)(2,1)S(1)} %fusion.4), channel_id=1, source_target_pairs={{0,4},{1,5},{2,6},{3,7},{4,0},{5,1},{6,2},{7,3},{8,12},{9,13},{10,... | collective-permute-start | bytes 344072 | tf_op jit(solution)/shard_map/ppermute | solution.py:37

commit v5 on v4

--- a/solution.py
+++ b/solution.py
@@ -21,6 +21,10 @@
 SMEM = pl.BlockSpec(memory_space=pltpu.SMEM)
 
 
+def whole(*shape):
+    return pl.BlockSpec(shape, lambda i: (0,) * len(shape))
+
+
 def permutation(names, target):
     pairs = []
     for place in itertools.product(*[range(SIZES[n]) for n in names]):
@@ -82,53 +86,70 @@
     chunk_ref[2 * ROWS :, :] = jnp.concatenate(split(gram_y, 2), axis=1)
 
 
-def gram_kernel(plane_ref, x_ref, y_ref, tiles_ref):
+def minibatch_grams(plane_ref, first):
+    rows = [
+        jnp.concatenate(
+            [plane_ref[t // 2, first + i, pl.ds((t % 2) * ROWS, ROWS), :] for t in range(8)], axis=1
+        )
+        for i in range(2)
+    ]
+    pair = gram(jnp.concatenate(rows, axis=0))
+    grams = []
+    for i in range(2):
+        gram_y = jnp.zeros((ROWS, ROWS), F32)
+        for x in range(4):
+            parts = plane_ref[x, first + i, pl.ds(2 * ROWS, ROWS), :].astype(F32)
+            gram_y = gram_y + (parts[:, :ROWS] + parts[:, ROWS:])
+        block = slice(i * ROWS, (i + 1) * ROWS)
+        grams.append((pair[block, block], gram_y))
+    return grams
+
+
+def sums_kernel(plane_ref, tiles_ref):
     sums = jnp.zeros((3, ROWS), F32)
-    for y in range(0, 4, 2):
-        rows = [
-            jnp.concatenate(
-                [plane_ref[t // 2, y + i, pl.ds((t % 2) * ROWS, ROWS), :] for t in range(8)], axis=1
-            )
-            for i in range(2)
-        ]
-        pair = gram(jnp.concatenate(rows, axis=0))
-        for i in range(2):
-            gram_x = pair[i * ROWS : (i + 1) * ROWS, i * ROWS : (i + 1) * ROWS]
-            gram_y = jnp.zeros((ROWS, ROWS), F32)
-            for x in range(4):
-                parts = plane_ref[x, y + i, pl.ds(2 * ROWS, ROWS), :].astype(F32)
-                gram_y = gram_y + (parts[:, :ROWS] + parts[:, ROWS:])
-            x_ref[y + i] = gram_x
-            y_ref[y + i] = gram_y
-            products = (gram_x * gram_x, gram_y * gram_y, gram_x * gram_y)
-            sums = sums + jnp.concatenate(
-                [jnp.sum(v, axis=0, keepdims=True) for v in products], axis=0
-            )
+    for gram_x, gram_y in minibatch_grams(plane_ref, 0) + minibatch_grams(plane_ref, 2):
+        products = (gram_x * gram_x, gram_y * gram_y, gram_x * gram_y)
+        sums = sums + jnp.concatenate([jnp.sum(v, axis=0, keepdims=True) for v in products], axis=0)
     tile = jnp.concatenate([sums, jnp.zeros((5, ROWS), F32)], axis=0)
     tiles_ref[...] = jnp.broadcast_to(tile[None], tiles_ref.shape)
 
 
-def plane_grams(plane):
-    return pl.pallas_call(
-        gram_kernel,
+def plane_sums(plane):
+    return pl.pallas_call(
+        sums_kernel,
         in_specs=[VMEM],
-        out_specs=[VMEM] * 3,
-        out_shape=[
-            jax.ShapeDtypeStruct((4, ROWS, ROWS), F32),
-            jax.ShapeDtypeStruct((4, ROWS, ROWS), F32),
-            jax.ShapeDtypeStruct((16, 8, ROWS), F32),
-        ],
+        out_specs=VMEM,
+        out_shape=jax.ShapeDtypeStruct((16, 8, ROWS), F32),
+        compiler_params=PARAMS,
+        name="plane_sums",
+    )(plane)
+
+
+def grams_kernel(own_ref, other_ref, grams_ref):
+    for base, ref in ((0, own_ref), (4, other_ref)):
+        for y in (0, 2):
+            for i, (gram_x, gram_y) in enumerate(minibatch_grams(ref, y)):
+                grams_ref[0, base + y + i] = gram_x
+                grams_ref[1, base + y + i] = gram_y
+
+
+def plane_grams(plane, other):
+    return pl.pallas_call(
+        grams_kernel,
+        in_specs=[VMEM] * 2,
+        out_specs=VMEM,
+        out_shape=jax.ShapeDtypeStruct((2, 8, ROWS, ROWS), F32),
         compiler_params=PARAMS,
         cost_estimate=pl.CostEstimate(
-            flops=2 << 30, bytes_accessed=4 << 20, transcendentals=0
+            flops=4 << 30, bytes_accessed=8 << 20, transcendentals=0
         ),
         name="plane_grams",
-    )(plane)
+    )(plane, other)
 
 
 def mix_kernel(
-    scale, core_ref, own_x_ref, own_y_ref, other_x_ref, other_y_ref, tiles_ref, hidden_ref,
-    mixed_ref, product_ref, cka_ref,
+    scale, core_ref, place_ref, grams_ref, tiles_ref, hidden_ref, own_ref, other_ref,
+    mixed_ref, product_ref, cka_ref, upper_ref, lower_ref,
 ):
     sums = jnp.sum(jnp.sum(tiles_ref[...], axis=0), axis=1, keepdims=True)
     sxx, syy, sxy = sums[0:1], sums[1:2], sums[2:3]
@@ -138,8 +159,7 @@
     cka_ref[...] = jnp.broadcast_to(sxy / root, cka_ref.shape)
     core = core_ref[0]
     for b in range(8):
-        x_ref, y_ref = (own_x_ref, own_y_ref) if b < 4 else (other_x_ref, other_y_ref)
-        mixed = coef * (y_ref[b % 4] - ratio * x_ref[b % 4])
+        mixed = coef * (grams_ref[1, b] - ratio * grams_ref[0, b])
         mixed_ref[b] = mixed
         place = b % 4 * 2 + (core if b < 4 else 1 - core)
         hidden = hidden_ref[:, pl.ds(pl.multiple_of(place * ROWS, ROWS), ROWS)]
@@ -149,21 +169,32 @@
             preferred_element_type=F32,
         )
         product_ref[:, b * ROWS : (b + 1) * ROWS] = product.astype(BF16)
-
-
-def mix(core, own, other, tiles, hidden, scale):
+    middle = upper_ref.shape[1]
+    for k in range(4):
+        value = weight_block(place_ref, product_ref, own_ref, other_ref, 4 + k).astype(BF16)
+        upper_ref[k] = value[:middle]
+        lower_ref[k] = value[middle:]
+
+
+def mix(core, place, grams, tiles, hidden, plane, other, scale):
+    units = hidden.shape[0]
+    half = jax.ShapeDtypeStruct((4, units // 2, WIDTH), BF16)
     return pl.pallas_call(
         functools.partial(mix_kernel, scale),
-        in_specs=[SMEM] + [VMEM] * 6,
-        out_specs=[VMEM] * 3,
+        grid=(1,),
+        in_specs=[SMEM] * 2
+        + [whole(2, 8, ROWS, ROWS), VMEM, whole(*hidden.shape), VMEM, VMEM],
+        out_specs=[VMEM] * 5,
         out_shape=[
             jax.ShapeDtypeStruct((8, ROWS, ROWS), F32),
             jax.ShapeDtypeStruct(hidden.shape, BF16),
             jax.ShapeDtypeStruct((8, ROWS), F32),
+            half,
+            half,
         ],
         compiler_params=PARAMS,
         name="mix",
-    )(core, own[0], own[1], other[0], other[1], tiles, hidden)
+    )(core, place, grams, tiles, hidden, plane, other)
 
 
 def column_block(place, k):
@@ -175,26 +206,27 @@
     return ref[lax.div(t, 2), :, pl.ds(start, ROWS), :].reshape(4 * ROWS, WIDTH)
 
 
-def weight_kernel(first, place_ref, product_ref, own_ref, other_ref, out_ref):
+def weight_block(place_ref, product_ref, own_ref, other_ref, k):
     half = 4 * ROWS
+    t = column_block(place_ref[0], k)
+    value = jnp.dot(product_ref[:, :half], token_rows(own_ref, t), preferred_element_type=F32)
+    return value + jnp.dot(
+        product_ref[:, half:], token_rows(other_ref, t), preferred_element_type=F32
+    )
+
+
+def weight_kernel(place_ref, product_ref, own_ref, other_ref, out_ref):
     for k in range(4):
-        t = column_block(place_ref[0], first + k)
-        value = jnp.dot(
-            product_ref[:, :half], token_rows(own_ref, t), preferred_element_type=F32
-        )
-        value = value + jnp.dot(
-            product_ref[:, half:], token_rows(other_ref, t), preferred_element_type=F32
-        )
-        out_ref[k] = value.astype(out_ref.dtype)
-
-
-def weight_parts(place, product, plane, other, first, dtype):
+        out_ref[k] = weight_block(place_ref, product_ref, own_ref, other_ref, k)
+
+
+def weight_parts(place, product, plane, other):
     units = product.shape[0]
     return pl.pallas_call(
-        functools.partial(weight_kernel, first),
+        weight_kernel,
         in_specs=[SMEM] + [VMEM] * 3,
         out_specs=VMEM,
-        out_shape=jax.ShapeDtypeStruct((4, units, WIDTH), dtype),
+        out_shape=jax.ShapeDtypeStruct((4, units, WIDTH), F32),
         compiler_params=PARAMS,
         cost_estimate=pl.CostEstimate(
             flops=2 * units * 8 * ROWS * 4 * WIDTH, bytes_accessed=4 << 20, transcendentals=0
@@ -245,6 +277,63 @@
     )(place, core, near, far, plane, other, mixed)
 
 
+def add_one_kernel(row, kept_ref, arrived_ref, out_ref, moved_ref):
+    value = kept_ref[:, row : row + arrived_ref.shape[1]] + arrived_ref[...].astype(F32)
+    out_ref[...] = value[:2]
+    moved_ref[...] = value[2:].astype(BF16)
+
+
+def add_one(kept, arrived, half):
+    rows = arrived.shape[1]
+    return pl.pallas_call(
+        functools.partial(add_one_kernel, half * rows),
+        in_specs=[VMEM] * 2,
+        out_specs=[VMEM] * 2,
+        out_shape=[
+            jax.ShapeDtypeStruct((2, rows, WIDTH), F32),
+            jax.ShapeDtypeStruct((2, rows, WIDTH), BF16),
+        ],
+        compiler_params=PARAMS,
+    )(kept, arrived)
+
+
+def add_two_kernel(kept_ref, arrived_ref, out_ref, moved_ref):
+    value = kept_ref[...] + arrived_ref[...].astype(F32)
+    out_ref[...] = value[0]
+    moved_ref[...] = value[1].astype(BF16)
+
+
+def add_two(kept, arrived):
+    rows = arrived.shape[1]
+    return pl.pallas_call(
+        add_two_kernel,
+        in_specs=[VMEM] * 2,
+        out_specs=[VMEM] * 2,
+        out_shape=[
+            jax.ShapeDtypeStruct((rows, WIDTH), F32),
+            jax.ShapeDtypeStruct((rows, WIDTH), BF16),
+        ],
+        compiler_params=PARAMS,
+    )(kept, arrived)
+
+
+def add_last_kernel(first_ref, one_ref, second_ref, two_ref, out_ref):
+    rows = first_ref.shape[0]
+    out_ref[:rows] = first_ref[...] + one_ref[...].astype(F32)
+    out_ref[rows:] = second_ref[...] + two_ref[...].astype(F32)
+
+
+def add_last(*values):
+    return pl.pallas_call(
+        add_last_kernel,
+        in_specs=[VMEM] * 4,
+        out_specs=VMEM,
+        out_shape=jax.ShapeDtypeStruct((2 * values[0].shape[0], WIDTH), F32),
+        compiler_params=PARAMS,
+        name="add_last",
+    )(*values)
+
+
 def flip(bit):
     return lambda d: {"t": d["t"] ^ bit}
 
@@ -263,7 +352,8 @@
     far = permute(near, ("t",), flip(1))
     piece = pl.pallas_call(
         source_kernel,
-        in_specs=[VMEM] * 2,
+        grid=(1,),
+        in_specs=[whole(ROWS, WIDTH)] * 2,
         out_specs=VMEM,
         out_shape=shape((2 * ROWS, WIDTH), BF16),
         compiler_params=PARAMS,
@@ -283,16 +373,21 @@
     other = permute(plane, ("c",), lambda d: {"c": 1 - d["c"]})
     plane = plane.reshape(4, 4, CHUNK, WIDTH)
     other = other.reshape(4, 4, CHUNK, WIDTH)
-    own_grams = plane_grams(plane)
-    tiles = exchange(own_grams[2], ("c", "t"))
-    mixed, product, cka = mix(core, own_grams, plane_grams(other), tiles, hidden, scale)
-    sent = weight_parts(place, product, plane, other, 4, BF16)
-    sent = permute(sent, ("t",), flip(1))
-    kept = weight_parts(place, product, plane, other, 0, F32)
-    later = permute((kept[2:] + sent[2:].astype(F32)).astype(BF16), ("t",), flip(2))
-    kept = kept[:2] + sent[:2].astype(F32)
-    last = permute((kept[1] + later[1].astype(F32)).astype(BF16), ("t",), flip(4))
-    grad_weight = kept[0] + later[0].astype(F32) + last.astype(F32)
+    tiles = exchange(plane_sums(plane), ("c", "t"))
+    grams = plane_grams(plane, other)
+    mixed, product, cka, *sent = mix(core, place, grams, tiles, hidden, plane, other, scale)
+    arrived, later, last = {}, {}, {}
+    for name, values in zip("ab", sent):
+        arrived[name] = permute(values, ("t",), flip(1))
+    kept = weight_parts(place, product, plane, other)
+    halves = {}
+    for i, name in enumerate("ab"):
+        halves[name], moved = add_one(kept, arrived[name], i)
+        later[name] = permute(moved, ("t",), flip(2))
+    for name in "ab":
+        halves[name], moved = add_two(halves[name], later[name])
+        last[name] = permute(moved, ("t",), flip(4))
+    grad_weight = add_last(halves["a"], last["a"], halves["b"], last["b"])
     grad_hidden = hidden_gradient(place, core, near, far, plane, other, mixed)
     return (grad_hidden, grad_weight, cka[0, 0])
 

time: 178 us -> 181 us (1.017)
  the two profiles are of different devices: /device:TPU:32 before, /device:TPU:1 now
where the time goes in v5:
time: 181 us
  starting transfers between devices  61.7 us (34%)
  waiting for transfers between devices  50.7 us (28%)
  blocking collectives  42.9 us (24%)
  Pallas kernels  16.2 us (9%)
  local copies, waits for them, and re-layouts  5.7 us (3%)
  other arithmetic  2.47 us (1%)
    ppermute x12, starting transfers between devices, permute(): return lax.ppermute(values, names, permutation(names, target))  50.5 us
    ppermute x12, waiting for transfers between devices, permute(): return lax.ppermute(values, names, permutation(names, target))  44.4 us
    all_to_all x1, blocking collectives, exchange(): return lax.all_to_all(values, names, split_axis=0, concat_axis=0)  42.9 us
    all_to_all x1, starting transfers between devices, exchange(): return lax.all_to_all(values, names, split_axis=0, concat_axis=0)  11.3 us
    all_to_all x1, waiting for transfers between devices, exchange(): return lax.all_to_all(values, names, split_axis=0, concat_axis=0)  6.25 us
    pallas_call x1, Pallas kernels, hidden_gradient(): pl.pallas_call(hidden_kernel, in_specs=[SMEM] * 2 + [VMEM] * 5, out_specs...  4.9 us
    unnamed x12, local copies, waits for them, and re-layouts  4.89 us
  transfers between devices with their start and end apart: 13, of which 9 were waited for; matrix products, arithmetic and copies ran while one was open for 2% of the time, Pallas kernels for 8%

profile of v5, /device:TPU:1, one launch (start us, length us, event | category | flops | bytes accessed | tf_op | source)
XLA Modules:
  0.0 180.6 jit_solution(12160854476252088630)
XLA Ops:
  0.6 0.0 copy-start.3
  0.6 0.8 copy-done.3
  1.5 0.0 copy-start.4
  1.5 0.8 copy-done.4
  2.4 0.7 collective-permute-start.3
  3.0 17.5 %collective-permute-start.4 = (bf16[256,256]{1,0:T(8,128)(2,1)S(1)}, bf16[256,256]{1,0:T(8,128)(2,1)S(1)}, u32[]{:S(2)}, u32[]{:S(2)}) collective-permute-start(bf16[256,256]{1,0:T(8,128)(2,1)S(1)} %source.1), channel_id=1, source_target_pairs={{0,64},{1,0},{2,192},{3,128},{4,320},{5,256},{6,448},{7,384},{64,6... | collective-permute-start | bytes 393224 | tf_op jit(solution)/shard_map/ppermute | solution.py:41
  20.6 0.0 collective-permute-done.3.first_ref
  20.6 14.0 %collective-permute-done.4.second_ref = bf16[256,256]{1,0:T(8,128)(2,1)S(1)} collective-permute-done((bf16[256,256]{1,0:T(8,128)(2,1)S(1)}, bf16[256,256]{1,0:T(8,128)(2,1)S(1)}, u32[]{:S(2)}, u32[]{:S(2)}) %collective-permute-start.4) | collective-permute-done | bytes 131104 | tf_op jit(solution)/shard_map/ppermute | solution.py:41
  34.5 0.2 chunk.1
  34.7 0.3 broadcast_in_dim.10
  35.0 0.0 copy-start.5
  35.1 42.9 %all_to_all.10 = bf16[16,384,256]{2,1,0:T(8,128)(2,1)S(1)} all-to-all(bf16[16,384,256]{2,1,0:T(8,128)(2,1)S(1)} %broadcast_in_dim.10), channel_id=1, replica_groups=mesh['x'=4,'zh'=2,'y'=4,'c'=2,'t'=8] {'x','y'}, dimensions={0} | all-to-all | bytes 6291456 | tf_op jit(solution)/shard_map/all_to_all | solution.py:45
  78.0 4.1 %collective-permute-start.5 = (bf16[16,384,256]{2,1,0:T(8,128)(2,1)S(1)}, bf16[16,384,256]{2,1,0:T(8,128)(2,1)}, u32[]{:S(2)}, u32[]{:S(2)}) collective-permute-start(bf16[16,384,256]{2,1,0:T(8,128)(2,1)S(1)} %all_to_all.10), channel_id=1, source_target_pairs={{0,8},{8,0},{1,9},{9,1},{2,10},{10,2},{3,11},{11,3},{4,12},{12,4},... | collective-permute-start | bytes 9437192 | tf_op jit(solution)/shard_map/ppermute | solution.py:41
  82.1 0.0 copy-done.5
  82.1 7.4 %collective-permute-start = (bf16[1,224,256]{2,1,0:T(8,128)(2,1)S(1)}, bf16[1,224,256]{2,1,0:T(8,128)(2,1)S(1)}, u32[]{:S(2)}, u32[]{:S(2)}) collective-permute-start(bf16[1,224,256]{2,1,0:T(8,128)(2,1)S(1)} %bitcast.12), channel_id=1, source_target_pairs={{0,4},{1,5},{2,6},{3,7},{4,0},{5,1},{6,2},{7,3},{8,12},{9,13},{10,... | collective-permute-start | bytes 344072 | tf_op jit(solution)/shard_map/ppermute | solution.py:41
  89.5 8.2 %collective-permute-done = bf16[1,224,256]{2,1,0:T(8,128)(2,1)S(1)} collective-permute-done((bf16[1,224,256]{2,1,0:T(8,128)(2,1)S(1)}, bf16[1,224,256]{2,1,0:T(8,128)(2,1)S(1)}, u32[]{:S(2)}, u32[]{:S(2)}) %collective-permute-start) | collective-permute-done | bytes 114720 | tf_op jit(solution)/shard_map/ppermute | solution.py:41
  97.8 0.7 pad_maximum_fusion.1
  98.5 3.3 %collective-permute-start.1 = (bf16[2,224,256]{2,1,0:T(8,128)(2,1)}, bf16[2,224,256]{2,1,0:T(8,128)(2,1)}, u32[]{:S(2)}, u32[]{:S(2)}) collective-permute-start(bf16[2,224,256]{2,1,0:T(8,128)(2,1)} %pad_maximum_fusion.1), channel_id=1, source_target_pairs={{0,2},{1,3},{2,0},{3,1},{4,6},{5,7},{6,4},{7,5},{8,10},{9,11},{10,... | collective-permute-start | bytes 688136 | tf_op jit(solution)/shard_map/ppermute | solution.py:41
  101.8 11.0 %collective-permute-done.1 = bf16[2,224,256]{2,1,0:T(8,128)(2,1)} collective-permute-done((bf16[2,224,256]{2,1,0:T(8,128)(2,1)}, bf16[2,224,256]{2,1,0:T(8,128)(2,1)}, u32[]{:S(2)}, u32[]{:S(2)}) %collective-permute-start.1) | collective-permute-done | bytes 229408 | tf_op jit(solution)/shard_map/ppermute | solution.py:41
  112.9 1.8 pad_maximum_fusion.near_ref
  114.6 2.6 %collective-permute-start.2 = (bf16[4,224,256]{2,1,0:T(8,128)(2,1)}, bf16[4,224,256]{2,1,0:T(8,128)(2,1)}, u32[]{:S(2)}, u32[]{:S(2)}) collective-permute-start(bf16[4,224,256]{2,1,0:T(8,128)(2,1)} %pad_maximum_fusion.near_ref), channel_id=1, source_target_pairs={{0,1},{1,0},{2,3},{3,2},{4,5},{5,4},{6,7},{7,6},{8,9},{9,8},{10,11... | collective-permute-start | bytes 1376264 | tf_op jit(solution)/shard_map/ppermute | solution.py:41
  117.2 1.4 plane_sums.1
  118.6 11.3 %all-to-all-start.1 = ((f32[16,8,128]{2,1,0:T(8,128)}), f32[16,8,128]{2,1,0:T(8,128)S(1)}, u32[]{:S(2)}, u32[]{:S(2)}) async-start(f32[16,8,128]{2,1,0:T(8,128)} %plane_sums.1), calls=%async_computation.1 | async-start | bytes 131072 | tf_op jit(solution)/shard_map/all_to_all | solution.py:45
  129.9 0.0 collective-permute-done.5
  129.9 3.2 %plane_grams.1.grams_ref = f32[2,8,128,128]{3,2,1,0:T(8,128)S(1)} custom-call(bf16[4,4,384,256]{3,2,1,0:T(8,128)(2,1)S(1)} %bitcast.8, bf16[4,4,384,256]{3,2,1,0:T(8,128)(2,1)} %bitcast.5.other_ref), custom_call_target="tpu_custom_call" | custom-call | flops 4294967296 | bytes 8388608 | tf_op jit(solution)/shard_map/plane_grams/pallas_call | solution.py:137
  133.2 0.0 copy-start
  133.2 1.0 copy-done
  134.1 6.2 %all-to-all-done.1.tiles_ref = f32[16,8,128]{2,1,0:T(8,128)S(1)} async-done(((f32[16,8,128]{2,1,0:T(8,128)}), f32[16,8,128]{2,1,0:T(8,128)S(1)}, u32[]{:S(2)}, u32[]{:S(2)}) %all-to-all-start.1) | async-done | bytes 65568 | tf_op jit(solution)/shard_map/all_to_all | solution.py:45
  140.4 1.2 copy-done.1
  141.6 1.0 copy-done.2
  142.6 3.0 %mix.1 = (f32[8,128,128]{2,1,0:T(8,128)S(1)}, bf16[224,1024]{1,0:T(8,128)(2,1)S(1)}, f32[8,128]{1,0:T(8,128)S(1)}, bf16[4,112,256]{2,1,0:T(8,128)(2,1)S(1)}, bf16[4,112,256]{2,1,0:T(8,128)(2,1)S(1)}) custom-call(s32[1]{0:T(128)} %bitcast.1.core_ref, s32[1]{0:T(128)} %bitcast.place_ref, f32[2,8,128,128]{3,2,1,0:T(8,128)S(1)} %copy-done.1, ...), custom_call_target="tpu_custom_call" | custom-call | tf_op jit(solution)/shard_map/mix/pallas_call | solution.py:182
  145.6 2.1 %collective-permute-start.9 = (bf16[4,112,256]{2,1,0:T(8,128)(2,1)S(1)}, bf16[4,112,256]{2,1,0:T(8,128)(2,1)S(1)}, u32[]{:S(2)}, u32[]{:S(2)}) collective-permute-start(bf16[4,112,256]{2,1,0:T(8,128)(2,1)S(1)} %get-tuple-element.23), channel_id=1, source_target_pairs={{0,1},{1,0},{2,3},{3,2},{4,5},{5,4},{6,7},{7,6},{8,9},{9,8},{10,11... | collective-permute-start | bytes 688136 | tf_op jit(solution)/shard_map/ppermute | solution.py:41
  147.7 3.2 %collective-permute-start.6 = (bf16[4,112,256]{2,1,0:T(8,128)(2,1)S(1)}, bf16[4,112,256]{2,1,0:T(8,128)(2,1)S(1)}, u32[]{:S(2)}, u32[]{:S(2)}) collective-permute-start(bf16[4,112,256]{2,1,0:T(8,128)(2,1)S(1)} %get-tuple-element.18), channel_id=1, source_target_pairs={{0,1},{1,0},{2,3},{3,2},{4,5},{5,4},{6,7},{7,6},{8,9},{9,8},{10,11... | collective-permute-start | bytes 688136 | tf_op jit(solution)/shard_map/ppermute | solution.py:41
  150.9 2.6 %weight_parts.1.kept_ref = f32[4,224,256]{2,1,0:T(8,128)S(1)} custom-call(s32[1]{0:T(128)} %bitcast.place_ref, bf16[224,1024]{1,0:T(8,128)(2,1)S(1)} %get-tuple-element.17.product_ref, bf16[4,4,384,256]{3,2,1,0:T(8,128)(2,1)S(1)} %bitcast.10, bf16[4,4,384,256]{3,2,1,0:T(8,128)(2,1)} %bitcast.5.other_ref), custom_call_target="tpu_custom_call" | custom-call | flops 469762048 | bytes 4194304 | tf_op jit(solution)/shard_map/weight_parts/pallas_call | solution.py:225
  153.5 0.8 collective-permute-done.9.arrived_ref
  154.3 1.9 %collective-permute-start.10 = (bf16[2,112,256]{2,1,0:T(8,128)(2,1)S(1)}, bf16[2,112,256]{2,1,0:T(8,128)(2,1)S(1)}, u32[]{:S(2)}, u32[]{:S(2)}) collective-permute-start(bf16[2,112,256]{2,1,0:T(8,128)(2,1)S(1)} %get-tuple-element.25), channel_id=1, source_target_pairs={{0,2},{1,3},{2,0},{3,1},{4,6},{5,7},{6,4},{7,5},{8,10},{9,11},{10,... | collective-permute-start | bytes 344072 | tf_op jit(solution)/shard_map/ppermute | solution.py:41
  156.3 2.9 %collective-permute-done.6.arrived_ref = bf16[4,112,256]{2,1,0:T(8,128)(2,1)S(1)} collective-permute-done((bf16[4,112,256]{2,1,0:T(8,128)(2,1)S(1)}, bf16[4,112,256]{2,1,0:T(8,128)(2,1)S(1)}, u32[]{:S(2)}, u32[]{:S(2)}) %collective-permute-start.6) | collective-permute-done | bytes 229408 | tf_op jit(solution)/shard_map/ppermute | solution.py:41
  159.3 1.9 %collective-permute-start.7 = (bf16[2,112,256]{2,1,0:T(8,128)(2,1)S(1)}, bf16[2,112,256]{2,1,0:T(8,128)(2,1)S(1)}, u32[]{:S(2)}, u32[]{:S(2)}) collective-permute-start(bf16[2,112,256]{2,1,0:T(8,128)(2,1)S(1)} %get-tuple-element.20), channel_id=1, source_target_pairs={{0,2},{1,3},{2,0},{3,1},{4,6},{5,7},{6,4},{7,5},{8,10},{9,11},{10,... | collective-permute-start | bytes 344072 | tf_op jit(solution)/shard_map/ppermute | solution.py:41
  161.2 0.5 slice.3
  161.7 1.9 %collective-permute-done.10.arrived_ref = bf16[2,112,256]{2,1,0:T(8,128)(2,1)S(1)} collective-permute-done((bf16[2,112,256]{2,1,0:T(8,128)(2,1)S(1)}, bf16[2,112,256]{2,1,0:T(8,128)(2,1)S(1)}, u32[]{:S(2)}, u32[]{:S(2)}) %collective-permute-start.10) | collective-permute-done | bytes 114720 | tf_op jit(solution)/shard_map/ppermute | solution.py:41
  163.6 1.9 %collective-permute-start.11 = (bf16[112,256]{1,0:T(8,128)(2,1)S(1)}, bf16[112,256]{1,0:T(8,128)(2,1)S(1)}, u32[]{:S(2)}, u32[]{:S(2)}) collective-permute-start(bf16[112,256]{1,0:T(8,128)(2,1)S(1)} %get-tuple-element.27), channel_id=1, source_target_pairs={{0,4},{1,5},{2,6},{3,7},{4,0},{5,1},{6,2},{7,3},{8,12},{9,13},{10,... | collective-permute-start | bytes 172040 | tf_op jit(solution)/shard_map/ppermute | solution.py:41
  165.6 3.5 %collective-permute-done.7.arrived_ref = bf16[2,112,256]{2,1,0:T(8,128)(2,1)S(1)} collective-permute-done((bf16[2,112,256]{2,1,0:T(8,128)(2,1)S(1)}, bf16[2,112,256]{2,1,0:T(8,128)(2,1)S(1)}, u32[]{:S(2)}, u32[]{:S(2)}) %collective-permute-start.7) | collective-permute-done | bytes 114720 | tf_op jit(solution)/shard_map/ppermute | solution.py:41
  169.1 3.8 %collective-permute-start.8 = (bf16[112,256]{1,0:T(8,128)(2,1)S(1)}, bf16[112,256]{1,0:T(8,128)(2,1)S(1)}, u32[]{:S(2)}, u32[]{:S(2)}) collective-permute-start(bf16[112,256]{1,0:T(8,128)(2,1)S(1)} %get-tuple-element.22), channel_id=1, source_target_pairs={{0,4},{1,5},{2,6},{3,7},{4,0},{5,1},{6,2},{7,3},{8,12},{9,13},{10,... | collective-permute-start | bytes 172040 | tf_op jit(solution)/shard_map/ppermute | solution.py:41
  172.9 0.0 collective-permute-done.2.far_ref
  172.9 4.9 %hidden_gradient.1 = bf16[224,1024]{1,0:T(8,128)(2,1)} custom-call(s32[1]{0:T(128)} %bitcast.place_ref, s32[1]{0:T(128)} %bitcast.1.core_ref, bf16[4,224,256]{2,1,0:T(8,128)(2,1)} %pad_maximum_fusion.near_ref, bf16[4,224,256]{2,1,0:T(8,128)(2,1)} %collective-permute-done.2.far_ref, bf16[4,4,384,256]{3,2,1,0:T(8,128)(2,1)S(1)} %bitcast.11, ...), custom_call_target="tpu_custom_call" | custom-call | flops 939524096 | bytes 8388608 | tf_op jit(solution)/shard_map/hidden_gradient/pallas_call | solution.py:267
  177.8 0.0 collective-permute-done.11.two_ref
  177.8 2.0 %collective-permute-done.8.one_ref = bf16[112,256]{1,0:T(8,128)(2,1)S(1)} collective-permute-done((bf16[112,256]{1,0:T(8,128)(2,1)S(1)}, bf16[112,256]{1,0:T(8,128)(2,1)S(1)}, u32[]{:S(2)}, u32[]{:S(2)}) %collective-permute-start.8) | collective-permute-done | bytes 57376 | tf_op jit(solution)/shard_map/ppermute | solution.py:41
  179.9 0.7 add_last.1
  (7 shorter events, 0.2 us)
Async XLA Ops:
  0.6 0.8 copy-start.3
  1.5 0.8 copy-start.4
  2.4 18.2 %collective-permute-start.3 = (bf16[256,256]{1,0:T(8,128)(2,1)S(1)}, bf16[256,256]{1,0:T(8,128)(2,1)S(1)}, u32[]{:S(2)}, u32[]{:S(2)}) collective-permute-start(bf16[256,256]{1,0:T(8,128)(2,1)S(1)} %source.1), channel_id=1, source_target_pairs={{0,0},{1,64},{2,128},{3,192},{4,256},{5,320},{6,384},{7,448},{64,1... | collective-permute-start | bytes 393224 | tf_op jit(solution)/shard_map/ppermute | solution.py:41
  3.0 31.5 %collective-permute-start.4 = (bf16[256,256]{1,0:T(8,128)(2,1)S(1)}, bf16[256,256]{1,0:T(8,128)(2,1)S(1)}, u32[]{:S(2)}, u32[]{:S(2)}) collective-permute-start(bf16[256,256]{1,0:T(8,128)(2,1)S(1)} %source.1), channel_id=1, source_target_pairs={{0,64},{1,0},{2,192},{3,128},{4,320},{5,256},{6,448},{7,384},{64,6... | collective-permute-start | bytes 393224 | tf_op jit(solution)/shard_map/ppermute | solution.py:41
  35.0 47.1 %copy-start.5 = (bf16[224,256]{1,0:T(8,128)(2,1)S(1)}, bf16[224,256]{1,0:T(8,128)(2,1)}, u32[]{:S(2)}) copy-start(bf16[224,256]{1,0:T(8,128)(2,1)} %param.7) | copy-start | bytes 344068
  78.0 51.9 %collective-permute-start.5 = (bf16[16,384,256]{2,1,0:T(8,128)(2,1)S(1)}, bf16[16,384,256]{2,1,0:T(8,128)(2,1)}, u32[]{:S(2)}, u32[]{:S(2)}) collective-permute-start(bf16[16,384,256]{2,1,0:T(8,128)(2,1)S(1)} %all_to_all.10), channel_id=1, source_target_pairs={{0,8},{8,0},{1,9},{9,1},{2,10},{10,2},{3,11},{11,3},{4,12},{12,4},... | collective-permute-start | bytes 9437192 | tf_op jit(solution)/shard_map/ppermute | solution.py:41
  82.1 15.6 %collective-permute-start = (bf16[1,224,256]{2,1,0:T(8,128)(2,1)S(1)}, bf16[1,224,256]{2,1,0:T(8,128)(2,1)S(1)}, u32[]{:S(2)}, u32[]{:S(2)}) collective-permute-start(bf16[1,224,256]{2,1,0:T(8,128)(2,1)S(1)} %bitcast.12), channel_id=1, source_target_pairs={{0,4},{1,5},{2,6},{3,7},{4,0},{5,1},{6,2},{7,3},{8,12},{9,13},{10,... | collective-permute-start | bytes 344072 | tf_op jit(solution)/shard_map/ppermute | solution.py:41
  98.5 14.4 %collective-permute-start.1 = (bf16[2,224,256]{2,1,0:T(8,128)(2,1)}, bf16[2,224,256]{2,1,0:T(8,128)(2,1)}, u32[]{:S(2)}, u32[]{:S(2)}) collective-permute-start(bf16[2,224,256]{2,1,0:T(8,128)(2,1)} %pad_maximum_fusion.1), channel_id=1, source_target_pairs={{0,2},{1,3},{2,0},{3,1},{4,6},{5,7},{6,4},{7,5},{8,10},{9,11},{10,... | collective-permute-start | bytes 688136 | tf_op jit(solution)/shard_map/ppermute | solution.py:41
  114.6 58.3 %collective-permute-start.2 = (bf16[4,224,256]{2,1,0:T(8,128)(2,1)}, bf16[4,224,256]{2,1,0:T(8,128)(2,1)}, u32[]{:S(2)}, u32[]{:S(2)}) collective-permute-start(bf16[4,224,256]{2,1,0:T(8,128)(2,1)} %pad_maximum_fusion.near_ref), channel_id=1, source_target_pairs={{0,1},{1,0},{2,3},{3,2},{4,5},{5,4},{6,7},{7,6},{8,9},{9,8},{10,11... | collective-permute-start | bytes 1376264 | tf_op jit(solution)/shard_map/ppermute | solution.py:41
  118.6 21.7 %all-to-all-start.1 = ((f32[16,8,128]{2,1,0:T(8,128)}), f32[16,8,128]{2,1,0:T(8,128)S(1)}, u32[]{:S(2)}, u32[]{:S(2)}) async-start(f32[16,8,128]{2,1,0:T(8,128)} %plane_sums.1), calls=%async_computation.1 | async-start | bytes 131072 | tf_op jit(solution)/shard_map/all_to_all | solution.py:45
  133.2 1.0 copy-start
  140.4 1.2 copy-start.1
  141.6 1.0 copy-start.2
  145.6 8.7 %collective-permute-start.9 = (bf16[4,112,256]{2,1,0:T(8,128)(2,1)S(1)}, bf16[4,112,256]{2,1,0:T(8,128)(2,1)S(1)}, u32[]{:S(2)}, u32[]{:S(2)}) collective-permute-start(bf16[4,112,256]{2,1,0:T(8,128)(2,1)S(1)} %get-tuple-element.23), channel_id=1, source_target_pairs={{0,1},{1,0},{2,3},{3,2},{4,5},{5,4},{6,7},{7,6},{8,9},{9,8},{10,11... | collective-permute-start | bytes 688136 | tf_op jit(solution)/shard_map/ppermute | solution.py:41
  147.7 11.5 %collective-permute-start.6 = (bf16[4,112,256]{2,1,0:T(8,128)(2,1)S(1)}, bf16[4,112,256]{2,1,0:T(8,128)(2,1)S(1)}, u32[]{:S(2)}, u32[]{:S(2)}) collective-permute-start(bf16[4,112,256]{2,1,0:T(8,128)(2,1)S(1)} %get-tuple-element.18), channel_id=1, source_target_pairs={{0,1},{1,0},{2,3},{3,2},{4,5},{5,4},{6,7},{7,6},{8,9},{9,8},{10,11... | collective-permute-start | bytes 688136 | tf_op jit(solution)/shard_map/ppermute | solution.py:41
  154.3 9.3 %collective-permute-start.10 = (bf16[2,112,256]{2,1,0:T(8,128)(2,1)S(1)}, bf16[2,112,256]{2,1,0:T(8,128)(2,1)S(1)}, u32[]{:S(2)}, u32[]{:S(2)}) collective-permute-start(bf16[2,112,256]{2,1,0:T(8,128)(2,1)S(1)} %get-tuple-element.25), channel_id=1, source_target_pairs={{0,2},{1,3},{2,0},{3,1},{4,6},{5,7},{6,4},{7,5},{8,10},{9,11},{10,... | collective-permute-start | bytes 344072 | tf_op jit(solution)/shard_map/ppermute | solution.py:41
  159.3 9.8 %collective-permute-start.7 = (bf16[2,112,256]{2,1,0:T(8,128)(2,1)S(1)}, bf16[2,112,256]{2,1,0:T(8,128)(2,1)S(1)}, u32[]{:S(2)}, u32[]{:S(2)}) collective-permute-start(bf16[2,112,256]{2,1,0:T(8,128)(2,1)S(1)} %get-tuple-element.20), channel_id=1, source_target_pairs={{0,2},{1,3},{2,0},{3,1},{4,6},{5,7},{6,4},{7,5},{8,10},{9,11},{10,... | collective-permute-start | bytes 344072 | tf_op jit(solution)/shard_map/ppermute | solution.py:41
  163.6 14.2 %collective-permute-start.11 = (bf16[112,256]{1,0:T(8,128)(2,1)S(1)}, bf16[112,256]{1,0:T(8,128)(2,1)S(1)}, u32[]{:S(2)}, u32[]{:S(2)}) collective-permute-start(bf16[112,256]{1,0:T(8,128)(2,1)S(1)} %get-tuple-element.27), channel_id=1, source_target_pairs={{0,4},{1,5},{2,6},{3,7},{4,0},{5,1},{6,2},{7,3},{8,12},{9,13},{10,... | collective-permute-start | bytes 172040 | tf_op jit(solution)/shard_map/ppermute | solution.py:41
  169.1 10.8 %collective-permute-start.8 = (bf16[112,256]{1,0:T(8,128)(2,1)S(1)}, bf16[112,256]{1,0:T(8,128)(2,1)S(1)}, u32[]{:S(2)}, u32[]{:S(2)}) collective-permute-start(bf16[112,256]{1,0:T(8,128)(2,1)S(1)} %get-tuple-element.22), channel_id=1, source_target_pairs={{0,4},{1,5},{2,6},{3,7},{4,0},{5,1},{6,2},{7,3},{8,12},{9,13},{10,... | collective-permute-start | bytes 172040 | tf_op jit(solution)/shard_map/ppermute | solution.py:41

commit v6 on v5

--- a/solution.py
+++ b/solution.py
@@ -15,7 +15,10 @@
 F32 = jnp.float32
 ROWS = 128
 WIDTH = 256
-CHUNK = 3 * ROWS
+HALF = ROWS // 2
+PACKED = HALF + HALF // 2
+PIECE = ROWS + PACKED
+CHUNK = 2 * ROWS + PACKED
 PARAMS = pltpu.CompilerParams(vmem_limit_bytes=16 << 20)
 VMEM = pl.BlockSpec(memory_space=pltpu.VMEM)
 SMEM = pl.BlockSpec(memory_space=pltpu.SMEM)
@@ -61,11 +64,6 @@
     return (floats - jnp.mean(floats, axis=0, keepdims=True)).astype(BF16)
 
 
-def source_kernel(acts_ref, partner_ref, out_ref):
-    out_ref[:ROWS, :] = center(acts_ref[...])
-    out_ref[ROWS:, :] = center(partner_ref[...])
-
-
 def split(values, parts):
     pieces = []
     for _ in range(parts):
@@ -75,15 +73,46 @@
     return pieces
 
 
+def left(rows):
+    return lax.broadcasted_iota(jnp.int32, (rows, ROWS), 1) < HALF
+
+
+def pack(values):
+    top, bottom = values[:HALF], values[HALF:]
+    corner = jnp.where(
+        left(HALF // 2), pltpu.roll(top[: HALF // 2], HALF, 1), top[HALF // 2 :]
+    )
+    return jnp.concatenate([jnp.where(left(HALF), top, bottom), corner], axis=0)
+
+
+def unpack(packed):
+    blocks, corner = packed[:HALF], packed[HALF:]
+    right = jnp.concatenate([pltpu.roll(corner, HALF, 1), corner], axis=0)
+    upper = jnp.concatenate([jnp.where(left(HALF), blocks, right), blocks], axis=0)
+    below = lax.broadcasted_iota(jnp.int32, (ROWS, ROWS), 0) >= HALF
+    return jnp.where(jnp.logical_and(below, left(ROWS)), upper.T, upper)
+
+
+def two_parts(values):
+    return jnp.concatenate(split(values, 2), axis=1)
+
+
+def joined(parts):
+    parts = parts.astype(F32)
+    return parts[:, :ROWS] + parts[:, ROWS:]
+
+
+def source_kernel(acts_ref, partner_ref, out_ref):
+    out_ref[:ROWS, :] = center(acts_ref[...])
+    out_ref[ROWS:, :] = two_parts(pack(gram(center(partner_ref[...]))))
+
+
 def chunk_kernel(flag_ref, first_ref, second_ref, chunk_ref):
     even = flag_ref[0] == 0
-    first, second = first_ref[...], second_ref[...]
-    low = jnp.where(even, first, second)
-    high = jnp.where(even, second, first)
-    chunk_ref[:ROWS, :] = low[:ROWS]
-    chunk_ref[ROWS : 2 * ROWS, :] = high[:ROWS]
-    gram_y = gram(jnp.concatenate([low[ROWS:], high[ROWS:]], axis=1))
-    chunk_ref[2 * ROWS :, :] = jnp.concatenate(split(gram_y, 2), axis=1)
+    first, second = first_ref[:ROWS, :], second_ref[:ROWS, :]
+    chunk_ref[:ROWS, :] = jnp.where(even, first, second)
+    chunk_ref[ROWS : 2 * ROWS, :] = jnp.where(even, second, first)
+    chunk_ref[2 * ROWS :, :] = two_parts(joined(first_ref[ROWS:, :]) + joined(second_ref[ROWS:, :]))
 
 
 def minibatch_grams(plane_ref, first):
@@ -96,12 +125,11 @@
     pair = gram(jnp.concatenate(rows, axis=0))
     grams = []
     for i in range(2):
-        gram_y = jnp.zeros((ROWS, ROWS), F32)
+        packed = jnp.zeros((PACKED, ROWS), F32)
         for x in range(4):
-            parts = plane_ref[x, first + i, pl.ds(2 * ROWS, ROWS), :].astype(F32)
-            gram_y = gram_y + (parts[:, :ROWS] + parts[:, ROWS:])
+            packed = packed + joined(plane_ref[x, first + i, pl.ds(2 * ROWS, PACKED), :])
         block = slice(i * ROWS, (i + 1) * ROWS)
-        grams.append((pair[block, block], gram_y))
+        grams.append((pair[block, block], unpack(packed)))
     return grams
 
 
@@ -355,7 +383,7 @@
         grid=(1,),
         in_specs=[whole(ROWS, WIDTH)] * 2,
         out_specs=VMEM,
-        out_shape=shape((2 * ROWS, WIDTH), BF16),
+        out_shape=shape((PIECE, WIDTH), BF16),
         compiler_params=PARAMS,
         name="source",
     )(acts, partner)

time: 181 us -> 174 us (0.961)
  waiting for transfers between devices: 50.7 us -> 48.3 us
  starting transfers between devices: 61.7 us -> 59.8 us
    ppermute x12, waiting for transfers between devices: 44.4 us -> 41.9 us  [permute(): return lax.ppermute(values, names, permutation(names, target))]
    ppermute x12, starting transfers between devices: 50.5 us -> 48.3 us  [permute(): return lax.ppermute(values, names, permutation(names, target))]
    unnamed x12 -> x14, local copies, waits for them, and re-layouts: 4.89 us -> 4.91 us
  transfers between devices with their start and end apart: 13 -> 13, of which waited for: 9 -> 9; matrix products, arithmetic and copies ran while one was open for 2% -> 1% of each run, Pallas kernels for 8% -> 8%
where the time goes in v6:
time: 174 us; the launch traced here: 173 us
  starting transfers between devices  59.8 us (34%)
  waiting for transfers between devices  48.3 us (28%)
  blocking collectives  41.9 us (24%)
  Pallas kernels  15.7 us (9%)
  local copies, waits for them, and re-layouts  5.7 us (3%)
    ppermute x12, starting transfers between devices, permute(): return lax.ppermute(values, names, permutation(names, target))  48.3 us
    ppermute x12, waiting for transfers between devices, permute(): return lax.ppermute(values, names, permutation(names, target))  41.9 us
    all_to_all x1, blocking collectives, exchange(): return lax.all_to_all(values, names, split_axis=0, concat_axis=0)  41.9 us
    all_to_all x1, starting transfers between devices, exchange(): return lax.all_to_all(values, names, split_axis=0, concat_axis=0)  11.5 us
    all_to_all x1, waiting for transfers between devices, exchange(): return lax.all_to_all(values, names, split_axis=0, concat_axis=0)  6.36 us
    unnamed x14, local copies, waits for them, and re-layouts  4.91 us
    pallas_call x1, Pallas kernels, hidden_gradient(): pl.pallas_call(hidden_kernel, in_specs=[SMEM] * 2 + [VMEM] * 5, out_specs...  4.68 us
  transfers between devices with their start and end apart: 13, of which 9 were waited for; matrix products, arithmetic and copies ran while one was open for 1% of the time, Pallas kernels for 8%

profile of v6, /device:TPU:1, one launch (start us, length us, event | category | flops | bytes accessed | tf_op | source)
XLA Modules:
  0.0 173.4 jit_solution(725512192667839605)
XLA Ops:
  0.6 0.0 copy-start.3
  0.6 0.8 copy-done.3
  1.5 0.0 copy-start.4
  1.5 0.8 copy-done.4
  2.3 0.2 source.1
  2.6 0.7 collective-permute-start.3
  3.2 17.5 %collective-permute-start.4 = (bf16[224,256]{1,0:T(8,128)(2,1)S(1)}, bf16[224,256]{1,0:T(8,128)(2,1)S(1)}, u32[]{:S(2)}, u32[]{:S(2)}) collective-permute-start(bf16[224,256]{1,0:T(8,128)(2,1)S(1)} %source.1), channel_id=1, source_target_pairs={{0,64},{1,0},{2,192},{3,128},{4,320},{5,256},{6,448},{7,384},{64,6... | collective-permute-start | bytes 344072 | tf_op jit(solution)/shard_map/ppermute | solution.py:44
  20.8 0.0 collective-permute-done.3.first_ref
  20.8 10.3 %collective-permute-done.4.second_ref = bf16[224,256]{1,0:T(8,128)(2,1)S(1)} collective-permute-done((bf16[224,256]{1,0:T(8,128)(2,1)S(1)}, bf16[224,256]{1,0:T(8,128)(2,1)S(1)}, u32[]{:S(2)}, u32[]{:S(2)}) %collective-permute-start.4) | collective-permute-done | bytes 114720 | tf_op jit(solution)/shard_map/ppermute | solution.py:44
  31.1 0.3 broadcast_in_dim.10
  31.4 0.0 copy-start.5
  31.4 41.9 %all_to_all.10 = bf16[16,352,256]{2,1,0:T(8,128)(2,1)S(1)} all-to-all(bf16[16,352,256]{2,1,0:T(8,128)(2,1)S(1)} %broadcast_in_dim.10), channel_id=1, replica_groups=mesh['x'=4,'zh'=2,'y'=4,'c'=2,'t'=8] {'x','y'}, dimensions={0} | all-to-all | bytes 5767168 | tf_op jit(solution)/shard_map/all_to_all | solution.py:48
  73.3 4.0 %collective-permute-start.5 = (bf16[16,352,256]{2,1,0:T(8,128)(2,1)S(1)}, bf16[16,352,256]{2,1,0:T(8,128)(2,1)}, u32[]{:S(2)}, u32[]{:S(2)}) collective-permute-start(bf16[16,352,256]{2,1,0:T(8,128)(2,1)S(1)} %all_to_all.10), channel_id=1, source_target_pairs={{0,8},{8,0},{1,9},{9,1},{2,10},{10,2},{3,11},{11,3},{4,12},{12,4},... | collective-permute-start | bytes 8650760 | tf_op jit(solution)/shard_map/ppermute | solution.py:44
  77.3 0.0 copy-done.5
  77.3 6.5 %collective-permute-start = (bf16[1,224,256]{2,1,0:T(8,128)(2,1)S(1)}, bf16[1,224,256]{2,1,0:T(8,128)(2,1)S(1)}, u32[]{:S(2)}, u32[]{:S(2)}) collective-permute-start(bf16[1,224,256]{2,1,0:T(8,128)(2,1)S(1)} %bitcast.12), channel_id=1, source_target_pairs={{0,4},{1,5},{2,6},{3,7},{4,0},{5,1},{6,2},{7,3},{8,12},{9,13},{10,... | collective-permute-start | bytes 344072 | tf_op jit(solution)/shard_map/ppermute | solution.py:44
  83.8 8.9 %collective-permute-done = bf16[1,224,256]{2,1,0:T(8,128)(2,1)S(1)} collective-permute-done((bf16[1,224,256]{2,1,0:T(8,128)(2,1)S(1)}, bf16[1,224,256]{2,1,0:T(8,128)(2,1)S(1)}, u32[]{:S(2)}, u32[]{:S(2)}) %collective-permute-start) | collective-permute-done | bytes 114720 | tf_op jit(solution)/shard_map/ppermute | solution.py:44
  92.8 2.8 %collective-permute-start.1 = (bf16[2,224,256]{2,1,0:T(8,128)(2,1)S(1)}, bf16[2,224,256]{2,1,0:T(8,128)(2,1)}, u32[]{:S(2)}, u32[]{:S(2)}) collective-permute-start(bf16[2,224,256]{2,1,0:T(8,128)(2,1)S(1)} %pad_maximum_fusion.1), channel_id=1, source_target_pairs={{0,2},{1,3},{2,0},{3,1},{4,6},{5,7},{6,4},{7,5},{8,10},{9,11},{10,... | collective-permute-start | bytes 688136 | tf_op jit(solution)/shard_map/ppermute | solution.py:44
  95.5 0.0 copy-done.6
  95.6 11.3 %collective-permute-done.1 = bf16[2,224,256]{2,1,0:T(8,128)(2,1)} collective-permute-done((bf16[2,224,256]{2,1,0:T(8,128)(2,1)S(1)}, bf16[2,224,256]{2,1,0:T(8,128)(2,1)}, u32[]{:S(2)}, u32[]{:S(2)}) %collective-permute-start.1) | collective-permute-done | bytes 229408 | tf_op jit(solution)/shard_map/ppermute | solution.py:44
  106.9 1.1 pad_maximum_fusion.near_ref
  107.9 2.0 %collective-permute-start.2 = (bf16[4,224,256]{2,1,0:T(8,128)(2,1)S(1)}, bf16[4,224,256]{2,1,0:T(8,128)(2,1)}, u32[]{:S(2)}, u32[]{:S(2)}) collective-permute-start(bf16[4,224,256]{2,1,0:T(8,128)(2,1)S(1)} %pad_maximum_fusion.near_ref), channel_id=1, source_target_pairs={{0,1},{1,0},{2,3},{3,2},{4,5},{5,4},{6,7},{7,6},{8,9},{9,8},{10,11... | collective-permute-start | bytes 1376264 | tf_op jit(solution)/shard_map/ppermute | solution.py:44
  109.9 1.4 plane_sums.1
  111.3 11.5 %all-to-all-start.1 = ((f32[16,8,128]{2,1,0:T(8,128)}), f32[16,8,128]{2,1,0:T(8,128)S(1)}, u32[]{:S(2)}, u32[]{:S(2)}) async-start(f32[16,8,128]{2,1,0:T(8,128)} %plane_sums.1), calls=%async_computation.1 | async-start | bytes 131072 | tf_op jit(solution)/shard_map/all_to_all | solution.py:48
  122.8 0.0 collective-permute-done.5
  122.8 3.1 %plane_grams.1.grams_ref = f32[2,8,128,128]{3,2,1,0:T(8,128)S(1)} custom-call(bf16[4,4,352,256]{3,2,1,0:T(8,128)(2,1)S(1)} %bitcast.8, bf16[4,4,352,256]{3,2,1,0:T(8,128)(2,1)} %bitcast.5.other_ref), custom_call_target="tpu_custom_call" | custom-call | flops 4294967296 | bytes 8388608 | tf_op jit(solution)/shard_map/plane_grams/pallas_call | solution.py:165
  125.9 0.0 copy-start
  125.9 1.0 copy-done
  126.9 6.4 %all-to-all-done.1.tiles_ref = f32[16,8,128]{2,1,0:T(8,128)S(1)} async-done(((f32[16,8,128]{2,1,0:T(8,128)}), f32[16,8,128]{2,1,0:T(8,128)S(1)}, u32[]{:S(2)}, u32[]{:S(2)}) %all-to-all-start.1) | async-done | bytes 65568 | tf_op jit(solution)/shard_map/all_to_all | solution.py:48
  133.3 1.2 copy-done.1
  134.5 1.0 copy-done.2
  135.5 2.9 %mix.1 = (f32[8,128,128]{2,1,0:T(8,128)S(1)}, bf16[224,1024]{1,0:T(8,128)(2,1)S(1)}, f32[8,128]{1,0:T(8,128)S(1)}, bf16[4,112,256]{2,1,0:T(8,128)(2,1)S(1)}, bf16[4,112,256]{2,1,0:T(8,128)(2,1)S(1)}) custom-call(s32[1]{0:T(128)} %bitcast.1.core_ref, s32[1]{0:T(128)} %bitcast.place_ref, f32[2,8,128,128]{3,2,1,0:T(8,128)S(1)} %copy-done.1, ...), custom_call_target="tpu_custom_call" | custom-call | tf_op jit(solution)/shard_map/mix/pallas_call | solution.py:210
  138.4 2.1 %collective-permute-start.9 = (bf16[4,112,256]{2,1,0:T(8,128)(2,1)S(1)}, bf16[4,112,256]{2,1,0:T(8,128)(2,1)S(1)}, u32[]{:S(2)}, u32[]{:S(2)}) collective-permute-start(bf16[4,112,256]{2,1,0:T(8,128)(2,1)S(1)} %get-tuple-element.23), channel_id=1, source_target_pairs={{0,1},{1,0},{2,3},{3,2},{4,5},{5,4},{6,7},{7,6},{8,9},{9,8},{10,11... | collective-permute-start | bytes 688136 | tf_op jit(solution)/shard_map/ppermute | solution.py:44
  140.5 3.2 %collective-permute-start.6 = (bf16[4,112,256]{2,1,0:T(8,128)(2,1)S(1)}, bf16[4,112,256]{2,1,0:T(8,128)(2,1)S(1)}, u32[]{:S(2)}, u32[]{:S(2)}) collective-permute-start(bf16[4,112,256]{2,1,0:T(8,128)(2,1)S(1)} %get-tuple-element.18), channel_id=1, source_target_pairs={{0,1},{1,0},{2,3},{3,2},{4,5},{5,4},{6,7},{7,6},{8,9},{9,8},{10,11... | collective-permute-start | bytes 688136 | tf_op jit(solution)/shard_map/ppermute | solution.py:44
  143.7 2.5 %weight_parts.1.kept_ref = f32[4,224,256]{2,1,0:T(8,128)S(1)} custom-call(s32[1]{0:T(128)} %bitcast.place_ref, bf16[224,1024]{1,0:T(8,128)(2,1)S(1)} %get-tuple-element.17.product_ref, bf16[4,4,352,256]{3,2,1,0:T(8,128)(2,1)S(1)} %bitcast.10, bf16[4,4,352,256]{3,2,1,0:T(8,128)(2,1)} %bitcast.5.other_ref), custom_call_target="tpu_custom_call" | custom-call | flops 469762048 | bytes 4194304 | tf_op jit(solution)/shard_map/weight_parts/pallas_call | solution.py:253
  146.2 0.9 collective-permute-done.9.arrived_ref
  147.1 1.9 %collective-permute-start.10 = (bf16[2,112,256]{2,1,0:T(8,128)(2,1)S(1)}, bf16[2,112,256]{2,1,0:T(8,128)(2,1)S(1)}, u32[]{:S(2)}, u32[]{:S(2)}) collective-permute-start(bf16[2,112,256]{2,1,0:T(8,128)(2,1)S(1)} %get-tuple-element.25), channel_id=1, source_target_pairs={{0,2},{1,3},{2,0},{3,1},{4,6},{5,7},{6,4},{7,5},{8,10},{9,11},{10,... | collective-permute-start | bytes 344072 | tf_op jit(solution)/shard_map/ppermute | solution.py:44
  149.1 2.9 %collective-permute-done.6.arrived_ref = bf16[4,112,256]{2,1,0:T(8,128)(2,1)S(1)} collective-permute-done((bf16[4,112,256]{2,1,0:T(8,128)(2,1)S(1)}, bf16[4,112,256]{2,1,0:T(8,128)(2,1)S(1)}, u32[]{:S(2)}, u32[]{:S(2)}) %collective-permute-start.6) | collective-permute-done | bytes 229408 | tf_op jit(solution)/shard_map/ppermute | solution.py:44
  152.1 1.9 %collective-permute-start.7 = (bf16[2,112,256]{2,1,0:T(8,128)(2,1)S(1)}, bf16[2,112,256]{2,1,0:T(8,128)(2,1)S(1)}, u32[]{:S(2)}, u32[]{:S(2)}) collective-permute-start(bf16[2,112,256]{2,1,0:T(8,128)(2,1)S(1)} %get-tuple-element.20), channel_id=1, source_target_pairs={{0,2},{1,3},{2,0},{3,1},{4,6},{5,7},{6,4},{7,5},{8,10},{9,11},{10,... | collective-permute-start | bytes 344072 | tf_op jit(solution)/shard_map/ppermute | solution.py:44
  154.0 0.5 slice.3
  154.5 1.9 %collective-permute-done.10.arrived_ref = bf16[2,112,256]{2,1,0:T(8,128)(2,1)S(1)} collective-permute-done((bf16[2,112,256]{2,1,0:T(8,128)(2,1)S(1)}, bf16[2,112,256]{2,1,0:T(8,128)(2,1)S(1)}, u32[]{:S(2)}, u32[]{:S(2)}) %collective-permute-start.10) | collective-permute-done | bytes 114720 | tf_op jit(solution)/shard_map/ppermute | solution.py:44
  156.5 1.9 %collective-permute-start.11 = (bf16[112,256]{1,0:T(8,128)(2,1)S(1)}, bf16[112,256]{1,0:T(8,128)(2,1)S(1)}, u32[]{:S(2)}, u32[]{:S(2)}) collective-permute-start(bf16[112,256]{1,0:T(8,128)(2,1)S(1)} %get-tuple-element.27), channel_id=1, source_target_pairs={{0,4},{1,5},{2,6},{3,7},{4,0},{5,1},{6,2},{7,3},{8,12},{9,13},{10,... | collective-permute-start | bytes 172040 | tf_op jit(solution)/shard_map/ppermute | solution.py:44
  158.4 3.4 %collective-permute-done.7.arrived_ref = bf16[2,112,256]{2,1,0:T(8,128)(2,1)S(1)} collective-permute-done((bf16[2,112,256]{2,1,0:T(8,128)(2,1)S(1)}, bf16[2,112,256]{2,1,0:T(8,128)(2,1)S(1)}, u32[]{:S(2)}, u32[]{:S(2)}) %collective-permute-start.7) | collective-permute-done | bytes 114720 | tf_op jit(solution)/shard_map/ppermute | solution.py:44
  161.9 3.8 %collective-permute-start.8 = (bf16[112,256]{1,0:T(8,128)(2,1)S(1)}, bf16[112,256]{1,0:T(8,128)(2,1)S(1)}, u32[]{:S(2)}, u32[]{:S(2)}) collective-permute-start(bf16[112,256]{1,0:T(8,128)(2,1)S(1)} %get-tuple-element.22), channel_id=1, source_target_pairs={{0,4},{1,5},{2,6},{3,7},{4,0},{5,1},{6,2},{7,3},{8,12},{9,13},{10,... | collective-permute-start | bytes 172040 | tf_op jit(solution)/shard_map/ppermute | solution.py:44
  165.7 0.0 collective-permute-done.2.far_ref
  165.7 4.7 %hidden_gradient.1 = bf16[224,1024]{1,0:T(8,128)(2,1)} custom-call(s32[1]{0:T(128)} %bitcast.place_ref, s32[1]{0:T(128)} %bitcast.1.core_ref, bf16[4,224,256]{2,1,0:T(8,128)(2,1)S(1)} %pad_maximum_fusion.near_ref, bf16[4,224,256]{2,1,0:T(8,128)(2,1)} %collective-permute-done.2.far_ref, bf16[4,4,352,256]{3,2,1,0:T(8,128)(2,1)S(1)} %bitcast.11, ...), custom_call_target="tpu_custom_call" | custom-call | flops 939524096 | bytes 8388608 | tf_op jit(solution)/shard_map/hidden_gradient/pallas_call | solution.py:295
  170.4 0.0 collective-permute-done.11.two_ref
  170.4 2.3 %collective-permute-done.8.one_ref = bf16[112,256]{1,0:T(8,128)(2,1)S(1)} collective-permute-done((bf16[112,256]{1,0:T(8,128)(2,1)S(1)}, bf16[112,256]{1,0:T(8,128)(2,1)S(1)}, u32[]{:S(2)}, u32[]{:S(2)}) %collective-permute-start.8) | collective-permute-done | bytes 57376 | tf_op jit(solution)/shard_map/ppermute | solution.py:44
  172.7 0.7 add_last.1
  (9 shorter events, 0.2 us)
Async XLA Ops:
  0.6 0.8 copy-start.3
  1.5 0.8 copy-start.4
  2.6 18.2 %collective-permute-start.3 = (bf16[224,256]{1,0:T(8,128)(2,1)S(1)}, bf16[224,256]{1,0:T(8,128)(2,1)S(1)}, u32[]{:S(2)}, u32[]{:S(2)}) collective-permute-start(bf16[224,256]{1,0:T(8,128)(2,1)S(1)} %source.1), channel_id=1, source_target_pairs={{0,0},{1,64},{2,128},{3,192},{4,256},{5,320},{6,384},{7,448},{64,1... | collective-permute-start | bytes 344072 | tf_op jit(solution)/shard_map/ppermute | solution.py:44
  3.2 27.8 %collective-permute-start.4 = (bf16[224,256]{1,0:T(8,128)(2,1)S(1)}, bf16[224,256]{1,0:T(8,128)(2,1)S(1)}, u32[]{:S(2)}, u32[]{:S(2)}) collective-permute-start(bf16[224,256]{1,0:T(8,128)(2,1)S(1)} %source.1), channel_id=1, source_target_pairs={{0,64},{1,0},{2,192},{3,128},{4,320},{5,256},{6,448},{7,384},{64,6... | collective-permute-start | bytes 344072 | tf_op jit(solution)/shard_map/ppermute | solution.py:44
  31.4 45.9 %copy-start.5 = (bf16[224,256]{1,0:T(8,128)(2,1)S(1)}, bf16[224,256]{1,0:T(8,128)(2,1)}, u32[]{:S(2)}) copy-start(bf16[224,256]{1,0:T(8,128)(2,1)} %param.7) | copy-start | bytes 344068
  73.3 49.5 %collective-permute-start.5 = (bf16[16,352,256]{2,1,0:T(8,128)(2,1)S(1)}, bf16[16,352,256]{2,1,0:T(8,128)(2,1)}, u32[]{:S(2)}, u32[]{:S(2)}) collective-permute-start(bf16[16,352,256]{2,1,0:T(8,128)(2,1)S(1)} %all_to_all.10), channel_id=1, source_target_pairs={{0,8},{8,0},{1,9},{9,1},{2,10},{10,2},{3,11},{11,3},{4,12},{12,4},... | collective-permute-start | bytes 8650760 | tf_op jit(solution)/shard_map/ppermute | solution.py:44
  77.3 15.4 %collective-permute-start = (bf16[1,224,256]{2,1,0:T(8,128)(2,1)S(1)}, bf16[1,224,256]{2,1,0:T(8,128)(2,1)S(1)}, u32[]{:S(2)}, u32[]{:S(2)}) collective-permute-start(bf16[1,224,256]{2,1,0:T(8,128)(2,1)S(1)} %bitcast.12), channel_id=1, source_target_pairs={{0,4},{1,5},{2,6},{3,7},{4,0},{5,1},{6,2},{7,3},{8,12},{9,13},{10,... | collective-permute-start | bytes 344072 | tf_op jit(solution)/shard_map/ppermute | solution.py:44
  92.7 2.8 %copy-start.6 = (bf16[1,224,256]{2,1,0:T(8,128)(2,1)}, bf16[1,224,256]{2,1,0:T(8,128)(2,1)S(1)}, u32[]{:S(2)}) copy-start(bf16[1,224,256]{2,1,0:T(8,128)(2,1)S(1)} %collective-permute-done) | copy-start | bytes 344068
  92.8 14.1 %collective-permute-start.1 = (bf16[2,224,256]{2,1,0:T(8,128)(2,1)S(1)}, bf16[2,224,256]{2,1,0:T(8,128)(2,1)}, u32[]{:S(2)}, u32[]{:S(2)}) collective-permute-start(bf16[2,224,256]{2,1,0:T(8,128)(2,1)S(1)} %pad_maximum_fusion.1), channel_id=1, source_target_pairs={{0,2},{1,3},{2,0},{3,1},{4,6},{5,7},{6,4},{7,5},{8,10},{9,11},{10,... | collective-permute-start | bytes 688136 | tf_op jit(solution)/shard_map/ppermute | solution.py:44
  107.9 57.8 %collective-permute-start.2 = (bf16[4,224,256]{2,1,0:T(8,128)(2,1)S(1)}, bf16[4,224,256]{2,1,0:T(8,128)(2,1)}, u32[]{:S(2)}, u32[]{:S(2)}) collective-permute-start(bf16[4,224,256]{2,1,0:T(8,128)(2,1)S(1)} %pad_maximum_fusion.near_ref), channel_id=1, source_target_pairs={{0,1},{1,0},{2,3},{3,2},{4,5},{5,4},{6,7},{7,6},{8,9},{9,8},{10,11... | collective-permute-start | bytes 1376264 | tf_op jit(solution)/shard_map/ppermute | solution.py:44
  111.3 22.0 %all-to-all-start.1 = ((f32[16,8,128]{2,1,0:T(8,128)}), f32[16,8,128]{2,1,0:T(8,128)S(1)}, u32[]{:S(2)}, u32[]{:S(2)}) async-start(f32[16,8,128]{2,1,0:T(8,128)} %plane_sums.1), calls=%async_computation.1 | async-start | bytes 131072 | tf_op jit(solution)/shard_map/all_to_all | solution.py:48
  125.9 1.0 copy-start
  133.3 1.2 copy-start.1
  134.5 1.0 copy-start.2
  138.4 8.7 %collective-permute-start.9 = (bf16[4,112,256]{2,1,0:T(8,128)(2,1)S(1)}, bf16[4,112,256]{2,1,0:T(8,128)(2,1)S(1)}, u32[]{:S(2)}, u32[]{:S(2)}) collective-permute-start(bf16[4,112,256]{2,1,0:T(8,128)(2,1)S(1)} %get-tuple-element.23), channel_id=1, source_target_pairs={{0,1},{1,0},{2,3},{3,2},{4,5},{5,4},{6,7},{7,6},{8,9},{9,8},{10,11... | collective-permute-start | bytes 688136 | tf_op jit(solution)/shard_map/ppermute | solution.py:44
  140.5 11.5 %collective-permute-start.6 = (bf16[4,112,256]{2,1,0:T(8,128)(2,1)S(1)}, bf16[4,112,256]{2,1,0:T(8,128)(2,1)S(1)}, u32[]{:S(2)}, u32[]{:S(2)}) collective-permute-start(bf16[4,112,256]{2,1,0:T(8,128)(2,1)S(1)} %get-tuple-element.18), channel_id=1, source_target_pairs={{0,1},{1,0},{2,3},{3,2},{4,5},{5,4},{6,7},{7,6},{8,9},{9,8},{10,11... | collective-permute-start | bytes 688136 | tf_op jit(solution)/shard_map/ppermute | solution.py:44
  147.1 9.3 %collective-permute-start.10 = (bf16[2,112,256]{2,1,0:T(8,128)(2,1)S(1)}, bf16[2,112,256]{2,1,0:T(8,128)(2,1)S(1)}, u32[]{:S(2)}, u32[]{:S(2)}) collective-permute-start(bf16[2,112,256]{2,1,0:T(8,128)(2,1)S(1)} %get-tuple-element.25), channel_id=1, source_target_pairs={{0,2},{1,3},{2,0},{3,1},{4,6},{5,7},{6,4},{7,5},{8,10},{9,11},{10,... | collective-permute-start | bytes 344072 | tf_op jit(solution)/shard_map/ppermute | solution.py:44
  152.1 9.8 %collective-permute-start.7 = (bf16[2,112,256]{2,1,0:T(8,128)(2,1)S(1)}, bf16[2,112,256]{2,1,0:T(8,128)(2,1)S(1)}, u32[]{:S(2)}, u32[]{:S(2)}) collective-permute-start(bf16[2,112,256]{2,1,0:T(8,128)(2,1)S(1)} %get-tuple-element.20), channel_id=1, source_target_pairs={{0,2},{1,3},{2,0},{3,1},{4,6},{5,7},{6,4},{7,5},{8,10},{9,11},{10,... | collective-permute-start | bytes 344072 | tf_op jit(solution)/shard_map/ppermute | solution.py:44
  156.5 13.9 %collective-permute-start.11 = (bf16[112,256]{1,0:T(8,128)(2,1)S(1)}, bf16[112,256]{1,0:T(8,128)(2,1)S(1)}, u32[]{:S(2)}, u32[]{:S(2)}) collective-permute-start(bf16[112,256]{1,0:T(8,128)(2,1)S(1)} %get-tuple-element.27), channel_id=1, source_target_pairs={{0,4},{1,5},{2,6},{3,7},{4,0},{5,1},{6,2},{7,3},{8,12},{9,13},{10,... | collective-permute-start | bytes 172040 | tf_op jit(solution)/shard_map/ppermute | solution.py:44
  161.9 10.8 %collective-permute-start.8 = (bf16[112,256]{1,0:T(8,128)(2,1)S(1)}, bf16[112,256]{1,0:T(8,128)(2,1)S(1)}, u32[]{:S(2)}, u32[]{:S(2)}) collective-permute-start(bf16[112,256]{1,0:T(8,128)(2,1)S(1)} %get-tuple-element.22), channel_id=1, source_target_pairs={{0,4},{1,5},{2,6},{3,7},{4,0},{5,1},{6,2},{7,3},{8,12},{9,13},{10,... | collective-permute-start | bytes 172040 | tf_op jit(solution)/shard_map/ppermute | solution.py:44

commit v7 on v6

--- a/solution.py
+++ b/solution.py
@@ -22,10 +22,7 @@
 PARAMS = pltpu.CompilerParams(vmem_limit_bytes=16 << 20)
 VMEM = pl.BlockSpec(memory_space=pltpu.VMEM)
 SMEM = pl.BlockSpec(memory_space=pltpu.SMEM)
-
-
-def whole(*shape):
-    return pl.BlockSpec(shape, lambda i: (0,) * len(shape))
+HBM = pl.BlockSpec(memory_space=pltpu.HBM)
 
 
 def permutation(names, target):
@@ -102,9 +99,23 @@
     return parts[:, :ROWS] + parts[:, ROWS:]
 
 
-def source_kernel(acts_ref, partner_ref, out_ref):
+def in_hbm(values):
+    return pltpu.with_memory_space_constraint(values, pltpu.HBM)
+
+
+def fetch(source, target, semaphores, i):
+    copy = pltpu.make_async_copy(source, target, semaphores.at[i])
+    copy.start()
+    return copy
+
+
+def source_kernel(acts_hbm, partner_hbm, out_ref, acts_ref, partner_ref, semaphores):
+    partner = fetch(partner_hbm, partner_ref, semaphores, 0)
+    acts = fetch(acts_hbm, acts_ref, semaphores, 1)
+    partner.wait()
+    out_ref[ROWS:, :] = two_parts(pack(gram(center(partner_ref[...]))))
+    acts.wait()
     out_ref[:ROWS, :] = center(acts_ref[...])
-    out_ref[ROWS:, :] = two_parts(pack(gram(center(partner_ref[...]))))
 
 
 def chunk_kernel(flag_ref, first_ref, second_ref, chunk_ref):
@@ -153,32 +164,12 @@
     )(plane)
 
 
-def grams_kernel(own_ref, other_ref, grams_ref):
-    for base, ref in ((0, own_ref), (4, other_ref)):
-        for y in (0, 2):
-            for i, (gram_x, gram_y) in enumerate(minibatch_grams(ref, y)):
-                grams_ref[0, base + y + i] = gram_x
-                grams_ref[1, base + y + i] = gram_y
-
-
-def plane_grams(plane, other):
-    return pl.pallas_call(
-        grams_kernel,
-        in_specs=[VMEM] * 2,
-        out_specs=VMEM,
-        out_shape=jax.ShapeDtypeStruct((2, 8, ROWS, ROWS), F32),
-        compiler_params=PARAMS,
-        cost_estimate=pl.CostEstimate(
-            flops=4 << 30, bytes_accessed=8 << 20, transcendentals=0
-        ),
-        name="plane_grams",
-    )(plane, other)
-
-
 def mix_kernel(
-    scale, core_ref, place_ref, grams_ref, tiles_ref, hidden_ref, own_ref, other_ref,
-    mixed_ref, product_ref, cka_ref, upper_ref, lower_ref,
+    scale, core_ref, place_ref, tiles_ref, own_ref, hidden_hbm, other_hbm,
+    mixed_ref, product_ref, cka_ref, upper_ref, lower_ref, hidden_ref, other_ref, semaphores,
 ):
+    other_copy = fetch(other_hbm, other_ref, semaphores, 0)
+    hidden_copy = fetch(hidden_hbm, hidden_ref, semaphores, 1)
     sums = jnp.sum(jnp.sum(tiles_ref[...], axis=0), axis=1, keepdims=True)
     sxx, syy, sxy = sums[0:1], sums[1:2], sums[2:3]
     root = jnp.sqrt(sxx * syy)
@@ -186,14 +177,23 @@
     coef = jnp.broadcast_to(-2.0 * scale / root, (1, ROWS))
     cka_ref[...] = jnp.broadcast_to(sxy / root, cka_ref.shape)
     core = core_ref[0]
+
+    def mix_pair(ref, base, first):
+        for i, (gram_x, gram_y) in enumerate(minibatch_grams(ref, first)):
+            mixed_ref[base + first + i] = coef * (gram_y - ratio * gram_x)
+
+    mix_pair(own_ref, 0, 0)
+    mix_pair(own_ref, 0, 2)
+    other_copy.wait()
+    mix_pair(other_ref, 4, 0)
+    mix_pair(other_ref, 4, 2)
+    hidden_copy.wait()
     for b in range(8):
-        mixed = coef * (grams_ref[1, b] - ratio * grams_ref[0, b])
-        mixed_ref[b] = mixed
         place = b % 4 * 2 + (core if b < 4 else 1 - core)
         hidden = hidden_ref[:, pl.ds(pl.multiple_of(place * ROWS, ROWS), ROWS)]
         product = jnp.dot(
             jnp.concatenate([hidden, hidden], axis=1),
-            jnp.concatenate(split(mixed, 2), axis=0),
+            jnp.concatenate(split(mixed_ref[b], 2), axis=0),
             preferred_element_type=F32,
         )
         product_ref[:, b * ROWS : (b + 1) * ROWS] = product.astype(BF16)
@@ -204,14 +204,12 @@
         lower_ref[k] = value[middle:]
 
 
-def mix(core, place, grams, tiles, hidden, plane, other, scale):
+def mix(core, place, tiles, hidden, plane, other, scale):
     units = hidden.shape[0]
     half = jax.ShapeDtypeStruct((4, units // 2, WIDTH), BF16)
     return pl.pallas_call(
         functools.partial(mix_kernel, scale),
-        grid=(1,),
-        in_specs=[SMEM] * 2
-        + [whole(2, 8, ROWS, ROWS), VMEM, whole(*hidden.shape), VMEM, VMEM],
+        in_specs=[SMEM] * 2 + [VMEM] * 2 + [HBM] * 2,
         out_specs=[VMEM] * 5,
         out_shape=[
             jax.ShapeDtypeStruct((8, ROWS, ROWS), F32),
@@ -220,9 +218,14 @@
             half,
             half,
         ],
+        scratch_shapes=[
+            pltpu.VMEM(hidden.shape, BF16),
+            pltpu.VMEM(other.shape, BF16),
+            pltpu.SemaphoreType.DMA((2,)),
+        ],
         compiler_params=PARAMS,
         name="mix",
-    )(core, place, grams, tiles, hidden, plane, other)
+    )(core, place, tiles, plane, in_hbm(hidden), other)
 
 
 def column_block(place, k):
@@ -264,13 +267,18 @@
 
 
 def hidden_kernel(
-    place_ref, core_ref, near_ref, far_ref, own_ref, other_ref, mixed_ref, out_ref
+    place_ref, core_ref, near_ref, two_ref, one_ref, three_ref, own_ref, mixed_ref, other_hbm,
+    out_ref, other_ref, semaphores,
 ):
+    other_copy = fetch(other_hbm, other_ref, semaphores, 0)
+    weights = [ref[i] for ref in (near_ref, two_ref, one_ref, three_ref) for i in range(2)]
     for ref, first in ((own_ref, 0), (other_ref, 4)):
+        if first == 4:
+            other_copy.wait()
         total = None
         for k in range(8):
             product = lax.dot_general(
-                near_ref[k] if k < 4 else far_ref[k - 4],
+                weights[k],
                 token_rows(ref, column_block(place_ref[0], k)),
                 (((1,), (1,)), ((), ())),
                 preferred_element_type=F32,
@@ -289,20 +297,21 @@
             out_ref[:, pl.ds(pl.multiple_of(place * ROWS, ROWS), ROWS)] = value.astype(BF16)
 
 
-def hidden_gradient(place, core, near, far, plane, other, mixed):
-    units = near.shape[1]
+def hidden_gradient(place, core, weights, plane, other, mixed):
+    units = weights[0].shape[1]
     tokens = 8 * ROWS
     return pl.pallas_call(
         hidden_kernel,
-        in_specs=[SMEM] * 2 + [VMEM] * 5,
+        in_specs=[SMEM] * 2 + [VMEM] * 6 + [HBM],
         out_specs=VMEM,
         out_shape=jax.ShapeDtypeStruct((units, tokens), BF16),
+        scratch_shapes=[pltpu.VMEM(other.shape, BF16), pltpu.SemaphoreType.DMA((1,))],
         compiler_params=PARAMS,
         cost_estimate=pl.CostEstimate(
             flops=2 * units * tokens * 8 * WIDTH, bytes_accessed=8 << 20, transcendentals=0
         ),
         name="hidden_gradient",
-    )(place, core, near, far, plane, other, mixed)
+    )(place, core, *weights, plane, mixed, other)
 
 
 def add_one_kernel(row, kept_ref, arrived_ref, out_ref, moved_ref):
@@ -375,18 +384,18 @@
     near = down_weight[None]
     far = permute(near, ("t",), flip(4))
     near = jnp.concatenate([near, far], axis=0)
-    far = permute(near, ("t",), flip(2))
-    near = jnp.concatenate([near, far], axis=0)
-    far = permute(near, ("t",), flip(1))
+    weights = [near]
+    for bit in (2, 1, 3):
+        weights.append(permute(near, ("t",), flip(bit)))
     piece = pl.pallas_call(
         source_kernel,
-        grid=(1,),
-        in_specs=[whole(ROWS, WIDTH)] * 2,
-        out_specs=VMEM,
+        in_specs=[HBM] * 2,
+        out_specs=VMEM,
+        scratch_shapes=[pltpu.VMEM((ROWS, WIDTH), BF16)] * 2 + [pltpu.SemaphoreType.DMA((2,))],
         out_shape=shape((PIECE, WIDTH), BF16),
         compiler_params=PARAMS,
         name="source",
-    )(acts, partner)
+    )(in_hbm(acts), in_hbm(partner))
     first = permute(piece, ("x", "zh", "t"), to_plane(0))
     second = permute(piece, ("x", "zh", "t"), to_plane(1))
     chunk = pl.pallas_call(
@@ -402,8 +411,7 @@
     plane = plane.reshape(4, 4, CHUNK, WIDTH)
     other = other.reshape(4, 4, CHUNK, WIDTH)
     tiles = exchange(plane_sums(plane), ("c", "t"))
-    grams = plane_grams(plane, other)
-    mixed, product, cka, *sent = mix(core, place, grams, tiles, hidden, plane, other, scale)
+    mixed, product, cka, *sent = mix(core, place, tiles, hidden, plane, other, scale)
     arrived, later, last = {}, {}, {}
     for name, values in zip("ab", sent):
         arrived[name] = permute(values, ("t",), flip(1))
@@ -416,7 +424,7 @@
         halves[name], moved = add_two(halves[name], later[name])
         last[name] = permute(moved, ("t",), flip(4))
     grad_weight = add_last(halves["a"], last["a"], halves["b"], last["b"])
-    grad_hidden = hidden_gradient(place, core, near, far, plane, other, mixed)
+    grad_hidden = hidden_gradient(place, core, weights, plane, other, mixed)
     return (grad_hidden, grad_weight, cka[0, 0])
 
 

time: 174 us -> 162 us (0.931); the launches traced: 173 us -> 159 us
  waiting for transfers between devices: 48.3 us -> 27.9 us
  starting transfers between devices: 59.8 us -> 74 us
  local copies, waits for them, and re-layouts: 5.7 us -> 0.79 us
  Pallas kernels: 15.7 us -> 13.6 us
    ppermute x12 -> x13, waiting for transfers between devices: 41.9 us -> 24.6 us  [permute(): return lax.ppermute(values, names, permutation(names, target))]
    ppermute x12 -> x13, starting transfers between devices: 48.3 us -> 59 us  [permute(): return lax.ppermute(values, names, permutation(names, target))]
    unnamed x14 -> x2, local copies, waits for them, and re-layouts: 4.91 us -> 0.01 us
    all_to_all x1, starting transfers between devices: 11.5 us -> 15 us  [exchange(): return lax.all_to_all(values, names, split_axis=0, concat_axis=0)]
    all_to_all x1, waiting for transfers between devices: 6.36 us -> 3.27 us  [exchange(): return lax.all_to_all(values, names, split_axis=0, concat_axis=0)]
    pallas_call x4 -> x3, Pallas kernels: 10.9 us -> 8.83 us  [the longest x1 4.17 us: hidden_gradient(): pl.pallas_call(hidden_kernel, in_specs=[SMEM] * 2 + [VMEM] * 6 + [HBM], o...]
  transfers between devices with their start and end apart: 13 -> 14, of which waited for: 9 -> 6; matrix products, arithmetic and copies ran while one was open for 1% -> 0% of each run, Pallas kernels for 8% -> 7%
where the time goes in v7:
time: 162 us; the launch traced here: 159 us
  starting transfers between devices  74 us (46%)
  blocking collectives  41.8 us (26%)
  waiting for transfers between devices  27.9 us (17%)
  Pallas kernels  13.6 us (8%)
    ppermute x13, starting transfers between devices, permute(): return lax.ppermute(values, names, permutation(names, target))  59 us
    all_to_all x1, blocking collectives, exchange(): return lax.all_to_all(values, names, split_axis=0, concat_axis=0)  41.8 us
    ppermute x13, waiting for transfers between devices, permute(): return lax.ppermute(values, names, permutation(names, target))  24.6 us
    all_to_all x1, starting transfers between devices, exchange(): return lax.all_to_all(values, names, split_axis=0, concat_axis=0)  15 us
    pallas_call x1, Pallas kernels, hidden_gradient(): pl.pallas_call(hidden_kernel, in_specs=[SMEM] * 2 + [VMEM] * 6 + [HBM], o...  4.17 us
    pallas_call x1, Pallas kernels, mix(): pl.pallas_call(functools.partial(mix_kernel, scale), in_specs=[SMEM] * 2...  3.51 us
    all_to_all x1, waiting for transfers between devices, exchange(): return lax.all_to_all(values, names, split_axis=0, concat_axis=0)  3.27 us
  transfers between devices with their start and end apart: 14, of which 6 were waited for; matrix products, arithmetic and copies ran while one was open for 0% of the time, Pallas kernels for 7%

profile of v7, /device:TPU:1, one launch (start us, length us, event | category | flops | bytes accessed | tf_op | source)
XLA Modules:
  0.0 158.9 jit_solution(12675666142376645256)
XLA Ops:
  0.6 1.1 source.1
  1.8 0.7 collective-permute-start.4
  2.5 17.5 %collective-permute-start.5 = (bf16[224,256]{1,0:T(8,128)(2,1)S(1)}, bf16[224,256]{1,0:T(8,128)(2,1)S(1)}, u32[]{:S(2)}, u32[]{:S(2)}) collective-permute-start(bf16[224,256]{1,0:T(8,128)(2,1)S(1)} %source.1), channel_id=1, source_target_pairs={{0,64},{1,0},{2,192},{3,128},{4,320},{5,256},{6,448},{7,384},{64,6... | collective-permute-start | bytes 344072 | tf_op jit(solution)/shard_map/ppermute | solution.py:41
  20.0 0.0 collective-permute-done.4.first_ref
  20.0 10.3 %collective-permute-done.5.second_ref = bf16[224,256]{1,0:T(8,128)(2,1)S(1)} collective-permute-done((bf16[224,256]{1,0:T(8,128)(2,1)S(1)}, bf16[224,256]{1,0:T(8,128)(2,1)S(1)}, u32[]{:S(2)}, u32[]{:S(2)}) %collective-permute-start.5) | collective-permute-done | bytes 114720 | tf_op jit(solution)/shard_map/ppermute | solution.py:41
  30.3 0.3 broadcast_in_dim.10
  30.6 41.8 %all_to_all.10 = bf16[16,352,256]{2,1,0:T(8,128)(2,1)S(1)} all-to-all(bf16[16,352,256]{2,1,0:T(8,128)(2,1)S(1)} %broadcast_in_dim.10), channel_id=1, replica_groups=mesh['x'=4,'zh'=2,'y'=4,'c'=2,'t'=8] {'x','y'}, dimensions={0} | all-to-all | bytes 5767168 | tf_op jit(solution)/shard_map/all_to_all | solution.py:45
  72.4 0.0 copy-start
  72.4 4.1 %collective-permute-start.6 = (bf16[16,352,256]{2,1,0:T(8,128)(2,1)S(1)}, bf16[16,352,256]{2,1,0:T(8,128)(2,1)}, u32[]{:S(2)}, u32[]{:S(2)}) collective-permute-start(bf16[16,352,256]{2,1,0:T(8,128)(2,1)S(1)} %all_to_all.10), channel_id=1, source_target_pairs={{0,8},{8,0},{1,9},{9,1},{2,10},{10,2},{3,11},{11,3},{4,12},{12,4},... | collective-permute-start | bytes 8650760 | tf_op jit(solution)/shard_map/ppermute | solution.py:41
  76.5 1.4 plane_sums.1
  77.9 15.0 %all-to-all-start.1 = ((f32[16,8,128]{2,1,0:T(8,128)}), f32[16,8,128]{2,1,0:T(8,128)S(1)}, u32[]{:S(2)}, u32[]{:S(2)}) async-start(f32[16,8,128]{2,1,0:T(8,128)} %plane_sums.1), calls=%async_computation.1 | async-start | bytes 131072 | tf_op jit(solution)/shard_map/all_to_all | solution.py:45
  92.9 0.0 copy-done
  92.9 7.2 %collective-permute-start = (bf16[1,224,256]{2,1,0:T(8,128)(2,1)S(1)}, bf16[1,224,256]{2,1,0:T(8,128)(2,1)S(1)}, u32[]{:S(2)}, u32[]{:S(2)}) collective-permute-start(bf16[1,224,256]{2,1,0:T(8,128)(2,1)S(1)} %bitcast.11), channel_id=1, source_target_pairs={{0,4},{1,5},{2,6},{3,7},{4,0},{5,1},{6,2},{7,3},{8,12},{9,13},{10,... | collective-permute-start | bytes 344072 | tf_op jit(solution)/shard_map/ppermute | solution.py:41
  100.1 3.3 %all-to-all-done.1.tiles_ref = f32[16,8,128]{2,1,0:T(8,128)S(1)} async-done(((f32[16,8,128]{2,1,0:T(8,128)}), f32[16,8,128]{2,1,0:T(8,128)S(1)}, u32[]{:S(2)}, u32[]{:S(2)}) %all-to-all-start.1) | async-done | bytes 65568 | tf_op jit(solution)/shard_map/all_to_all | solution.py:45
  103.4 0.0 collective-permute-done.6
  103.4 3.5 %mix.1 = (f32[8,128,128]{2,1,0:T(8,128)S(1)}, bf16[224,1024]{1,0:T(8,128)(2,1)S(1)}, f32[8,128]{1,0:T(8,128)S(1)}, bf16[4,112,256]{2,1,0:T(8,128)(2,1)S(1)}, bf16[4,112,256]{2,1,0:T(8,128)(2,1)S(1)}) custom-call(s32[1]{0:T(128)} %bitcast.1.core_ref, s32[1]{0:T(128)} %bitcast.place_ref, f32[16,8,128]{2,1,0:T(8,128)S(1)} %all-to-all-done.1.tiles_ref, ...), custom_call_target="tpu_custom_call" | custom-call | tf_op jit(solution)/shard_map/mix/pallas_call | solution.py:210
  106.9 2.1 %collective-permute-start.10 = (bf16[4,112,256]{2,1,0:T(8,128)(2,1)S(1)}, bf16[4,112,256]{2,1,0:T(8,128)(2,1)S(1)}, u32[]{:S(2)}, u32[]{:S(2)}) collective-permute-start(bf16[4,112,256]{2,1,0:T(8,128)(2,1)S(1)} %get-tuple-element.23), channel_id=1, source_target_pairs={{0,1},{1,0},{2,3},{3,2},{4,5},{5,4},{6,7},{7,6},{8,9},{9,8},{10,11... | collective-permute-start | bytes 688136 | tf_op jit(solution)/shard_map/ppermute | solution.py:41
  109.0 3.2 %collective-permute-start.7 = (bf16[4,112,256]{2,1,0:T(8,128)(2,1)S(1)}, bf16[4,112,256]{2,1,0:T(8,128)(2,1)S(1)}, u32[]{:S(2)}, u32[]{:S(2)}) collective-permute-start(bf16[4,112,256]{2,1,0:T(8,128)(2,1)S(1)} %get-tuple-element.18), channel_id=1, source_target_pairs={{0,1},{1,0},{2,3},{3,2},{4,5},{5,4},{6,7},{7,6},{8,9},{9,8},{10,11... | collective-permute-start | bytes 688136 | tf_op jit(solution)/shard_map/ppermute | solution.py:41
  112.2 0.4 collective-permute-done
  112.6 1.9 %collective-permute-start.1 = (bf16[2,224,256]{2,1,0:T(8,128)(2,1)S(1)}, bf16[2,224,256]{2,1,0:T(8,128)(2,1)S(1)}, u32[]{:S(2)}, u32[]{:S(2)}) collective-permute-start(bf16[2,224,256]{2,1,0:T(8,128)(2,1)S(1)} %pad_maximum_fusion.near_ref), channel_id=1, source_target_pairs={{0,2},{1,3},{2,0},{3,1},{4,6},{5,7},{6,4},{7,5},{8,10},{9,11},{10,... | collective-permute-start | bytes 688136 | tf_op jit(solution)/shard_map/ppermute | solution.py:41
  114.5 3.0 %collective-permute-start.2 = (bf16[2,224,256]{2,1,0:T(8,128)(2,1)S(1)}, bf16[2,224,256]{2,1,0:T(8,128)(2,1)S(1)}, u32[]{:S(2)}, u32[]{:S(2)}) collective-permute-start(bf16[2,224,256]{2,1,0:T(8,128)(2,1)S(1)} %pad_maximum_fusion.near_ref), channel_id=1, source_target_pairs={{0,1},{1,0},{2,3},{3,2},{4,5},{5,4},{6,7},{7,6},{8,9},{9,8},{10,11... | collective-permute-start | bytes 688136 | tf_op jit(solution)/shard_map/ppermute | solution.py:41
  117.5 4.4 %collective-permute-start.3 = (bf16[2,224,256]{2,1,0:T(8,128)(2,1)S(1)}, bf16[2,224,256]{2,1,0:T(8,128)(2,1)S(1)}, u32[]{:S(2)}, u32[]{:S(2)}) collective-permute-start(bf16[2,224,256]{2,1,0:T(8,128)(2,1)S(1)} %pad_maximum_fusion.near_ref), channel_id=1, source_target_pairs={{0,3},{1,2},{2,1},{3,0},{4,7},{5,6},{6,5},{7,4},{8,11},{9,10},{10,... | collective-permute-start | bytes 688136 | tf_op jit(solution)/shard_map/ppermute | solution.py:41
  121.9 2.5 %weight_parts.1.kept_ref = f32[4,224,256]{2,1,0:T(8,128)S(1)} custom-call(s32[1]{0:T(128)} %bitcast.place_ref, bf16[224,1024]{1,0:T(8,128)(2,1)S(1)} %get-tuple-element.17.product_ref, bf16[4,4,352,256]{3,2,1,0:T(8,128)(2,1)S(1)} %bitcast.9, bf16[4,4,352,256]{3,2,1,0:T(8,128)(2,1)} %bitcast.5.other_hbm.other_ref), custom_call_target="tpu_custom_call" | custom-call | flops 469762048 | bytes 4194304 | tf_op jit(solution)/shard_map/weight_parts/pallas_call | solution.py:256
  124.4 0.0 collective-permute-done.10.arrived_ref
  124.4 1.9 %collective-permute-start.11 = (bf16[2,112,256]{2,1,0:T(8,128)(2,1)S(1)}, bf16[2,112,256]{2,1,0:T(8,128)(2,1)S(1)}, u32[]{:S(2)}, u32[]{:S(2)}) collective-permute-start(bf16[2,112,256]{2,1,0:T(8,128)(2,1)S(1)} %get-tuple-element.25), channel_id=1, source_target_pairs={{0,2},{1,3},{2,0},{3,1},{4,6},{5,7},{6,4},{7,5},{8,10},{9,11},{10,... | collective-permute-start | bytes 344072 | tf_op jit(solution)/shard_map/ppermute | solution.py:41
  126.4 0.5 collective-permute-done.7.arrived_ref
  126.9 3.8 %collective-permute-start.8 = (bf16[2,112,256]{2,1,0:T(8,128)(2,1)S(1)}, bf16[2,112,256]{2,1,0:T(8,128)(2,1)S(1)}, u32[]{:S(2)}, u32[]{:S(2)}) collective-permute-start(bf16[2,112,256]{2,1,0:T(8,128)(2,1)S(1)} %get-tuple-element.20), channel_id=1, source_target_pairs={{0,2},{1,3},{2,0},{3,1},{4,6},{5,7},{6,4},{7,5},{8,10},{9,11},{10,... | collective-permute-start | bytes 344072 | tf_op jit(solution)/shard_map/ppermute | solution.py:41
  130.7 0.5 slice.3
  131.2 13.2 %collective-permute-done.11.arrived_ref = bf16[2,112,256]{2,1,0:T(8,128)(2,1)S(1)} collective-permute-done((bf16[2,112,256]{2,1,0:T(8,128)(2,1)S(1)}, bf16[2,112,256]{2,1,0:T(8,128)(2,1)S(1)}, u32[]{:S(2)}, u32[]{:S(2)}) %collective-permute-start.11) | collective-permute-done | bytes 114720 | tf_op jit(solution)/shard_map/ppermute | solution.py:41
  144.4 3.1 %collective-permute-start.12 = (bf16[112,256]{1,0:T(8,128)(2,1)S(1)}, bf16[112,256]{1,0:T(8,128)(2,1)S(1)}, u32[]{:S(2)}, u32[]{:S(2)}) collective-permute-start(bf16[112,256]{1,0:T(8,128)(2,1)S(1)} %get-tuple-element.27), channel_id=1, source_target_pairs={{0,4},{1,5},{2,6},{3,7},{4,0},{5,1},{6,2},{7,3},{8,12},{9,13},{10,... | collective-permute-start | bytes 172040 | tf_op jit(solution)/shard_map/ppermute | solution.py:41
  147.5 0.0 collective-permute-done.8.arrived_ref
  147.6 6.1 %collective-permute-start.9 = (bf16[112,256]{1,0:T(8,128)(2,1)S(1)}, bf16[112,256]{1,0:T(8,128)(2,1)S(1)}, u32[]{:S(2)}, u32[]{:S(2)}) collective-permute-start(bf16[112,256]{1,0:T(8,128)(2,1)S(1)} %get-tuple-element.22), channel_id=1, source_target_pairs={{0,4},{1,5},{2,6},{3,7},{4,0},{5,1},{6,2},{7,3},{8,12},{9,13},{10,... | collective-permute-start | bytes 172040 | tf_op jit(solution)/shard_map/ppermute | solution.py:41
  153.6 0.0 collective-permute-done.1.two_ref
  153.7 0.0 collective-permute-done.2.one_ref
  153.7 0.0 collective-permute-done.3.three_ref
  153.7 4.2 %hidden_gradient.1 = bf16[224,1024]{1,0:T(8,128)(2,1)} custom-call(s32[1]{0:T(128)} %bitcast.place_ref, s32[1]{0:T(128)} %bitcast.1.core_ref, bf16[2,224,256]{2,1,0:T(8,128)(2,1)S(1)} %pad_maximum_fusion.near_ref, bf16[2,224,256]{2,1,0:T(8,128)(2,1)S(1)} %collective-permute-done.1.two_ref, bf16[2,224,256]{2,1,0:T(8,128)(2,1)S(1)} %collective-permute-done.2.one_ref, ...), custom_call_target="tpu_custom_call" | custom-call | flops 939524096 | bytes 8388608 | tf_op jit(solution)/shard_map/hidden_gradient/pallas_call | solution.py:303
  157.9 0.0 collective-permute-done.12.two_ref
  157.9 0.3 collective-permute-done.9.one_ref
  158.2 0.7 add_last.1
  (6 shorter events, 0.2 us)
Async XLA Ops:
  1.8 18.2 %collective-permute-start.4 = (bf16[224,256]{1,0:T(8,128)(2,1)S(1)}, bf16[224,256]{1,0:T(8,128)(2,1)S(1)}, u32[]{:S(2)}, u32[]{:S(2)}) collective-permute-start(bf16[224,256]{1,0:T(8,128)(2,1)S(1)} %source.1), channel_id=1, source_target_pairs={{0,0},{1,64},{2,128},{3,192},{4,256},{5,320},{6,384},{7,448},{64,1... | collective-permute-start | bytes 344072 | tf_op jit(solution)/shard_map/ppermute | solution.py:41
  2.5 27.8 %collective-permute-start.5 = (bf16[224,256]{1,0:T(8,128)(2,1)S(1)}, bf16[224,256]{1,0:T(8,128)(2,1)S(1)}, u32[]{:S(2)}, u32[]{:S(2)}) collective-permute-start(bf16[224,256]{1,0:T(8,128)(2,1)S(1)} %source.1), channel_id=1, source_target_pairs={{0,64},{1,0},{2,192},{3,128},{4,320},{5,256},{6,448},{7,384},{64,6... | collective-permute-start | bytes 344072 | tf_op jit(solution)/shard_map/ppermute | solution.py:41
  72.4 20.5 %copy-start = (bf16[224,256]{1,0:T(8,128)(2,1)S(1)}, bf16[224,256]{1,0:T(8,128)(2,1)}, u32[]{:S(2)}) copy-start(bf16[224,256]{1,0:T(8,128)(2,1)} %param.7) | copy-start | bytes 344068
  72.4 31.0 %collective-permute-start.6 = (bf16[16,352,256]{2,1,0:T(8,128)(2,1)S(1)}, bf16[16,352,256]{2,1,0:T(8,128)(2,1)}, u32[]{:S(2)}, u32[]{:S(2)}) collective-permute-start(bf16[16,352,256]{2,1,0:T(8,128)(2,1)S(1)} %all_to_all.10), channel_id=1, source_target_pairs={{0,8},{8,0},{1,9},{9,1},{2,10},{10,2},{3,11},{11,3},{4,12},{12,4},... | collective-permute-start | bytes 8650760 | tf_op jit(solution)/shard_map/ppermute | solution.py:41
  77.9 25.5 %all-to-all-start.1 = ((f32[16,8,128]{2,1,0:T(8,128)}), f32[16,8,128]{2,1,0:T(8,128)S(1)}, u32[]{:S(2)}, u32[]{:S(2)}) async-start(f32[16,8,128]{2,1,0:T(8,128)} %plane_sums.1), calls=%async_computation.1 | async-start | bytes 131072 | tf_op jit(solution)/shard_map/all_to_all | solution.py:45
  92.9 19.6 %collective-permute-start = (bf16[1,224,256]{2,1,0:T(8,128)(2,1)S(1)}, bf16[1,224,256]{2,1,0:T(8,128)(2,1)S(1)}, u32[]{:S(2)}, u32[]{:S(2)}) collective-permute-start(bf16[1,224,256]{2,1,0:T(8,128)(2,1)S(1)} %bitcast.11), channel_id=1, source_target_pairs={{0,4},{1,5},{2,6},{3,7},{4,0},{5,1},{6,2},{7,3},{8,12},{9,13},{10,... | collective-permute-start | bytes 344072 | tf_op jit(solution)/shard_map/ppermute | solution.py:41
  106.9 17.5 %collective-permute-start.10 = (bf16[4,112,256]{2,1,0:T(8,128)(2,1)S(1)}, bf16[4,112,256]{2,1,0:T(8,128)(2,1)S(1)}, u32[]{:S(2)}, u32[]{:S(2)}) collective-permute-start(bf16[4,112,256]{2,1,0:T(8,128)(2,1)S(1)} %get-tuple-element.23), channel_id=1, source_target_pairs={{0,1},{1,0},{2,3},{3,2},{4,5},{5,4},{6,7},{7,6},{8,9},{9,8},{10,11... | collective-permute-start | bytes 688136 | tf_op jit(solution)/shard_map/ppermute | solution.py:41
  109.0 17.8 %collective-permute-start.7 = (bf16[4,112,256]{2,1,0:T(8,128)(2,1)S(1)}, bf16[4,112,256]{2,1,0:T(8,128)(2,1)S(1)}, u32[]{:S(2)}, u32[]{:S(2)}) collective-permute-start(bf16[4,112,256]{2,1,0:T(8,128)(2,1)S(1)} %get-tuple-element.18), channel_id=1, source_target_pairs={{0,1},{1,0},{2,3},{3,2},{4,5},{5,4},{6,7},{7,6},{8,9},{9,8},{10,11... | collective-permute-start | bytes 688136 | tf_op jit(solution)/shard_map/ppermute | solution.py:41
  112.6 41.0 %collective-permute-start.1 = (bf16[2,224,256]{2,1,0:T(8,128)(2,1)S(1)}, bf16[2,224,256]{2,1,0:T(8,128)(2,1)S(1)}, u32[]{:S(2)}, u32[]{:S(2)}) collective-permute-start(bf16[2,224,256]{2,1,0:T(8,128)(2,1)S(1)} %pad_maximum_fusion.near_ref), channel_id=1, source_target_pairs={{0,2},{1,3},{2,0},{3,1},{4,6},{5,7},{6,4},{7,5},{8,10},{9,11},{10,... | collective-permute-start | bytes 688136 | tf_op jit(solution)/shard_map/ppermute | solution.py:41
  114.5 39.1 %collective-permute-start.2 = (bf16[2,224,256]{2,1,0:T(8,128)(2,1)S(1)}, bf16[2,224,256]{2,1,0:T(8,128)(2,1)S(1)}, u32[]{:S(2)}, u32[]{:S(2)}) collective-permute-start(bf16[2,224,256]{2,1,0:T(8,128)(2,1)S(1)} %pad_maximum_fusion.near_ref), channel_id=1, source_target_pairs={{0,1},{1,0},{2,3},{3,2},{4,5},{5,4},{6,7},{7,6},{8,9},{9,8},{10,11... | collective-permute-start | bytes 688136 | tf_op jit(solution)/shard_map/ppermute | solution.py:41
  117.5 36.2 %collective-permute-start.3 = (bf16[2,224,256]{2,1,0:T(8,128)(2,1)S(1)}, bf16[2,224,256]{2,1,0:T(8,128)(2,1)S(1)}, u32[]{:S(2)}, u32[]{:S(2)}) collective-permute-start(bf16[2,224,256]{2,1,0:T(8,128)(2,1)S(1)} %pad_maximum_fusion.near_ref), channel_id=1, source_target_pairs={{0,3},{1,2},{2,1},{3,0},{4,7},{5,6},{6,5},{7,4},{8,11},{9,10},{10,... | collective-permute-start | bytes 688136 | tf_op jit(solution)/shard_map/ppermute | solution.py:41
  124.4 19.9 %collective-permute-start.11 = (bf16[2,112,256]{2,1,0:T(8,128)(2,1)S(1)}, bf16[2,112,256]{2,1,0:T(8,128)(2,1)S(1)}, u32[]{:S(2)}, u32[]{:S(2)}) collective-permute-start(bf16[2,112,256]{2,1,0:T(8,128)(2,1)S(1)} %get-tuple-element.25), channel_id=1, source_target_pairs={{0,2},{1,3},{2,0},{3,1},{4,6},{5,7},{6,4},{7,5},{8,10},{9,11},{10,... | collective-permute-start | bytes 344072 | tf_op jit(solution)/shard_map/ppermute | solution.py:41
  126.9 20.7 %collective-permute-start.8 = (bf16[2,112,256]{2,1,0:T(8,128)(2,1)S(1)}, bf16[2,112,256]{2,1,0:T(8,128)(2,1)S(1)}, u32[]{:S(2)}, u32[]{:S(2)}) collective-permute-start(bf16[2,112,256]{2,1,0:T(8,128)(2,1)S(1)} %get-tuple-element.20), channel_id=1, source_target_pairs={{0,2},{1,3},{2,0},{3,1},{4,6},{5,7},{6,4},{7,5},{8,10},{9,11},{10,... | collective-permute-start | bytes 344072 | tf_op jit(solution)/shard_map/ppermute | solution.py:41
  144.4 13.5 %collective-permute-start.12 = (bf16[112,256]{1,0:T(8,128)(2,1)S(1)}, bf16[112,256]{1,0:T(8,128)(2,1)S(1)}, u32[]{:S(2)}, u32[]{:S(2)}) collective-permute-start(bf16[112,256]{1,0:T(8,128)(2,1)S(1)} %get-tuple-element.27), channel_id=1, source_target_pairs={{0,4},{1,5},{2,6},{3,7},{4,0},{5,1},{6,2},{7,3},{8,12},{9,13},{10,... | collective-permute-start | bytes 172040 | tf_op jit(solution)/shard_map/ppermute | solution.py:41
  147.6 10.6 %collective-permute-start.9 = (bf16[112,256]{1,0:T(8,128)(2,1)S(1)}, bf16[112,256]{1,0:T(8,128)(2,1)S(1)}, u32[]{:S(2)}, u32[]{:S(2)}) collective-permute-start(bf16[112,256]{1,0:T(8,128)(2,1)S(1)} %get-tuple-element.22), channel_id=1, source_target_pairs={{0,4},{1,5},{2,6},{3,7},{4,0},{5,1},{6,2},{7,3},{8,12},{9,13},{10,... | collective-permute-start | bytes 172040 | tf_op jit(solution)/shard_map/ppermute | solution.py:41

commit v8 on v7

--- a/solution.py
+++ b/solution.py
@@ -16,7 +16,8 @@
 ROWS = 128
 WIDTH = 256
 HALF = ROWS // 2
-PACKED = HALF + HALF // 2
+PART = ROWS // 4
+PACKED = 2 * PART + PART // 2
 PIECE = ROWS + PACKED
 CHUNK = 2 * ROWS + PACKED
 PARAMS = pltpu.CompilerParams(vmem_limit_bytes=16 << 20)
@@ -70,24 +71,38 @@
     return pieces
 
 
+def lanes(rows):
+    return lax.broadcasted_iota(jnp.int32, (rows, ROWS), 1)
+
+
 def left(rows):
-    return lax.broadcasted_iota(jnp.int32, (rows, ROWS), 1) < HALF
+    return lanes(rows) < HALF
+
+
+def left_of_half(rows):
+    return lax.rem(lanes(rows), HALF) < PART
 
 
 def pack(values):
     top, bottom = values[:HALF], values[HALF:]
-    corner = jnp.where(
-        left(HALF // 2), pltpu.roll(top[: HALF // 2], HALF, 1), top[HALF // 2 :]
+    corner = jnp.where(left(PART), pltpu.roll(top[:PART], HALF, 1), top[PART:])
+    diagonal = jnp.where(left(HALF), top, bottom)
+    inner = jnp.where(left_of_half(PART), diagonal[:PART], diagonal[PART:])
+    half = PART // 2
+    outer = jnp.where(
+        left_of_half(half), pltpu.roll(diagonal[:half], ROWS - PART, 1), diagonal[half:PART]
     )
-    return jnp.concatenate([jnp.where(left(HALF), top, bottom), corner], axis=0)
+    return jnp.concatenate([inner, corner, outer], axis=0)
 
 
 def unpack(packed):
-    blocks, corner = packed[:HALF], packed[HALF:]
+    inner, corner, outer = packed[:PART], packed[PART : 2 * PART], packed[2 * PART :]
+    outer = jnp.concatenate([pltpu.roll(outer, PART, 1), outer], axis=0)
+    diagonal = jnp.concatenate([jnp.where(left_of_half(PART), inner, outer), inner], axis=0)
     right = jnp.concatenate([pltpu.roll(corner, HALF, 1), corner], axis=0)
-    upper = jnp.concatenate([jnp.where(left(HALF), blocks, right), blocks], axis=0)
-    below = lax.broadcasted_iota(jnp.int32, (ROWS, ROWS), 0) >= HALF
-    return jnp.where(jnp.logical_and(below, left(ROWS)), upper.T, upper)
+    upper = jnp.concatenate([jnp.where(left(HALF), diagonal, right), diagonal], axis=0)
+    rows = lax.broadcasted_iota(jnp.int32, (ROWS, ROWS), 0)
+    return jnp.where(lax.div(rows, PART) > lax.div(lanes(ROWS), PART), upper.T, upper)
 
 
 def two_parts(values):

time: 162 us -> 159 us (0.981)
  waiting for transfers between devices: 27.9 us -> 25 us
    ppermute x13, waiting for transfers between devices: 24.6 us -> 21.7 us  [permute(): return lax.ppermute(values, names, permutation(names, target))]
where the time goes in v8:
time: 159 us; the launch traced here: 156 us
  starting transfers between devices  74.7 us (47%)
  blocking collectives  41.7 us (26%)
  waiting for transfers between devices  25 us (16%)
  Pallas kernels  13.5 us (8%)
    ppermute x13, starting transfers between devices, permute(): return lax.ppermute(values, names, permutation(names, target))  59.5 us
    all_to_all x1, blocking collectives, exchange(): return lax.all_to_all(values, names, split_axis=0, concat_axis=0)  41.7 us
    ppermute x13, waiting for transfers between devices, permute(): return lax.ppermute(values, names, permutation(names, target))  21.7 us
    all_to_all x1, starting transfers between devices, exchange(): return lax.all_to_all(values, names, split_axis=0, concat_axis=0)  15.2 us
    pallas_call x1, Pallas kernels, hidden_gradient(): pl.pallas_call(hidden_kernel, in_specs=[SMEM] * 2 + [VMEM] * 6 + [HBM], o...  4.14 us
    pallas_call x1, Pallas kernels, mix(): pl.pallas_call(functools.partial(mix_kernel, scale), in_specs=[SMEM] * 2...  3.5 us
    all_to_all x1, waiting for transfers between devices, exchange(): return lax.all_to_all(values, names, split_axis=0, concat_axis=0)  3.27 us
  transfers between devices with their start and end apart: 14, of which 6 were waited for; matrix products, arithmetic and copies ran while one was open for 0% of the time, Pallas kernels for 7%

profile of v8, /device:TPU:1, one launch (start us, length us, event | category | flops | bytes accessed | tf_op | source)
XLA Modules:
  0.0 156.4 jit_solution(3094905476658601540)
XLA Ops:
  0.6 1.1 source.1
  1.8 0.7 collective-permute-start.4
  2.5 17.5 %collective-permute-start.5 = (bf16[208,256]{1,0:T(8,128)(2,1)S(1)}, bf16[208,256]{1,0:T(8,128)(2,1)S(1)}, u32[]{:S(2)}, u32[]{:S(2)}) collective-permute-start(bf16[208,256]{1,0:T(8,128)(2,1)S(1)} %source.1), channel_id=1, source_target_pairs={{0,64},{1,0},{2,192},{3,128},{4,320},{5,256},{6,448},{7,384},{64,6... | collective-permute-start | bytes 319496 | tf_op jit(solution)/shard_map/ppermute | solution.py:42
  20.0 0.0 collective-permute-done.4.first_ref
  20.0 7.3 %collective-permute-done.5.second_ref = bf16[208,256]{1,0:T(8,128)(2,1)S(1)} collective-permute-done((bf16[208,256]{1,0:T(8,128)(2,1)S(1)}, bf16[208,256]{1,0:T(8,128)(2,1)S(1)}, u32[]{:S(2)}, u32[]{:S(2)}) %collective-permute-start.5) | collective-permute-done | bytes 106528 | tf_op jit(solution)/shard_map/ppermute | solution.py:42
  27.3 0.2 broadcast_in_dim.10
  27.5 41.7 %all_to_all.10 = bf16[16,336,256]{2,1,0:T(8,128)(2,1)S(1)} all-to-all(bf16[16,336,256]{2,1,0:T(8,128)(2,1)S(1)} %broadcast_in_dim.10), channel_id=1, replica_groups=mesh['x'=4,'zh'=2,'y'=4,'c'=2,'t'=8] {'x','y'}, dimensions={0} | all-to-all | bytes 5505024 | tf_op jit(solution)/shard_map/all_to_all | solution.py:46
  69.2 0.0 copy-start
  69.2 4.6 %collective-permute-start.6 = (bf16[16,336,256]{2,1,0:T(8,128)(2,1)S(1)}, bf16[16,336,256]{2,1,0:T(8,128)(2,1)}, u32[]{:S(2)}, u32[]{:S(2)}) collective-permute-start(bf16[16,336,256]{2,1,0:T(8,128)(2,1)S(1)} %all_to_all.10), channel_id=1, source_target_pairs={{0,8},{8,0},{1,9},{9,1},{2,10},{10,2},{3,11},{11,3},{4,12},{12,4},... | collective-permute-start | bytes 8257544 | tf_op jit(solution)/shard_map/ppermute | solution.py:42
  73.8 1.4 plane_sums.1
  75.2 15.2 %all-to-all-start.1 = ((f32[16,8,128]{2,1,0:T(8,128)}), f32[16,8,128]{2,1,0:T(8,128)S(1)}, u32[]{:S(2)}, u32[]{:S(2)}) async-start(f32[16,8,128]{2,1,0:T(8,128)} %plane_sums.1), calls=%async_computation.1 | async-start | bytes 131072 | tf_op jit(solution)/shard_map/all_to_all | solution.py:46
  90.4 0.0 copy-done
  90.4 7.2 %collective-permute-start = (bf16[1,224,256]{2,1,0:T(8,128)(2,1)S(1)}, bf16[1,224,256]{2,1,0:T(8,128)(2,1)S(1)}, u32[]{:S(2)}, u32[]{:S(2)}) collective-permute-start(bf16[1,224,256]{2,1,0:T(8,128)(2,1)S(1)} %bitcast.11), channel_id=1, source_target_pairs={{0,4},{1,5},{2,6},{3,7},{4,0},{5,1},{6,2},{7,3},{8,12},{9,13},{10,... | collective-permute-start | bytes 344072 | tf_op jit(solution)/shard_map/ppermute | solution.py:42
  97.6 3.3 %all-to-all-done.1.tiles_ref = f32[16,8,128]{2,1,0:T(8,128)S(1)} async-done(((f32[16,8,128]{2,1,0:T(8,128)}), f32[16,8,128]{2,1,0:T(8,128)S(1)}, u32[]{:S(2)}, u32[]{:S(2)}) %all-to-all-start.1) | async-done | bytes 65568 | tf_op jit(solution)/shard_map/all_to_all | solution.py:46
  100.9 0.0 collective-permute-done.6
  100.9 3.5 %mix.1 = (f32[8,128,128]{2,1,0:T(8,128)S(1)}, bf16[224,1024]{1,0:T(8,128)(2,1)S(1)}, f32[8,128]{1,0:T(8,128)S(1)}, bf16[4,112,256]{2,1,0:T(8,128)(2,1)S(1)}, bf16[4,112,256]{2,1,0:T(8,128)(2,1)S(1)}) custom-call(s32[1]{0:T(128)} %bitcast.1.core_ref, s32[1]{0:T(128)} %bitcast.place_ref, f32[16,8,128]{2,1,0:T(8,128)S(1)} %all-to-all-done.1.tiles_ref, ...), custom_call_target="tpu_custom_call" | custom-call | tf_op jit(solution)/shard_map/mix/pallas_call | solution.py:225
  104.4 2.1 %collective-permute-start.10 = (bf16[4,112,256]{2,1,0:T(8,128)(2,1)S(1)}, bf16[4,112,256]{2,1,0:T(8,128)(2,1)S(1)}, u32[]{:S(2)}, u32[]{:S(2)}) collective-permute-start(bf16[4,112,256]{2,1,0:T(8,128)(2,1)S(1)} %get-tuple-element.23), channel_id=1, source_target_pairs={{0,1},{1,0},{2,3},{3,2},{4,5},{5,4},{6,7},{7,6},{8,9},{9,8},{10,11... | collective-permute-start | bytes 688136 | tf_op jit(solution)/shard_map/ppermute | solution.py:42
  106.5 3.2 %collective-permute-start.7 = (bf16[4,112,256]{2,1,0:T(8,128)(2,1)S(1)}, bf16[4,112,256]{2,1,0:T(8,128)(2,1)S(1)}, u32[]{:S(2)}, u32[]{:S(2)}) collective-permute-start(bf16[4,112,256]{2,1,0:T(8,128)(2,1)S(1)} %get-tuple-element.18), channel_id=1, source_target_pairs={{0,1},{1,0},{2,3},{3,2},{4,5},{5,4},{6,7},{7,6},{8,9},{9,8},{10,11... | collective-permute-start | bytes 688136 | tf_op jit(solution)/shard_map/ppermute | solution.py:42
  109.7 0.4 collective-permute-done
  110.1 1.9 %collective-permute-start.1 = (bf16[2,224,256]{2,1,0:T(8,128)(2,1)S(1)}, bf16[2,224,256]{2,1,0:T(8,128)(2,1)S(1)}, u32[]{:S(2)}, u32[]{:S(2)}) collective-permute-start(bf16[2,224,256]{2,1,0:T(8,128)(2,1)S(1)} %pad_maximum_fusion.near_ref), channel_id=1, source_target_pairs={{0,2},{1,3},{2,0},{3,1},{4,6},{5,7},{6,4},{7,5},{8,10},{9,11},{10,... | collective-permute-start | bytes 688136 | tf_op jit(solution)/shard_map/ppermute | solution.py:42
  112.0 3.0 %collective-permute-start.2 = (bf16[2,224,256]{2,1,0:T(8,128)(2,1)S(1)}, bf16[2,224,256]{2,1,0:T(8,128)(2,1)S(1)}, u32[]{:S(2)}, u32[]{:S(2)}) collective-permute-start(bf16[2,224,256]{2,1,0:T(8,128)(2,1)S(1)} %pad_maximum_fusion.near_ref), channel_id=1, source_target_pairs={{0,1},{1,0},{2,3},{3,2},{4,5},{5,4},{6,7},{7,6},{8,9},{9,8},{10,11... | collective-permute-start | bytes 688136 | tf_op jit(solution)/shard_map/ppermute | solution.py:42
  115.0 4.4 %collective-permute-start.3 = (bf16[2,224,256]{2,1,0:T(8,128)(2,1)S(1)}, bf16[2,224,256]{2,1,0:T(8,128)(2,1)S(1)}, u32[]{:S(2)}, u32[]{:S(2)}) collective-permute-start(bf16[2,224,256]{2,1,0:T(8,128)(2,1)S(1)} %pad_maximum_fusion.near_ref), channel_id=1, source_target_pairs={{0,3},{1,2},{2,1},{3,0},{4,7},{5,6},{6,5},{7,4},{8,11},{9,10},{10,... | collective-permute-start | bytes 688136 | tf_op jit(solution)/shard_map/ppermute | solution.py:42
  119.4 2.4 %weight_parts.1.kept_ref = f32[4,224,256]{2,1,0:T(8,128)S(1)} custom-call(s32[1]{0:T(128)} %bitcast.place_ref, bf16[224,1024]{1,0:T(8,128)(2,1)S(1)} %get-tuple-element.17.product_ref, bf16[4,4,336,256]{3,2,1,0:T(8,128)(2,1)S(1)} %bitcast.9, bf16[4,4,336,256]{3,2,1,0:T(8,128)(2,1)} %bitcast.5.other_hbm.other_ref), custom_call_target="tpu_custom_call" | custom-call | flops 469762048 | bytes 4194304 | tf_op jit(solution)/shard_map/weight_parts/pallas_call | solution.py:271
  121.9 0.0 collective-permute-done.10.arrived_ref
  121.9 1.9 %collective-permute-start.11 = (bf16[2,112,256]{2,1,0:T(8,128)(2,1)S(1)}, bf16[2,112,256]{2,1,0:T(8,128)(2,1)S(1)}, u32[]{:S(2)}, u32[]{:S(2)}) collective-permute-start(bf16[2,112,256]{2,1,0:T(8,128)(2,1)S(1)} %get-tuple-element.25), channel_id=1, source_target_pairs={{0,2},{1,3},{2,0},{3,1},{4,6},{5,7},{6,4},{7,5},{8,10},{9,11},{10,... | collective-permute-start | bytes 344072 | tf_op jit(solution)/shard_map/ppermute | solution.py:42
  123.8 0.5 collective-permute-done.7.arrived_ref
  124.3 0.1 shard_map.67
  124.4 3.8 %collective-permute-start.8 = (bf16[2,112,256]{2,1,0:T(8,128)(2,1)S(1)}, bf16[2,112,256]{2,1,0:T(8,128)(2,1)S(1)}, u32[]{:S(2)}, u32[]{:S(2)}) collective-permute-start(bf16[2,112,256]{2,1,0:T(8,128)(2,1)S(1)} %get-tuple-element.20), channel_id=1, source_target_pairs={{0,2},{1,3},{2,0},{3,1},{4,6},{5,7},{6,4},{7,5},{8,10},{9,11},{10,... | collective-permute-start | bytes 344072 | tf_op jit(solution)/shard_map/ppermute | solution.py:42
  128.2 0.5 slice.3
  128.7 13.2 %collective-permute-done.11.arrived_ref = bf16[2,112,256]{2,1,0:T(8,128)(2,1)S(1)} collective-permute-done((bf16[2,112,256]{2,1,0:T(8,128)(2,1)S(1)}, bf16[2,112,256]{2,1,0:T(8,128)(2,1)S(1)}, u32[]{:S(2)}, u32[]{:S(2)}) %collective-permute-start.11) | collective-permute-done | bytes 114720 | tf_op jit(solution)/shard_map/ppermute | solution.py:42
  141.9 3.1 %collective-permute-start.12 = (bf16[112,256]{1,0:T(8,128)(2,1)S(1)}, bf16[112,256]{1,0:T(8,128)(2,1)S(1)}, u32[]{:S(2)}, u32[]{:S(2)}) collective-permute-start(bf16[112,256]{1,0:T(8,128)(2,1)S(1)} %get-tuple-element.27), channel_id=1, source_target_pairs={{0,4},{1,5},{2,6},{3,7},{4,0},{5,1},{6,2},{7,3},{8,12},{9,13},{10,... | collective-permute-start | bytes 172040 | tf_op jit(solution)/shard_map/ppermute | solution.py:42
  145.0 0.0 collective-permute-done.8.arrived_ref
  145.1 6.1 %collective-permute-start.9 = (bf16[112,256]{1,0:T(8,128)(2,1)S(1)}, bf16[112,256]{1,0:T(8,128)(2,1)S(1)}, u32[]{:S(2)}, u32[]{:S(2)}) collective-permute-start(bf16[112,256]{1,0:T(8,128)(2,1)S(1)} %get-tuple-element.22), channel_id=1, source_target_pairs={{0,4},{1,5},{2,6},{3,7},{4,0},{5,1},{6,2},{7,3},{8,12},{9,13},{10,... | collective-permute-start | bytes 172040 | tf_op jit(solution)/shard_map/ppermute | solution.py:42
  151.1 0.0 collective-permute-done.1.two_ref
  151.1 0.0 collective-permute-done.2.one_ref
  151.2 0.0 collective-permute-done.3.three_ref
  151.2 4.1 %hidden_gradient.1 = bf16[224,1024]{1,0:T(8,128)(2,1)} custom-call(s32[1]{0:T(128)} %bitcast.place_ref, s32[1]{0:T(128)} %bitcast.1.core_ref, bf16[2,224,256]{2,1,0:T(8,128)(2,1)S(1)} %pad_maximum_fusion.near_ref, bf16[2,224,256]{2,1,0:T(8,128)(2,1)S(1)} %collective-permute-done.1.two_ref, bf16[2,224,256]{2,1,0:T(8,128)(2,1)S(1)} %collective-permute-done.2.one_ref, ...), custom_call_target="tpu_custom_call" | custom-call | flops 939524096 | bytes 8388608 | tf_op jit(solution)/shard_map/hidden_gradient/pallas_call | solution.py:318
  155.3 0.0 collective-permute-done.12.two_ref
  155.3 0.4 collective-permute-done.9.one_ref
  155.7 0.7 add_last.1
  (5 shorter events, 0.1 us)
Async XLA Ops:
  1.8 18.2 %collective-permute-start.4 = (bf16[208,256]{1,0:T(8,128)(2,1)S(1)}, bf16[208,256]{1,0:T(8,128)(2,1)S(1)}, u32[]{:S(2)}, u32[]{:S(2)}) collective-permute-start(bf16[208,256]{1,0:T(8,128)(2,1)S(1)} %source.1), channel_id=1, source_target_pairs={{0,0},{1,64},{2,128},{3,192},{4,256},{5,320},{6,384},{7,448},{64,1... | collective-permute-start | bytes 319496 | tf_op jit(solution)/shard_map/ppermute | solution.py:42
  2.5 24.8 %collective-permute-start.5 = (bf16[208,256]{1,0:T(8,128)(2,1)S(1)}, bf16[208,256]{1,0:T(8,128)(2,1)S(1)}, u32[]{:S(2)}, u32[]{:S(2)}) collective-permute-start(bf16[208,256]{1,0:T(8,128)(2,1)S(1)} %source.1), channel_id=1, source_target_pairs={{0,64},{1,0},{2,192},{3,128},{4,320},{5,256},{6,448},{7,384},{64,6... | collective-permute-start | bytes 319496 | tf_op jit(solution)/shard_map/ppermute | solution.py:42
  69.2 21.3 %copy-start = (bf16[224,256]{1,0:T(8,128)(2,1)S(1)}, bf16[224,256]{1,0:T(8,128)(2,1)}, u32[]{:S(2)}) copy-start(bf16[224,256]{1,0:T(8,128)(2,1)} %param.7) | copy-start | bytes 344068
  69.2 31.7 %collective-permute-start.6 = (bf16[16,336,256]{2,1,0:T(8,128)(2,1)S(1)}, bf16[16,336,256]{2,1,0:T(8,128)(2,1)}, u32[]{:S(2)}, u32[]{:S(2)}) collective-permute-start(bf16[16,336,256]{2,1,0:T(8,128)(2,1)S(1)} %all_to_all.10), channel_id=1, source_target_pairs={{0,8},{8,0},{1,9},{9,1},{2,10},{10,2},{3,11},{11,3},{4,12},{12,4},... | collective-permute-start | bytes 8257544 | tf_op jit(solution)/shard_map/ppermute | solution.py:42
  75.2 25.7 %all-to-all-start.1 = ((f32[16,8,128]{2,1,0:T(8,128)}), f32[16,8,128]{2,1,0:T(8,128)S(1)}, u32[]{:S(2)}, u32[]{:S(2)}) async-start(f32[16,8,128]{2,1,0:T(8,128)} %plane_sums.1), calls=%async_computation.1 | async-start | bytes 131072 | tf_op jit(solution)/shard_map/all_to_all | solution.py:46
  90.4 19.6 %collective-permute-start = (bf16[1,224,256]{2,1,0:T(8,128)(2,1)S(1)}, bf16[1,224,256]{2,1,0:T(8,128)(2,1)S(1)}, u32[]{:S(2)}, u32[]{:S(2)}) collective-permute-start(bf16[1,224,256]{2,1,0:T(8,128)(2,1)S(1)} %bitcast.11), channel_id=1, source_target_pairs={{0,4},{1,5},{2,6},{3,7},{4,0},{5,1},{6,2},{7,3},{8,12},{9,13},{10,... | collective-permute-start | bytes 344072 | tf_op jit(solution)/shard_map/ppermute | solution.py:42
  104.4 17.5 %collective-permute-start.10 = (bf16[4,112,256]{2,1,0:T(8,128)(2,1)S(1)}, bf16[4,112,256]{2,1,0:T(8,128)(2,1)S(1)}, u32[]{:S(2)}, u32[]{:S(2)}) collective-permute-start(bf16[4,112,256]{2,1,0:T(8,128)(2,1)S(1)} %get-tuple-element.23), channel_id=1, source_target_pairs={{0,1},{1,0},{2,3},{3,2},{4,5},{5,4},{6,7},{7,6},{8,9},{9,8},{10,11... | collective-permute-start | bytes 688136 | tf_op jit(solution)/shard_map/ppermute | solution.py:42
  106.5 17.8 %collective-permute-start.7 = (bf16[4,112,256]{2,1,0:T(8,128)(2,1)S(1)}, bf16[4,112,256]{2,1,0:T(8,128)(2,1)S(1)}, u32[]{:S(2)}, u32[]{:S(2)}) collective-permute-start(bf16[4,112,256]{2,1,0:T(8,128)(2,1)S(1)} %get-tuple-element.18), channel_id=1, source_target_pairs={{0,1},{1,0},{2,3},{3,2},{4,5},{5,4},{6,7},{7,6},{8,9},{9,8},{10,11... | collective-permute-start | bytes 688136 | tf_op jit(solution)/shard_map/ppermute | solution.py:42
  110.1 41.0 %collective-permute-start.1 = (bf16[2,224,256]{2,1,0:T(8,128)(2,1)S(1)}, bf16[2,224,256]{2,1,0:T(8,128)(2,1)S(1)}, u32[]{:S(2)}, u32[]{:S(2)}) collective-permute-start(bf16[2,224,256]{2,1,0:T(8,128)(2,1)S(1)} %pad_maximum_fusion.near_ref), channel_id=1, source_target_pairs={{0,2},{1,3},{2,0},{3,1},{4,6},{5,7},{6,4},{7,5},{8,10},{9,11},{10,... | collective-permute-start | bytes 688136 | tf_op jit(solution)/shard_map/ppermute | solution.py:42
  112.0 39.1 %collective-permute-start.2 = (bf16[2,224,256]{2,1,0:T(8,128)(2,1)S(1)}, bf16[2,224,256]{2,1,0:T(8,128)(2,1)S(1)}, u32[]{:S(2)}, u32[]{:S(2)}) collective-permute-start(bf16[2,224,256]{2,1,0:T(8,128)(2,1)S(1)} %pad_maximum_fusion.near_ref), channel_id=1, source_target_pairs={{0,1},{1,0},{2,3},{3,2},{4,5},{5,4},{6,7},{7,6},{8,9},{9,8},{10,11... | collective-permute-start | bytes 688136 | tf_op jit(solution)/shard_map/ppermute | solution.py:42
  115.0 36.1 %collective-permute-start.3 = (bf16[2,224,256]{2,1,0:T(8,128)(2,1)S(1)}, bf16[2,224,256]{2,1,0:T(8,128)(2,1)S(1)}, u32[]{:S(2)}, u32[]{:S(2)}) collective-permute-start(bf16[2,224,256]{2,1,0:T(8,128)(2,1)S(1)} %pad_maximum_fusion.near_ref), channel_id=1, source_target_pairs={{0,3},{1,2},{2,1},{3,0},{4,7},{5,6},{6,5},{7,4},{8,11},{9,10},{10,... | collective-permute-start | bytes 688136 | tf_op jit(solution)/shard_map/ppermute | solution.py:42
  121.9 19.9 %collective-permute-start.11 = (bf16[2,112,256]{2,1,0:T(8,128)(2,1)S(1)}, bf16[2,112,256]{2,1,0:T(8,128)(2,1)S(1)}, u32[]{:S(2)}, u32[]{:S(2)}) collective-permute-start(bf16[2,112,256]{2,1,0:T(8,128)(2,1)S(1)} %get-tuple-element.25), channel_id=1, source_target_pairs={{0,2},{1,3},{2,0},{3,1},{4,6},{5,7},{6,4},{7,5},{8,10},{9,11},{10,... | collective-permute-start | bytes 344072 | tf_op jit(solution)/shard_map/ppermute | solution.py:42
  124.4 20.6 %collective-permute-start.8 = (bf16[2,112,256]{2,1,0:T(8,128)(2,1)S(1)}, bf16[2,112,256]{2,1,0:T(8,128)(2,1)S(1)}, u32[]{:S(2)}, u32[]{:S(2)}) collective-permute-start(bf16[2,112,256]{2,1,0:T(8,128)(2,1)S(1)} %get-tuple-element.20), channel_id=1, source_target_pairs={{0,2},{1,3},{2,0},{3,1},{4,6},{5,7},{6,4},{7,5},{8,10},{9,11},{10,... | collective-permute-start | bytes 344072 | tf_op jit(solution)/shard_map/ppermute | solution.py:42
  141.9 13.4 %collective-permute-start.12 = (bf16[112,256]{1,0:T(8,128)(2,1)S(1)}, bf16[112,256]{1,0:T(8,128)(2,1)S(1)}, u32[]{:S(2)}, u32[]{:S(2)}) collective-permute-start(bf16[112,256]{1,0:T(8,128)(2,1)S(1)} %get-tuple-element.27), channel_id=1, source_target_pairs={{0,4},{1,5},{2,6},{3,7},{4,0},{5,1},{6,2},{7,3},{8,12},{9,13},{10,... | collective-permute-start | bytes 172040 | tf_op jit(solution)/shard_map/ppermute | solution.py:42
  145.1 10.6 %collective-permute-start.9 = (bf16[112,256]{1,0:T(8,128)(2,1)S(1)}, bf16[112,256]{1,0:T(8,128)(2,1)S(1)}, u32[]{:S(2)}, u32[]{:S(2)}) collective-permute-start(bf16[112,256]{1,0:T(8,128)(2,1)S(1)} %get-tuple-element.22), channel_id=1, source_target_pairs={{0,4},{1,5},{2,6},{3,7},{4,0},{5,1},{6,2},{7,3},{8,12},{9,13},{10,... | collective-permute-start | bytes 172040 | tf_op jit(solution)/shard_map/ppermute | solution.py:42

commit v9 on v8

--- a/solution.py
+++ b/solution.py
@@ -190,7 +190,7 @@
     root = jnp.sqrt(sxx * syy)
     ratio = jnp.broadcast_to(sxy / sxx, (1, ROWS))
     coef = jnp.broadcast_to(-2.0 * scale / root, (1, ROWS))
-    cka_ref[...] = jnp.broadcast_to(sxy / root, cka_ref.shape)
+    cka_ref[...] = sxy / root
     core = core_ref[0]
 
     def mix_pair(ref, base, first):
@@ -229,7 +229,7 @@
         out_shape=[
             jax.ShapeDtypeStruct((8, ROWS, ROWS), F32),
             jax.ShapeDtypeStruct(hidden.shape, BF16),
-            jax.ShapeDtypeStruct((8, ROWS), F32),
+            jax.ShapeDtypeStruct((1, 1), F32),
             half,
             half,
         ],
@@ -440,7 +440,7 @@
         last[name] = permute(moved, ("t",), flip(4))
     grad_weight = add_last(halves["a"], last["a"], halves["b"], last["b"])
     grad_hidden = hidden_gradient(place, core, weights, plane, other, mixed)
-    return (grad_hidden, grad_weight, cka[0, 0])
+    return (grad_hidden, grad_weight, cka.reshape(()))
 
 
 def solution(mesh):

time: 159 us -> 159 us (level)
  transfers between devices with their start and end apart: 14 -> 14, of which waited for: 6 -> 6; matrix products, arithmetic and copies ran while one was open for 0% -> 0% of each run, Pallas kernels for 7% -> 8%
where the time goes in v9:
time: 159 us; the launch traced here: 156 us
  starting transfers between devices  74.7 us (47%)
  blocking collectives  41.7 us (26%)
  waiting for transfers between devices  25.2 us (16%)
  Pallas kernels  13.9 us (9%)
    ppermute x13, starting transfers between devices, permute(): return lax.ppermute(values, names, permutation(names, target))  59.5 us
    all_to_all x1, blocking collectives, exchange(): return lax.all_to_all(values, names, split_axis=0, concat_axis=0)  41.7 us
    ppermute x13, waiting for transfers between devices, permute(): return lax.ppermute(values, names, permutation(names, target))  21.9 us
    all_to_all x1, starting transfers between devices, exchange(): return lax.all_to_all(values, names, split_axis=0, concat_axis=0)  15.2 us
    pallas_call x1, Pallas kernels, hidden_gradient(): pl.pallas_call(hidden_kernel, in_specs=[SMEM] * 2 + [VMEM] * 6 + [HBM], o...  4.14 us
    pallas_call x1, Pallas kernels, mix(): pl.pallas_call(functools.partial(mix_kernel, scale), in_specs=[SMEM] * 2...  3.83 us
    all_to_all x1, waiting for transfers between devices, exchange(): return lax.all_to_all(values, names, split_axis=0, concat_axis=0)  3.27 us
  transfers between devices with their start and end apart: 14, of which 6 were waited for; matrix products, arithmetic and copies ran while one was open for 0% of the time, Pallas kernels for 8%

profile of v9, /device:TPU:1, one launch (start us, length us, event | category | flops | bytes accessed | tf_op | source)
XLA Modules:
  0.0 156.4 jit_solution(15194766160556897331)
XLA Ops:
  0.6 1.1 source.1
  1.8 0.7 collective-permute-start.4
  2.5 17.5 %collective-permute-start.5 = (bf16[208,256]{1,0:T(8,128)(2,1)S(1)}, bf16[208,256]{1,0:T(8,128)(2,1)S(1)}, u32[]{:S(2)}, u32[]{:S(2)}) collective-permute-start(bf16[208,256]{1,0:T(8,128)(2,1)S(1)} %source.1), channel_id=1, source_target_pairs={{0,64},{1,0},{2,192},{3,128},{4,320},{5,256},{6,448},{7,384},{64,6... | collective-permute-start | bytes 319496 | tf_op jit(solution)/shard_map/ppermute | solution.py:42
  20.0 0.0 collective-permute-done.4.first_ref
  20.0 7.3 %collective-permute-done.5.second_ref = bf16[208,256]{1,0:T(8,128)(2,1)S(1)} collective-permute-done((bf16[208,256]{1,0:T(8,128)(2,1)S(1)}, bf16[208,256]{1,0:T(8,128)(2,1)S(1)}, u32[]{:S(2)}, u32[]{:S(2)}) %collective-permute-start.5) | collective-permute-done | bytes 106528 | tf_op jit(solution)/shard_map/ppermute | solution.py:42
  27.3 0.2 broadcast_in_dim.10
  27.5 41.7 %all_to_all.10 = bf16[16,336,256]{2,1,0:T(8,128)(2,1)S(1)} all-to-all(bf16[16,336,256]{2,1,0:T(8,128)(2,1)S(1)} %broadcast_in_dim.10), channel_id=1, replica_groups=mesh['x'=4,'zh'=2,'y'=4,'c'=2,'t'=8] {'x','y'}, dimensions={0} | all-to-all | bytes 5505024 | tf_op jit(solution)/shard_map/all_to_all | solution.py:46
  69.2 0.0 copy-start
  69.2 4.6 %collective-permute-start.6 = (bf16[16,336,256]{2,1,0:T(8,128)(2,1)S(1)}, bf16[16,336,256]{2,1,0:T(8,128)(2,1)}, u32[]{:S(2)}, u32[]{:S(2)}) collective-permute-start(bf16[16,336,256]{2,1,0:T(8,128)(2,1)S(1)} %all_to_all.10), channel_id=1, source_target_pairs={{0,8},{8,0},{1,9},{9,1},{2,10},{10,2},{3,11},{11,3},{4,12},{12,4},... | collective-permute-start | bytes 8257544 | tf_op jit(solution)/shard_map/ppermute | solution.py:42
  73.8 1.4 plane_sums.1
  75.2 15.2 %all-to-all-start.1 = ((f32[16,8,128]{2,1,0:T(8,128)}), f32[16,8,128]{2,1,0:T(8,128)S(1)}, u32[]{:S(2)}, u32[]{:S(2)}) async-start(f32[16,8,128]{2,1,0:T(8,128)} %plane_sums.1), calls=%async_computation.1 | async-start | bytes 131072 | tf_op jit(solution)/shard_map/all_to_all | solution.py:46
  90.4 0.0 copy-done
  90.4 7.2 %collective-permute-start = (bf16[1,224,256]{2,1,0:T(8,128)(2,1)S(1)}, bf16[1,224,256]{2,1,0:T(8,128)(2,1)S(1)}, u32[]{:S(2)}, u32[]{:S(2)}) collective-permute-start(bf16[1,224,256]{2,1,0:T(8,128)(2,1)S(1)} %bitcast.11), channel_id=1, source_target_pairs={{0,4},{1,5},{2,6},{3,7},{4,0},{5,1},{6,2},{7,3},{8,12},{9,13},{10,... | collective-permute-start | bytes 344072 | tf_op jit(solution)/shard_map/ppermute | solution.py:42
  97.6 3.3 %all-to-all-done.1.tiles_ref = f32[16,8,128]{2,1,0:T(8,128)S(1)} async-done(((f32[16,8,128]{2,1,0:T(8,128)}), f32[16,8,128]{2,1,0:T(8,128)S(1)}, u32[]{:S(2)}, u32[]{:S(2)}) %all-to-all-start.1) | async-done | bytes 65568 | tf_op jit(solution)/shard_map/all_to_all | solution.py:46
  100.9 0.0 collective-permute-done.6
  100.9 3.8 %mix.1 = (f32[8,128,128]{2,1,0:T(8,128)S(1)}, bf16[224,1024]{1,0:T(8,128)(2,1)S(1)}, f32[1,1]{1,0:T(1,128)}, bf16[4,112,256]{2,1,0:T(8,128)(2,1)S(1)}, bf16[4,112,256]{2,1,0:T(8,128)(2,1)S(1)}) custom-call(s32[1]{0:T(128)} %bitcast.1.core_ref, s32[1]{0:T(128)} %bitcast.place_ref, f32[16,8,128]{2,1,0:T(8,128)S(1)} %all-to-all-done.1.tiles_ref, ...), custom_call_target="tpu_custom_call" | custom-call | tf_op jit(solution)/shard_map/mix/pallas_call | solution.py:225
  104.7 2.1 %collective-permute-start.10 = (bf16[4,112,256]{2,1,0:T(8,128)(2,1)S(1)}, bf16[4,112,256]{2,1,0:T(8,128)(2,1)S(1)}, u32[]{:S(2)}, u32[]{:S(2)}) collective-permute-start(bf16[4,112,256]{2,1,0:T(8,128)(2,1)S(1)} %get-tuple-element.23), channel_id=1, source_target_pairs={{0,1},{1,0},{2,3},{3,2},{4,5},{5,4},{6,7},{7,6},{8,9},{9,8},{10,11... | collective-permute-start | bytes 688136 | tf_op jit(solution)/shard_map/ppermute | solution.py:42
  106.8 3.2 %collective-permute-start.7 = (bf16[4,112,256]{2,1,0:T(8,128)(2,1)S(1)}, bf16[4,112,256]{2,1,0:T(8,128)(2,1)S(1)}, u32[]{:S(2)}, u32[]{:S(2)}) collective-permute-start(bf16[4,112,256]{2,1,0:T(8,128)(2,1)S(1)} %get-tuple-element.18), channel_id=1, source_target_pairs={{0,1},{1,0},{2,3},{3,2},{4,5},{5,4},{6,7},{7,6},{8,9},{9,8},{10,11... | collective-permute-start | bytes 688136 | tf_op jit(solution)/shard_map/ppermute | solution.py:42
  110.0 0.1 collective-permute-done
  110.1 1.9 %collective-permute-start.1 = (bf16[2,224,256]{2,1,0:T(8,128)(2,1)S(1)}, bf16[2,224,256]{2,1,0:T(8,128)(2,1)S(1)}, u32[]{:S(2)}, u32[]{:S(2)}) collective-permute-start(bf16[2,224,256]{2,1,0:T(8,128)(2,1)S(1)} %pad_maximum_fusion.near_ref), channel_id=1, source_target_pairs={{0,2},{1,3},{2,0},{3,1},{4,6},{5,7},{6,4},{7,5},{8,10},{9,11},{10,... | collective-permute-start | bytes 688136 | tf_op jit(solution)/shard_map/ppermute | solution.py:42
  112.0 3.0 %collective-permute-start.2 = (bf16[2,224,256]{2,1,0:T(8,128)(2,1)S(1)}, bf16[2,224,256]{2,1,0:T(8,128)(2,1)S(1)}, u32[]{:S(2)}, u32[]{:S(2)}) collective-permute-start(bf16[2,224,256]{2,1,0:T(8,128)(2,1)S(1)} %pad_maximum_fusion.near_ref), channel_id=1, source_target_pairs={{0,1},{1,0},{2,3},{3,2},{4,5},{5,4},{6,7},{7,6},{8,9},{9,8},{10,11... | collective-permute-start | bytes 688136 | tf_op jit(solution)/shard_map/ppermute | solution.py:42
  115.0 4.4 %collective-permute-start.3 = (bf16[2,224,256]{2,1,0:T(8,128)(2,1)S(1)}, bf16[2,224,256]{2,1,0:T(8,128)(2,1)S(1)}, u32[]{:S(2)}, u32[]{:S(2)}) collective-permute-start(bf16[2,224,256]{2,1,0:T(8,128)(2,1)S(1)} %pad_maximum_fusion.near_ref), channel_id=1, source_target_pairs={{0,3},{1,2},{2,1},{3,0},{4,7},{5,6},{6,5},{7,4},{8,11},{9,10},{10,... | collective-permute-start | bytes 688136 | tf_op jit(solution)/shard_map/ppermute | solution.py:42
  119.4 2.4 %weight_parts.1.kept_ref = f32[4,224,256]{2,1,0:T(8,128)S(1)} custom-call(s32[1]{0:T(128)} %bitcast.place_ref, bf16[224,1024]{1,0:T(8,128)(2,1)S(1)} %get-tuple-element.17.product_ref, bf16[4,4,336,256]{3,2,1,0:T(8,128)(2,1)S(1)} %bitcast.9, bf16[4,4,336,256]{3,2,1,0:T(8,128)(2,1)} %bitcast.5.other_hbm.other_ref), custom_call_target="tpu_custom_call" | custom-call | flops 469762048 | bytes 4194304 | tf_op jit(solution)/shard_map/weight_parts/pallas_call | solution.py:271
  121.9 0.0 collective-permute-done.10.arrived_ref
  121.9 1.9 %collective-permute-start.11 = (bf16[2,112,256]{2,1,0:T(8,128)(2,1)S(1)}, bf16[2,112,256]{2,1,0:T(8,128)(2,1)S(1)}, u32[]{:S(2)}, u32[]{:S(2)}) collective-permute-start(bf16[2,112,256]{2,1,0:T(8,128)(2,1)S(1)} %get-tuple-element.25), channel_id=1, source_target_pairs={{0,2},{1,3},{2,0},{3,1},{4,6},{5,7},{6,4},{7,5},{8,10},{9,11},{10,... | collective-permute-start | bytes 344072 | tf_op jit(solution)/shard_map/ppermute | solution.py:42
  123.8 0.5 collective-permute-done.7.arrived_ref
  124.3 0.1 shard_map.67
  124.4 3.8 %collective-permute-start.8 = (bf16[2,112,256]{2,1,0:T(8,128)(2,1)S(1)}, bf16[2,112,256]{2,1,0:T(8,128)(2,1)S(1)}, u32[]{:S(2)}, u32[]{:S(2)}) collective-permute-start(bf16[2,112,256]{2,1,0:T(8,128)(2,1)S(1)} %get-tuple-element.20), channel_id=1, source_target_pairs={{0,2},{1,3},{2,0},{3,1},{4,6},{5,7},{6,4},{7,5},{8,10},{9,11},{10,... | collective-permute-start | bytes 344072 | tf_op jit(solution)/shard_map/ppermute | solution.py:42
  128.2 13.7 %collective-permute-done.11.arrived_ref = bf16[2,112,256]{2,1,0:T(8,128)(2,1)S(1)} collective-permute-done((bf16[2,112,256]{2,1,0:T(8,128)(2,1)S(1)}, bf16[2,112,256]{2,1,0:T(8,128)(2,1)S(1)}, u32[]{:S(2)}, u32[]{:S(2)}) %collective-permute-start.11) | collective-permute-done | bytes 114720 | tf_op jit(solution)/shard_map/ppermute | solution.py:42
  141.9 3.1 %collective-permute-start.12 = (bf16[112,256]{1,0:T(8,128)(2,1)S(1)}, bf16[112,256]{1,0:T(8,128)(2,1)S(1)}, u32[]{:S(2)}, u32[]{:S(2)}) collective-permute-start(bf16[112,256]{1,0:T(8,128)(2,1)S(1)} %get-tuple-element.27), channel_id=1, source_target_pairs={{0,4},{1,5},{2,6},{3,7},{4,0},{5,1},{6,2},{7,3},{8,12},{9,13},{10,... | collective-permute-start | bytes 172040 | tf_op jit(solution)/shard_map/ppermute | solution.py:42
  145.0 0.0 collective-permute-done.8.arrived_ref
  145.1 6.1 %collective-permute-start.9 = (bf16[112,256]{1,0:T(8,128)(2,1)S(1)}, bf16[112,256]{1,0:T(8,128)(2,1)S(1)}, u32[]{:S(2)}, u32[]{:S(2)}) collective-permute-start(bf16[112,256]{1,0:T(8,128)(2,1)S(1)} %get-tuple-element.22), channel_id=1, source_target_pairs={{0,4},{1,5},{2,6},{3,7},{4,0},{5,1},{6,2},{7,3},{8,12},{9,13},{10,... | collective-permute-start | bytes 172040 | tf_op jit(solution)/shard_map/ppermute | solution.py:42
  151.1 0.0 collective-permute-done.1.two_ref
  151.1 0.0 collective-permute-done.2.one_ref
  151.2 0.0 collective-permute-done.3.three_ref
  151.2 4.1 %hidden_gradient.1 = bf16[224,1024]{1,0:T(8,128)(2,1)} custom-call(s32[1]{0:T(128)} %bitcast.place_ref, s32[1]{0:T(128)} %bitcast.1.core_ref, bf16[2,224,256]{2,1,0:T(8,128)(2,1)S(1)} %pad_maximum_fusion.near_ref, bf16[2,224,256]{2,1,0:T(8,128)(2,1)S(1)} %collective-permute-done.1.two_ref, bf16[2,224,256]{2,1,0:T(8,128)(2,1)S(1)} %collective-permute-done.2.one_ref, ...), custom_call_target="tpu_custom_call" | custom-call | flops 939524096 | bytes 8388608 | tf_op jit(solution)/shard_map/hidden_gradient/pallas_call | solution.py:318
  155.3 0.0 collective-permute-done.12.two_ref
  155.3 0.4 collective-permute-done.9.one_ref
  155.7 0.7 add_last.1
  (5 shorter events, 0.1 us)
Async XLA Ops:
  1.8 18.2 %collective-permute-start.4 = (bf16[208,256]{1,0:T(8,128)(2,1)S(1)}, bf16[208,256]{1,0:T(8,128)(2,1)S(1)}, u32[]{:S(2)}, u32[]{:S(2)}) collective-permute-start(bf16[208,256]{1,0:T(8,128)(2,1)S(1)} %source.1), channel_id=1, source_target_pairs={{0,0},{1,64},{2,128},{3,192},{4,256},{5,320},{6,384},{7,448},{64,1... | collective-permute-start | bytes 319496 | tf_op jit(solution)/shard_map/ppermute | solution.py:42
  2.5 24.8 %collective-permute-start.5 = (bf16[208,256]{1,0:T(8,128)(2,1)S(1)}, bf16[208,256]{1,0:T(8,128)(2,1)S(1)}, u32[]{:S(2)}, u32[]{:S(2)}) collective-permute-start(bf16[208,256]{1,0:T(8,128)(2,1)S(1)} %source.1), channel_id=1, source_target_pairs={{0,64},{1,0},{2,192},{3,128},{4,320},{5,256},{6,448},{7,384},{64,6... | collective-permute-start | bytes 319496 | tf_op jit(solution)/shard_map/ppermute | solution.py:42
  69.2 21.3 %copy-start = (bf16[224,256]{1,0:T(8,128)(2,1)S(1)}, bf16[224,256]{1,0:T(8,128)(2,1)}, u32[]{:S(2)}) copy-start(bf16[224,256]{1,0:T(8,128)(2,1)} %param.7) | copy-start | bytes 344068
  69.2 31.7 %collective-permute-start.6 = (bf16[16,336,256]{2,1,0:T(8,128)(2,1)S(1)}, bf16[16,336,256]{2,1,0:T(8,128)(2,1)}, u32[]{:S(2)}, u32[]{:S(2)}) collective-permute-start(bf16[16,336,256]{2,1,0:T(8,128)(2,1)S(1)} %all_to_all.10), channel_id=1, source_target_pairs={{0,8},{8,0},{1,9},{9,1},{2,10},{10,2},{3,11},{11,3},{4,12},{12,4},... | collective-permute-start | bytes 8257544 | tf_op jit(solution)/shard_map/ppermute | solution.py:42
  75.2 25.7 %all-to-all-start.1 = ((f32[16,8,128]{2,1,0:T(8,128)}), f32[16,8,128]{2,1,0:T(8,128)S(1)}, u32[]{:S(2)}, u32[]{:S(2)}) async-start(f32[16,8,128]{2,1,0:T(8,128)} %plane_sums.1), calls=%async_computation.1 | async-start | bytes 131072 | tf_op jit(solution)/shard_map/all_to_all | solution.py:46
  90.4 19.6 %collective-permute-start = (bf16[1,224,256]{2,1,0:T(8,128)(2,1)S(1)}, bf16[1,224,256]{2,1,0:T(8,128)(2,1)S(1)}, u32[]{:S(2)}, u32[]{:S(2)}) collective-permute-start(bf16[1,224,256]{2,1,0:T(8,128)(2,1)S(1)} %bitcast.11), channel_id=1, source_target_pairs={{0,4},{1,5},{2,6},{3,7},{4,0},{5,1},{6,2},{7,3},{8,12},{9,13},{10,... | collective-permute-start | bytes 344072 | tf_op jit(solution)/shard_map/ppermute | solution.py:42
  104.7 17.1 %collective-permute-start.10 = (bf16[4,112,256]{2,1,0:T(8,128)(2,1)S(1)}, bf16[4,112,256]{2,1,0:T(8,128)(2,1)S(1)}, u32[]{:S(2)}, u32[]{:S(2)}) collective-permute-start(bf16[4,112,256]{2,1,0:T(8,128)(2,1)S(1)} %get-tuple-element.23), channel_id=1, source_target_pairs={{0,1},{1,0},{2,3},{3,2},{4,5},{5,4},{6,7},{7,6},{8,9},{9,8},{10,11... | collective-permute-start | bytes 688136 | tf_op jit(solution)/shard_map/ppermute | solution.py:42
  106.8 17.5 %collective-permute-start.7 = (bf16[4,112,256]{2,1,0:T(8,128)(2,1)S(1)}, bf16[4,112,256]{2,1,0:T(8,128)(2,1)S(1)}, u32[]{:S(2)}, u32[]{:S(2)}) collective-permute-start(bf16[4,112,256]{2,1,0:T(8,128)(2,1)S(1)} %get-tuple-element.18), channel_id=1, source_target_pairs={{0,1},{1,0},{2,3},{3,2},{4,5},{5,4},{6,7},{7,6},{8,9},{9,8},{10,11... | collective-permute-start | bytes 688136 | tf_op jit(solution)/shard_map/ppermute | solution.py:42
  110.1 41.0 %collective-permute-start.1 = (bf16[2,224,256]{2,1,0:T(8,128)(2,1)S(1)}, bf16[2,224,256]{2,1,0:T(8,128)(2,1)S(1)}, u32[]{:S(2)}, u32[]{:S(2)}) collective-permute-start(bf16[2,224,256]{2,1,0:T(8,128)(2,1)S(1)} %pad_maximum_fusion.near_ref), channel_id=1, source_target_pairs={{0,2},{1,3},{2,0},{3,1},{4,6},{5,7},{6,4},{7,5},{8,10},{9,11},{10,... | collective-permute-start | bytes 688136 | tf_op jit(solution)/shard_map/ppermute | solution.py:42
  112.0 39.1 %collective-permute-start.2 = (bf16[2,224,256]{2,1,0:T(8,128)(2,1)S(1)}, bf16[2,224,256]{2,1,0:T(8,128)(2,1)S(1)}, u32[]{:S(2)}, u32[]{:S(2)}) collective-permute-start(bf16[2,224,256]{2,1,0:T(8,128)(2,1)S(1)} %pad_maximum_fusion.near_ref), channel_id=1, source_target_pairs={{0,1},{1,0},{2,3},{3,2},{4,5},{5,4},{6,7},{7,6},{8,9},{9,8},{10,11... | collective-permute-start | bytes 688136 | tf_op jit(solution)/shard_map/ppermute | solution.py:42
  115.0 36.1 %collective-permute-start.3 = (bf16[2,224,256]{2,1,0:T(8,128)(2,1)S(1)}, bf16[2,224,256]{2,1,0:T(8,128)(2,1)S(1)}, u32[]{:S(2)}, u32[]{:S(2)}) collective-permute-start(bf16[2,224,256]{2,1,0:T(8,128)(2,1)S(1)} %pad_maximum_fusion.near_ref), channel_id=1, source_target_pairs={{0,3},{1,2},{2,1},{3,0},{4,7},{5,6},{6,5},{7,4},{8,11},{9,10},{10,... | collective-permute-start | bytes 688136 | tf_op jit(solution)/shard_map/ppermute | solution.py:42
  121.9 19.9 %collective-permute-start.11 = (bf16[2,112,256]{2,1,0:T(8,128)(2,1)S(1)}, bf16[2,112,256]{2,1,0:T(8,128)(2,1)S(1)}, u32[]{:S(2)}, u32[]{:S(2)}) collective-permute-start(bf16[2,112,256]{2,1,0:T(8,128)(2,1)S(1)} %get-tuple-element.25), channel_id=1, source_target_pairs={{0,2},{1,3},{2,0},{3,1},{4,6},{5,7},{6,4},{7,5},{8,10},{9,11},{10,... | collective-permute-start | bytes 344072 | tf_op jit(solution)/shard_map/ppermute | solution.py:42
  124.4 20.6 %collective-permute-start.8 = (bf16[2,112,256]{2,1,0:T(8,128)(2,1)S(1)}, bf16[2,112,256]{2,1,0:T(8,128)(2,1)S(1)}, u32[]{:S(2)}, u32[]{:S(2)}) collective-permute-start(bf16[2,112,256]{2,1,0:T(8,128)(2,1)S(1)} %get-tuple-element.20), channel_id=1, source_target_pairs={{0,2},{1,3},{2,0},{3,1},{4,6},{5,7},{6,4},{7,5},{8,10},{9,11},{10,... | collective-permute-start | bytes 344072 | tf_op jit(solution)/shard_map/ppermute | solution.py:42
  141.9 13.4 %collective-permute-start.12 = (bf16[112,256]{1,0:T(8,128)(2,1)S(1)}, bf16[112,256]{1,0:T(8,128)(2,1)S(1)}, u32[]{:S(2)}, u32[]{:S(2)}) collective-permute-start(bf16[112,256]{1,0:T(8,128)(2,1)S(1)} %get-tuple-element.27), channel_id=1, source_target_pairs={{0,4},{1,5},{2,6},{3,7},{4,0},{5,1},{6,2},{7,3},{8,12},{9,13},{10,... | collective-permute-start | bytes 172040 | tf_op jit(solution)/shard_map/ppermute | solution.py:42
  145.1 10.6 %collective-permute-start.9 = (bf16[112,256]{1,0:T(8,128)(2,1)S(1)}, bf16[112,256]{1,0:T(8,128)(2,1)S(1)}, u32[]{:S(2)}, u32[]{:S(2)}) collective-permute-start(bf16[112,256]{1,0:T(8,128)(2,1)S(1)} %get-tuple-element.22), channel_id=1, source_target_pairs={{0,4},{1,5},{2,6},{3,7},{4,0},{5,1},{6,2},{7,3},{8,12},{9,13},{10,... | collective-permute-start | bytes 172040 | tf_op jit(solution)/shard_map/ppermute | solution.py:42

commit v10 on v9

--- a/solution.py
+++ b/solution.py
@@ -179,30 +179,7 @@
     )(plane)
 
 
-def mix_kernel(
-    scale, core_ref, place_ref, tiles_ref, own_ref, hidden_hbm, other_hbm,
-    mixed_ref, product_ref, cka_ref, upper_ref, lower_ref, hidden_ref, other_ref, semaphores,
-):
-    other_copy = fetch(other_hbm, other_ref, semaphores, 0)
-    hidden_copy = fetch(hidden_hbm, hidden_ref, semaphores, 1)
-    sums = jnp.sum(jnp.sum(tiles_ref[...], axis=0), axis=1, keepdims=True)
-    sxx, syy, sxy = sums[0:1], sums[1:2], sums[2:3]
-    root = jnp.sqrt(sxx * syy)
-    ratio = jnp.broadcast_to(sxy / sxx, (1, ROWS))
-    coef = jnp.broadcast_to(-2.0 * scale / root, (1, ROWS))
-    cka_ref[...] = sxy / root
-    core = core_ref[0]
-
-    def mix_pair(ref, base, first):
-        for i, (gram_x, gram_y) in enumerate(minibatch_grams(ref, first)):
-            mixed_ref[base + first + i] = coef * (gram_y - ratio * gram_x)
-
-    mix_pair(own_ref, 0, 0)
-    mix_pair(own_ref, 0, 2)
-    other_copy.wait()
-    mix_pair(other_ref, 4, 0)
-    mix_pair(other_ref, 4, 2)
-    hidden_copy.wait()
+def mix_rows(core, mixed_ref, hidden_ref, product_ref):
     for b in range(8):
         place = b % 4 * 2 + (core if b < 4 else 1 - core)
         hidden = hidden_ref[:, pl.ds(pl.multiple_of(place * ROWS, ROWS), ROWS)]
@@ -212,6 +189,35 @@
             preferred_element_type=F32,
         )
         product_ref[:, b * ROWS : (b + 1) * ROWS] = product.astype(BF16)
+
+
+def mix_kernel(
+    scale, core_ref, place_ref, tiles_ref, own_ref, hidden_hbm, other_hbm,
+    mixed_ref, product_ref, cka_ref, upper_ref, lower_ref, hidden_ref, other_ref, semaphores,
+):
+    pairs = [
+        fetch(other_hbm.at[:, pl.ds(y, 2)], other_ref.at[:, pl.ds(y, 2)], semaphores, y // 2)
+        for y in (0, 2)
+    ]
+    hidden_copy = fetch(hidden_hbm, hidden_ref, semaphores, 2)
+    sums = jnp.sum(jnp.sum(tiles_ref[...], axis=0), axis=1, keepdims=True)
+    sxx, syy, sxy = sums[0:1], sums[1:2], sums[2:3]
+    root = jnp.sqrt(sxx * syy)
+    ratio = jnp.broadcast_to(sxy / sxx, (1, ROWS))
+    coef = jnp.broadcast_to(-2.0 * scale / root, (1, ROWS))
+    cka_ref[...] = sxy / root
+
+    def mix_pair(ref, base, first):
+        for i, (gram_x, gram_y) in enumerate(minibatch_grams(ref, first)):
+            mixed_ref[base + first + i] = coef * (gram_y - ratio * gram_x)
+
+    mix_pair(own_ref, 0, 0)
+    mix_pair(own_ref, 0, 2)
+    for pair, y in zip(pairs, (0, 2)):
+        pair.wait()
+        mix_pair(other_ref, 4, y)
+    hidden_copy.wait()
+    mix_rows(core_ref[0], mixed_ref, hidden_ref, product_ref)
     middle = upper_ref.shape[1]
     for k in range(4):
         value = weight_block(place_ref, product_ref, own_ref, other_ref, 4 + k).astype(BF16)
@@ -236,7 +242,7 @@
         scratch_shapes=[
             pltpu.VMEM(hidden.shape, BF16),
             pltpu.VMEM(other.shape, BF16),
-            pltpu.SemaphoreType.DMA((2,)),
+            pltpu.SemaphoreType.DMA((3,)),
         ],
         compiler_params=PARAMS,
         name="mix",
@@ -261,18 +267,30 @@
     )
 
 
-def weight_kernel(place_ref, product_ref, own_ref, other_ref, out_ref):
+def weight_kernel(place_ref, product_ref, own_ref, other_hbm, out_ref, other_ref, semaphores):
+    other_copy = fetch(other_hbm, other_ref, semaphores, 0)
+    half = 4 * ROWS
     for k in range(4):
-        out_ref[k] = weight_block(place_ref, product_ref, own_ref, other_ref, k)
+        t = column_block(place_ref[0], k)
+        out_ref[k] = jnp.dot(
+            product_ref[:, :half], token_rows(own_ref, t), preferred_element_type=F32
+        )
+    other_copy.wait()
+    for k in range(4):
+        t = column_block(place_ref[0], k)
+        out_ref[k] += jnp.dot(
+            product_ref[:, half:], token_rows(other_ref, t), preferred_element_type=F32
+        )
 
 
 def weight_parts(place, product, plane, other):
     units = product.shape[0]
     return pl.pallas_call(
         weight_kernel,
-        in_specs=[SMEM] + [VMEM] * 3,
+        in_specs=[SMEM] + [VMEM] * 2 + [HBM],
         out_specs=VMEM,
         out_shape=jax.ShapeDtypeStruct((4, units, WIDTH), F32),
+        scratch_shapes=[pltpu.VMEM(other.shape, BF16), pltpu.SemaphoreType.DMA((1,))],
         compiler_params=PARAMS,
         cost_estimate=pl.CostEstimate(
             flops=2 * units * 8 * ROWS * 4 * WIDTH, bytes_accessed=4 << 20, transcendentals=0

time: 159 us -> 159 us (level)
  transfers between devices with their start and end apart: 14 -> 14, of which waited for: 6 -> 5; matrix products, arithmetic and copies ran while one was open for 0% -> 0% of each run, Pallas kernels for 8% -> 8%
where the time goes in v10:
time: 159 us; the launch traced here: 158 us
  starting transfers between devices  75 us (47%)
  blocking collectives  41.7 us (26%)
  waiting for transfers between devices  26.1 us (16%)
  Pallas kernels  13.9 us (9%)
    ppermute x13, starting transfers between devices, permute(): return lax.ppermute(values, names, permutation(names, target))  59.8 us
    all_to_all x1, blocking collectives, exchange(): return lax.all_to_all(values, names, split_axis=0, concat_axis=0)  41.7 us
    ppermute x13, waiting for transfers between devices, permute(): return lax.ppermute(values, names, permutation(names, target))  22.8 us
    all_to_all x1, starting transfers between devices, exchange(): return lax.all_to_all(values, names, split_axis=0, concat_axis=0)  15.2 us
    pallas_call x1, Pallas kernels, hidden_gradient(): pl.pallas_call(hidden_kernel, in_specs=[SMEM] * 2 + [VMEM] * 6 + [HBM], o...  4.14 us
    pallas_call x1, Pallas kernels, mix(): pl.pallas_call(functools.partial(mix_kernel, scale), in_specs=[SMEM] * 2...  4.11 us
    all_to_all x1, waiting for transfers between devices, exchange(): return lax.all_to_all(values, names, split_axis=0, concat_axis=0)  3.27 us
  transfers between devices with their start and end apart: 14, of which 5 were waited for; matrix products, arithmetic and copies ran while one was open for 0% of the time, Pallas kernels for 8%

profile of v10, /device:TPU:1, one launch (start us, length us, event | category | flops | bytes accessed | tf_op | source)
XLA Modules:
  0.0 157.8 jit_solution(16488143503542247883)
XLA Ops:
  0.6 1.1 source.1
  1.8 0.7 collective-permute-start.4
  2.5 17.5 %collective-permute-start.5 = (bf16[208,256]{1,0:T(8,128)(2,1)S(1)}, bf16[208,256]{1,0:T(8,128)(2,1)S(1)}, u32[]{:S(2)}, u32[]{:S(2)}) collective-permute-start(bf16[208,256]{1,0:T(8,128)(2,1)S(1)} %source.1), channel_id=1, source_target_pairs={{0,64},{1,0},{2,192},{3,128},{4,320},{5,256},{6,448},{7,384},{64,6... | collective-permute-start | bytes 319496 | tf_op jit(solution)/shard_map/ppermute | solution.py:42
  20.0 0.0 collective-permute-done.4.first_ref
  20.0 7.3 %collective-permute-done.5.second_ref = bf16[208,256]{1,0:T(8,128)(2,1)S(1)} collective-permute-done((bf16[208,256]{1,0:T(8,128)(2,1)S(1)}, bf16[208,256]{1,0:T(8,128)(2,1)S(1)}, u32[]{:S(2)}, u32[]{:S(2)}) %collective-permute-start.5) | collective-permute-done | bytes 106528 | tf_op jit(solution)/shard_map/ppermute | solution.py:42
  27.3 0.2 broadcast_in_dim.10
  27.5 41.7 %all_to_all.10 = bf16[16,336,256]{2,1,0:T(8,128)(2,1)S(1)} all-to-all(bf16[16,336,256]{2,1,0:T(8,128)(2,1)S(1)} %broadcast_in_dim.10), channel_id=1, replica_groups=mesh['x'=4,'zh'=2,'y'=4,'c'=2,'t'=8] {'x','y'}, dimensions={0} | all-to-all | bytes 5505024 | tf_op jit(solution)/shard_map/all_to_all | solution.py:46
  69.2 0.0 copy-start
  69.2 4.6 %collective-permute-start.6 = (bf16[16,336,256]{2,1,0:T(8,128)(2,1)S(1)}, bf16[16,336,256]{2,1,0:T(8,128)(2,1)}, u32[]{:S(2)}, u32[]{:S(2)}) collective-permute-start(bf16[16,336,256]{2,1,0:T(8,128)(2,1)S(1)} %all_to_all.10), channel_id=1, source_target_pairs={{0,8},{8,0},{1,9},{9,1},{2,10},{10,2},{3,11},{11,3},{4,12},{12,4},... | collective-permute-start | bytes 8257544 | tf_op jit(solution)/shard_map/ppermute | solution.py:42
  73.8 1.4 plane_sums.1
  75.2 15.2 %all-to-all-start.1 = ((f32[16,8,128]{2,1,0:T(8,128)}), f32[16,8,128]{2,1,0:T(8,128)S(1)}, u32[]{:S(2)}, u32[]{:S(2)}) async-start(f32[16,8,128]{2,1,0:T(8,128)} %plane_sums.1), calls=%async_computation.1 | async-start | bytes 131072 | tf_op jit(solution)/shard_map/all_to_all | solution.py:46
  90.4 0.0 copy-done
  90.4 7.2 %collective-permute-start = (bf16[1,224,256]{2,1,0:T(8,128)(2,1)S(1)}, bf16[1,224,256]{2,1,0:T(8,128)(2,1)S(1)}, u32[]{:S(2)}, u32[]{:S(2)}) collective-permute-start(bf16[1,224,256]{2,1,0:T(8,128)(2,1)S(1)} %bitcast.11), channel_id=1, source_target_pairs={{0,4},{1,5},{2,6},{3,7},{4,0},{5,1},{6,2},{7,3},{8,12},{9,13},{10,... | collective-permute-start | bytes 344072 | tf_op jit(solution)/shard_map/ppermute | solution.py:42
  97.6 3.3 %all-to-all-done.1.tiles_ref = f32[16,8,128]{2,1,0:T(8,128)S(1)} async-done(((f32[16,8,128]{2,1,0:T(8,128)}), f32[16,8,128]{2,1,0:T(8,128)S(1)}, u32[]{:S(2)}, u32[]{:S(2)}) %all-to-all-start.1) | async-done | bytes 65568 | tf_op jit(solution)/shard_map/all_to_all | solution.py:46
  100.9 0.0 collective-permute-done.6
  100.9 4.1 %mix.1 = (f32[8,128,128]{2,1,0:T(8,128)S(1)}, bf16[224,1024]{1,0:T(8,128)(2,1)S(1)}, f32[1,1]{1,0:T(1,128)}, bf16[4,112,256]{2,1,0:T(8,128)(2,1)S(1)}, bf16[4,112,256]{2,1,0:T(8,128)(2,1)S(1)}) custom-call(s32[1]{0:T(128)} %bitcast.1.core_ref, s32[1]{0:T(128)} %bitcast.place_ref, f32[16,8,128]{2,1,0:T(8,128)S(1)} %all-to-all-done.1.tiles_ref, ...), custom_call_target="tpu_custom_call" | custom-call | tf_op jit(solution)/shard_map/mix/pallas_call | solution.py:231
  105.0 2.1 %collective-permute-start.10 = (bf16[4,112,256]{2,1,0:T(8,128)(2,1)S(1)}, bf16[4,112,256]{2,1,0:T(8,128)(2,1)S(1)}, u32[]{:S(2)}, u32[]{:S(2)}) collective-permute-start(bf16[4,112,256]{2,1,0:T(8,128)(2,1)S(1)} %get-tuple-element.23), channel_id=1, source_target_pairs={{0,1},{1,0},{2,3},{3,2},{4,5},{5,4},{6,7},{7,6},{8,9},{9,8},{10,11... | collective-permute-start | bytes 688136 | tf_op jit(solution)/shard_map/ppermute | solution.py:42
  107.1 3.2 %collective-permute-start.7 = (bf16[4,112,256]{2,1,0:T(8,128)(2,1)S(1)}, bf16[4,112,256]{2,1,0:T(8,128)(2,1)S(1)}, u32[]{:S(2)}, u32[]{:S(2)}) collective-permute-start(bf16[4,112,256]{2,1,0:T(8,128)(2,1)S(1)} %get-tuple-element.18), channel_id=1, source_target_pairs={{0,1},{1,0},{2,3},{3,2},{4,5},{5,4},{6,7},{7,6},{8,9},{9,8},{10,11... | collective-permute-start | bytes 688136 | tf_op jit(solution)/shard_map/ppermute | solution.py:42
  110.3 0.0 collective-permute-done
  110.3 1.9 %collective-permute-start.1 = (bf16[2,224,256]{2,1,0:T(8,128)(2,1)S(1)}, bf16[2,224,256]{2,1,0:T(8,128)(2,1)S(1)}, u32[]{:S(2)}, u32[]{:S(2)}) collective-permute-start(bf16[2,224,256]{2,1,0:T(8,128)(2,1)S(1)} %pad_maximum_fusion.near_ref), channel_id=1, source_target_pairs={{0,2},{1,3},{2,0},{3,1},{4,6},{5,7},{6,4},{7,5},{8,10},{9,11},{10,... | collective-permute-start | bytes 688136 | tf_op jit(solution)/shard_map/ppermute | solution.py:42
  112.3 2.7 %collective-permute-start.2 = (bf16[2,224,256]{2,1,0:T(8,128)(2,1)S(1)}, bf16[2,224,256]{2,1,0:T(8,128)(2,1)S(1)}, u32[]{:S(2)}, u32[]{:S(2)}) collective-permute-start(bf16[2,224,256]{2,1,0:T(8,128)(2,1)S(1)} %pad_maximum_fusion.near_ref), channel_id=1, source_target_pairs={{0,1},{1,0},{2,3},{3,2},{4,5},{5,4},{6,7},{7,6},{8,9},{9,8},{10,11... | collective-permute-start | bytes 688136 | tf_op jit(solution)/shard_map/ppermute | solution.py:42
  115.0 4.6 %collective-permute-start.3 = (bf16[2,224,256]{2,1,0:T(8,128)(2,1)S(1)}, bf16[2,224,256]{2,1,0:T(8,128)(2,1)S(1)}, u32[]{:S(2)}, u32[]{:S(2)}) collective-permute-start(bf16[2,224,256]{2,1,0:T(8,128)(2,1)S(1)} %pad_maximum_fusion.near_ref), channel_id=1, source_target_pairs={{0,3},{1,2},{2,1},{3,0},{4,7},{5,6},{6,5},{7,4},{8,11},{9,10},{10,... | collective-permute-start | bytes 688136 | tf_op jit(solution)/shard_map/ppermute | solution.py:42
  119.6 2.3 %weight_parts.1.kept_ref = f32[4,224,256]{2,1,0:T(8,128)S(1)} custom-call(s32[1]{0:T(128)} %bitcast.place_ref, bf16[224,1024]{1,0:T(8,128)(2,1)S(1)} %get-tuple-element.17.product_ref, bf16[4,4,336,256]{3,2,1,0:T(8,128)(2,1)S(1)} %bitcast.9, bf16[4,4,336,256]{3,2,1,0:T(8,128)(2,1)} %bitcast.5.other_hbm), custom_call_target="tpu_custom_call" | custom-call | flops 469762048 | bytes 4194304 | tf_op jit(solution)/shard_map/weight_parts/pallas_call | solution.py:288
  121.9 0.0 collective-permute-done.10.arrived_ref
  122.0 1.9 %collective-permute-start.11 = (bf16[2,112,256]{2,1,0:T(8,128)(2,1)S(1)}, bf16[2,112,256]{2,1,0:T(8,128)(2,1)S(1)}, u32[]{:S(2)}, u32[]{:S(2)}) collective-permute-start(bf16[2,112,256]{2,1,0:T(8,128)(2,1)S(1)} %get-tuple-element.25), channel_id=1, source_target_pairs={{0,2},{1,3},{2,0},{3,1},{4,6},{5,7},{6,4},{7,5},{8,10},{9,11},{10,... | collective-permute-start | bytes 344072 | tf_op jit(solution)/shard_map/ppermute | solution.py:42
  123.9 0.1 collective-permute-done.7.arrived_ref
  124.0 0.1 shard_map.67
  124.1 4.1 %collective-permute-start.8 = (bf16[2,112,256]{2,1,0:T(8,128)(2,1)S(1)}, bf16[2,112,256]{2,1,0:T(8,128)(2,1)S(1)}, u32[]{:S(2)}, u32[]{:S(2)}) collective-permute-start(bf16[2,112,256]{2,1,0:T(8,128)(2,1)S(1)} %get-tuple-element.20), channel_id=1, source_target_pairs={{0,2},{1,3},{2,0},{3,1},{4,6},{5,7},{6,4},{7,5},{8,10},{9,11},{10,... | collective-permute-start | bytes 344072 | tf_op jit(solution)/shard_map/ppermute | solution.py:42
  128.2 13.8 %collective-permute-done.11.arrived_ref = bf16[2,112,256]{2,1,0:T(8,128)(2,1)S(1)} collective-permute-done((bf16[2,112,256]{2,1,0:T(8,128)(2,1)S(1)}, bf16[2,112,256]{2,1,0:T(8,128)(2,1)S(1)}, u32[]{:S(2)}, u32[]{:S(2)}) %collective-permute-start.11) | collective-permute-done | bytes 114720 | tf_op jit(solution)/shard_map/ppermute | solution.py:42
  142.0 2.9 %collective-permute-start.12 = (bf16[112,256]{1,0:T(8,128)(2,1)S(1)}, bf16[112,256]{1,0:T(8,128)(2,1)S(1)}, u32[]{:S(2)}, u32[]{:S(2)}) collective-permute-start(bf16[112,256]{1,0:T(8,128)(2,1)S(1)} %get-tuple-element.27), channel_id=1, source_target_pairs={{0,4},{1,5},{2,6},{3,7},{4,0},{5,1},{6,2},{7,3},{8,12},{9,13},{10,... | collective-permute-start | bytes 172040 | tf_op jit(solution)/shard_map/ppermute | solution.py:42
  145.0 0.0 collective-permute-done.8.arrived_ref
  145.0 6.3 %collective-permute-start.9 = (bf16[112,256]{1,0:T(8,128)(2,1)S(1)}, bf16[112,256]{1,0:T(8,128)(2,1)S(1)}, u32[]{:S(2)}, u32[]{:S(2)}) collective-permute-start(bf16[112,256]{1,0:T(8,128)(2,1)S(1)} %get-tuple-element.22), channel_id=1, source_target_pairs={{0,4},{1,5},{2,6},{3,7},{4,0},{5,1},{6,2},{7,3},{8,12},{9,13},{10,... | collective-permute-start | bytes 172040 | tf_op jit(solution)/shard_map/ppermute | solution.py:42
  151.3 0.0 collective-permute-done.1.two_ref
  151.3 0.0 collective-permute-done.2.one_ref
  151.3 0.0 collective-permute-done.3.three_ref
  151.3 4.1 %hidden_gradient.1 = bf16[224,1024]{1,0:T(8,128)(2,1)} custom-call(s32[1]{0:T(128)} %bitcast.place_ref, s32[1]{0:T(128)} %bitcast.1.core_ref, bf16[2,224,256]{2,1,0:T(8,128)(2,1)S(1)} %pad_maximum_fusion.near_ref, bf16[2,224,256]{2,1,0:T(8,128)(2,1)S(1)} %collective-permute-done.1.two_ref, bf16[2,224,256]{2,1,0:T(8,128)(2,1)S(1)} %collective-permute-done.2.one_ref, ...), custom_call_target="tpu_custom_call" | custom-call | flops 939524096 | bytes 8388608 | tf_op jit(solution)/shard_map/hidden_gradient/pallas_call | solution.py:336
  155.5 0.0 collective-permute-done.12.two_ref
  155.5 1.6 collective-permute-done.9.one_ref
  157.0 0.7 add_last.1
  (5 shorter events, 0.2 us)
Async XLA Ops:
  1.8 18.2 %collective-permute-start.4 = (bf16[208,256]{1,0:T(8,128)(2,1)S(1)}, bf16[208,256]{1,0:T(8,128)(2,1)S(1)}, u32[]{:S(2)}, u32[]{:S(2)}) collective-permute-start(bf16[208,256]{1,0:T(8,128)(2,1)S(1)} %source.1), channel_id=1, source_target_pairs={{0,0},{1,64},{2,128},{3,192},{4,256},{5,320},{6,384},{7,448},{64,1... | collective-permute-start | bytes 319496 | tf_op jit(solution)/shard_map/ppermute | solution.py:42
  2.5 24.8 %collective-permute-start.5 = (bf16[208,256]{1,0:T(8,128)(2,1)S(1)}, bf16[208,256]{1,0:T(8,128)(2,1)S(1)}, u32[]{:S(2)}, u32[]{:S(2)}) collective-permute-start(bf16[208,256]{1,0:T(8,128)(2,1)S(1)} %source.1), channel_id=1, source_target_pairs={{0,64},{1,0},{2,192},{3,128},{4,320},{5,256},{6,448},{7,384},{64,6... | collective-permute-start | bytes 319496 | tf_op jit(solution)/shard_map/ppermute | solution.py:42
  69.2 21.3 %copy-start = (bf16[224,256]{1,0:T(8,128)(2,1)S(1)}, bf16[224,256]{1,0:T(8,128)(2,1)}, u32[]{:S(2)}) copy-start(bf16[224,256]{1,0:T(8,128)(2,1)} %param.7) | copy-start | bytes 344068
  69.2 31.7 %collective-permute-start.6 = (bf16[16,336,256]{2,1,0:T(8,128)(2,1)S(1)}, bf16[16,336,256]{2,1,0:T(8,128)(2,1)}, u32[]{:S(2)}, u32[]{:S(2)}) collective-permute-start(bf16[16,336,256]{2,1,0:T(8,128)(2,1)S(1)} %all_to_all.10), channel_id=1, source_target_pairs={{0,8},{8,0},{1,9},{9,1},{2,10},{10,2},{3,11},{11,3},{4,12},{12,4},... | collective-permute-start | bytes 8257544 | tf_op jit(solution)/shard_map/ppermute | solution.py:42
  75.2 25.7 %all-to-all-start.1 = ((f32[16,8,128]{2,1,0:T(8,128)}), f32[16,8,128]{2,1,0:T(8,128)S(1)}, u32[]{:S(2)}, u32[]{:S(2)}) async-start(f32[16,8,128]{2,1,0:T(8,128)} %plane_sums.1), calls=%async_computation.1 | async-start | bytes 131072 | tf_op jit(solution)/shard_map/all_to_all | solution.py:46
  90.4 19.9 %collective-permute-start = (bf16[1,224,256]{2,1,0:T(8,128)(2,1)S(1)}, bf16[1,224,256]{2,1,0:T(8,128)(2,1)S(1)}, u32[]{:S(2)}, u32[]{:S(2)}) collective-permute-start(bf16[1,224,256]{2,1,0:T(8,128)(2,1)S(1)} %bitcast.11), channel_id=1, source_target_pairs={{0,4},{1,5},{2,6},{3,7},{4,0},{5,1},{6,2},{7,3},{8,12},{9,13},{10,... | collective-permute-start | bytes 344072 | tf_op jit(solution)/shard_map/ppermute | solution.py:42
  105.0 16.9 %collective-permute-start.10 = (bf16[4,112,256]{2,1,0:T(8,128)(2,1)S(1)}, bf16[4,112,256]{2,1,0:T(8,128)(2,1)S(1)}, u32[]{:S(2)}, u32[]{:S(2)}) collective-permute-start(bf16[4,112,256]{2,1,0:T(8,128)(2,1)S(1)} %get-tuple-element.23), channel_id=1, source_target_pairs={{0,1},{1,0},{2,3},{3,2},{4,5},{5,4},{6,7},{7,6},{8,9},{9,8},{10,11... | collective-permute-start | bytes 688136 | tf_op jit(solution)/shard_map/ppermute | solution.py:42
  107.1 16.9 %collective-permute-start.7 = (bf16[4,112,256]{2,1,0:T(8,128)(2,1)S(1)}, bf16[4,112,256]{2,1,0:T(8,128)(2,1)S(1)}, u32[]{:S(2)}, u32[]{:S(2)}) collective-permute-start(bf16[4,112,256]{2,1,0:T(8,128)(2,1)S(1)} %get-tuple-element.18), channel_id=1, source_target_pairs={{0,1},{1,0},{2,3},{3,2},{4,5},{5,4},{6,7},{7,6},{8,9},{9,8},{10,11... | collective-permute-start | bytes 688136 | tf_op jit(solution)/shard_map/ppermute | solution.py:42
  110.3 40.9 %collective-permute-start.1 = (bf16[2,224,256]{2,1,0:T(8,128)(2,1)S(1)}, bf16[2,224,256]{2,1,0:T(8,128)(2,1)S(1)}, u32[]{:S(2)}, u32[]{:S(2)}) collective-permute-start(bf16[2,224,256]{2,1,0:T(8,128)(2,1)S(1)} %pad_maximum_fusion.near_ref), channel_id=1, source_target_pairs={{0,2},{1,3},{2,0},{3,1},{4,6},{5,7},{6,4},{7,5},{8,10},{9,11},{10,... | collective-permute-start | bytes 688136 | tf_op jit(solution)/shard_map/ppermute | solution.py:42
  112.3 39.0 %collective-permute-start.2 = (bf16[2,224,256]{2,1,0:T(8,128)(2,1)S(1)}, bf16[2,224,256]{2,1,0:T(8,128)(2,1)S(1)}, u32[]{:S(2)}, u32[]{:S(2)}) collective-permute-start(bf16[2,224,256]{2,1,0:T(8,128)(2,1)S(1)} %pad_maximum_fusion.near_ref), channel_id=1, source_target_pairs={{0,1},{1,0},{2,3},{3,2},{4,5},{5,4},{6,7},{7,6},{8,9},{9,8},{10,11... | collective-permute-start | bytes 688136 | tf_op jit(solution)/shard_map/ppermute | solution.py:42
  115.0 36.3 %collective-permute-start.3 = (bf16[2,224,256]{2,1,0:T(8,128)(2,1)S(1)}, bf16[2,224,256]{2,1,0:T(8,128)(2,1)S(1)}, u32[]{:S(2)}, u32[]{:S(2)}) collective-permute-start(bf16[2,224,256]{2,1,0:T(8,128)(2,1)S(1)} %pad_maximum_fusion.near_ref), channel_id=1, source_target_pairs={{0,3},{1,2},{2,1},{3,0},{4,7},{5,6},{6,5},{7,4},{8,11},{9,10},{10,... | collective-permute-start | bytes 688136 | tf_op jit(solution)/shard_map/ppermute | solution.py:42
  122.0 20.0 %collective-permute-start.11 = (bf16[2,112,256]{2,1,0:T(8,128)(2,1)S(1)}, bf16[2,112,256]{2,1,0:T(8,128)(2,1)S(1)}, u32[]{:S(2)}, u32[]{:S(2)}) collective-permute-start(bf16[2,112,256]{2,1,0:T(8,128)(2,1)S(1)} %get-tuple-element.25), channel_id=1, source_target_pairs={{0,2},{1,3},{2,0},{3,1},{4,6},{5,7},{6,4},{7,5},{8,10},{9,11},{10,... | collective-permute-start | bytes 344072 | tf_op jit(solution)/shard_map/ppermute | solution.py:42
  124.1 20.9 %collective-permute-start.8 = (bf16[2,112,256]{2,1,0:T(8,128)(2,1)S(1)}, bf16[2,112,256]{2,1,0:T(8,128)(2,1)S(1)}, u32[]{:S(2)}, u32[]{:S(2)}) collective-permute-start(bf16[2,112,256]{2,1,0:T(8,128)(2,1)S(1)} %get-tuple-element.20), channel_id=1, source_target_pairs={{0,2},{1,3},{2,0},{3,1},{4,6},{5,7},{6,4},{7,5},{8,10},{9,11},{10,... | collective-permute-start | bytes 344072 | tf_op jit(solution)/shard_map/ppermute | solution.py:42
  142.0 13.4 %collective-permute-start.12 = (bf16[112,256]{1,0:T(8,128)(2,1)S(1)}, bf16[112,256]{1,0:T(8,128)(2,1)S(1)}, u32[]{:S(2)}, u32[]{:S(2)}) collective-permute-start(bf16[112,256]{1,0:T(8,128)(2,1)S(1)} %get-tuple-element.27), channel_id=1, source_target_pairs={{0,4},{1,5},{2,6},{3,7},{4,0},{5,1},{6,2},{7,3},{8,12},{9,13},{10,... | collective-permute-start | bytes 172040 | tf_op jit(solution)/shard_map/ppermute | solution.py:42
  145.0 12.0 %collective-permute-start.9 = (bf16[112,256]{1,0:T(8,128)(2,1)S(1)}, bf16[112,256]{1,0:T(8,128)(2,1)S(1)}, u32[]{:S(2)}, u32[]{:S(2)}) collective-permute-start(bf16[112,256]{1,0:T(8,128)(2,1)S(1)} %get-tuple-element.22), channel_id=1, source_target_pairs={{0,4},{1,5},{2,6},{3,7},{4,0},{5,1},{6,2},{7,3},{8,12},{9,13},{10,... | collective-permute-start | bytes 172040 | tf_op jit(solution)/shard_map/ppermute | solution.py:42
